TPU v7x, 256 devices: a whole 4x4x8 slice. The times are simulated.
256 devices in a mesh: section: 2 (over core), expert: 32 (over z, y), dp: 4 (over x).
Axes of the slice: x: 4, y: 4, z: 8, core: 2. Of those that a mesh axis runs over, the one named last changes fastest.
Arguments:
- x_in: bfloat16 [2, 128, 64, 3584], P(None, ('expert', 'dp')), may hold values from -6 to 6
- dy_out: bfloat16 [2, 128, 64, 3584], P(None, ('expert', 'dp')), may hold values from -6 to 6
- routes: int32 [2, 2, 128, 64, 1], P('section', None, ('expert', 'dp')), may hold values from 0 to 31; in each aligned block of 64 rows (0 to 63, 64 to 127, ..., all dimensions but the last counted through in order) at most 3 rows name the same one
- gates: float32 [2, 2, 128, 64, 1], P('section', None, ('expert', 'dp')), may hold values from 0.2 to 1
- w_down: bfloat16 [2, 3584, 256], P('section'), may hold values from -0.09375 to 0.09375
- w_qk: bfloat16 [2, 256, 256], P('section'), may hold values from -0.375 to 0.375
- w_up: bfloat16 [2, 256, 3584], P('section'), may hold values from -0.375 to 0.375
- e_gate: bfloat16 [2, 32, 3584, 1024], P('section', 'expert', None, 'dp'), may hold values from -0.09375 to 0.09375
- e_up: bfloat16 [2, 32, 3584, 1024], P('section', 'expert', None, 'dp'), may hold values from -0.09375 to 0.09375
- e_down: bfloat16 [2, 32, 1024, 3584], P('section', 'expert', 'dp'), may hold values from -0.1875 to 0.1875
Outputs:
- activations: bfloat16 [2, 2, 128, 64, 3584], P('section', None, ('expert', 'dp'))
- grads_in: bfloat16 [2, 2, 128, 64, 3584], P('section', None, ('expert', 'dp'))
- g_down: float32 [2, 3584, 256], P('section', ('expert', 'dp'))
- g_qk: float32 [2, 256, 256], P('section', ('expert', 'dp'))
- g_up_t: float32 [2, 3584, 256], P('section', ('expert', 'dp'))
Inputs may be any that keep to these rules, and one draw needn't show every extreme that they name: `routes`: within each sequence of one micro-batch and layer, every expert is named by at most 3 tokens, a bound that some block reaches.
All inputs are finite; a program needn't handle non-finite values.
Results may differ from a plain program's by a relative error of at most 0.035.
Values may be sent and summed in bfloat16 or wider, within the bound.
A program may use at most 128 MiB of HBM per device.

v0:
```python
import jax
import jax.numpy as jnp
from jax import lax
from jax.sharding import PartitionSpec as P

epsilon = 1e-06


def from_partner(x, axis, bit):
    return lax.ppermute(x, axis, [(i, i ^ 1 << bit) for i in range(lax.axis_size(axis))])


def times_t(left, right):
    return lax.dot_general(
        left,
        right,
        (((left.ndim - 1,), (right.ndim - 1,)), ((), ())),
        preferred_element_type=jnp.float32,
    )


def t_times(left, right):
    return lax.dot_general(
        left, right, (((0,), (0,)), ((), ())), preferred_element_type=jnp.float32
    )


def rms_norm(values):
    inv_rms = lax.rsqrt(jnp.mean(values * values, axis=-1, keepdims=True) + epsilon)
    return (values * inv_rms, inv_rms)


def rms_back(normed, inv_rms, upstream):
    return inv_rms * (upstream - normed * jnp.mean(upstream * normed, axis=-1, keepdims=True))


def silu_parts(gate_pre):
    sigmoid = jax.nn.sigmoid(gate_pre)
    return (gate_pre * sigmoid, sigmoid * (1.0 + gate_pre * (1.0 - sigmoid)))


def attend_forward(inputs, w_down, w_qk, w_up):
    normed, inv_rms = rms_norm(inputs.astype(jnp.float32))
    normed_b = normed.astype(jnp.bfloat16)
    latent = jnp.dot(normed_b, w_down, preferred_element_type=jnp.float32).astype(jnp.bfloat16)
    queries = jnp.dot(latent, w_qk, preferred_element_type=jnp.float32).astype(jnp.bfloat16)
    length = inputs.shape[0]
    scale_qk = latent.shape[1] ** (-0.5)
    scores = times_t(queries, latent) * scale_qk
    causal = lax.broadcasted_iota(jnp.int32, (length, length), 0) >= lax.broadcasted_iota(
        jnp.int32, (length, length), 1
    )
    scores = jnp.where(causal, scores, -1e30)
    row_max = jnp.max(scores, axis=-1, keepdims=True)
    exponent = jnp.exp(scores - row_max)
    attn_probs = exponent / jnp.sum(exponent, axis=-1, keepdims=True)
    probs_b = attn_probs.astype(jnp.bfloat16)
    mixed_rows = jnp.dot(probs_b, latent, preferred_element_type=jnp.float32).astype(jnp.bfloat16)
    residual = (
        inputs.astype(jnp.float32) + jnp.dot(mixed_rows, w_up, preferred_element_type=jnp.float32)
    ).astype(jnp.bfloat16)
    return (residual, (normed, inv_rms, normed_b, latent, queries, attn_probs, probs_b, mixed_rows))


def attend_backward(kept, upstream, w_down, w_qk, w_up):
    normed, inv_rms, normed_b, latent, queries, attn_probs, probs_b, mixed_rows = kept
    scale_qk = latent.shape[1] ** (-0.5)
    upstream_b = upstream.astype(jnp.bfloat16)
    d_mixed = times_t(upstream_b, w_up).astype(jnp.bfloat16)
    d_probs = times_t(d_mixed, latent)
    d_scores = (
        attn_probs * (d_probs - jnp.sum(d_probs * attn_probs, axis=-1, keepdims=True)) * scale_qk
    ).astype(jnp.bfloat16)
    d_queries = jnp.dot(d_scores, latent, preferred_element_type=jnp.float32).astype(jnp.bfloat16)
    d_latent = (
        t_times(probs_b, d_mixed) + t_times(d_scores, queries) + times_t(d_queries, w_qk)
    ).astype(jnp.bfloat16)
    d_normed = times_t(d_latent, w_down)
    factors = (normed_b, d_latent, latent, d_queries, upstream_b, mixed_rows)
    return (upstream + rms_back(normed, inv_rms, d_normed), factors)


def slot_table(route_ids, experts, capacity):
    one_hot = (route_ids[:, None] == jnp.arange(experts, dtype=jnp.int32)[None, :]).astype(
        jnp.int32
    )
    order_rank = jnp.sum((jnp.cumsum(one_hot, axis=0) - one_hot) * one_hot, axis=1)
    return route_ids * capacity + order_rank


def pass_section(values):
    return from_partner(values, "section", 0)


def trade(block):
    return lax.all_to_all(block, ("expert", "dp"), split_axis=0, concat_axis=0, tiled=True)


def to_experts(sent, experts):
    dp_count = lax.axis_size("dp")
    total_rows, model_width = sent.shape
    flat = sent.reshape(experts, total_rows // experts * model_width)
    copies = jnp.concatenate([flat] * dp_count, axis=1)
    return trade(copies.reshape(total_rows * dp_count, model_width))


def down_part(hidden_b, down_w):
    return jnp.dot(hidden_b, down_w, preferred_element_type=jnp.float32).astype(jnp.bfloat16)


def back_part(d_gate, d_up, gate_w, up_w):
    return (times_t(d_gate, gate_w) + times_t(d_up, up_w)).astype(jnp.bfloat16)


def from_experts(partial_value, experts):
    dp_count = lax.axis_size("dp")
    returned = trade(partial_value)
    total_rows, model_width = returned.shape
    width = total_rows // (experts * dp_count) * model_width
    flat = returned.reshape(experts, dp_count * width)
    summed = flat[:, 0:width].astype(jnp.float32)
    for quarter in range(1, dp_count):
        summed = summed + flat[:, quarter * width : (quarter + 1) * width].astype(jnp.float32)
    return summed.reshape(total_rows // dp_count, model_width)


def layer_forward(inputs, route_ids, gate_vals, weights):
    w_down, w_qk, w_up, gate_w, up_w, down_w = weights
    length, model_width = inputs.shape
    top_count = route_ids.shape[1]
    experts = lax.axis_size("expert")
    capacity = max(2, (3 * length * top_count + 2 * experts - 1) // (2 * experts))
    residual, kept_attn = attend_forward(inputs, w_down, w_qk, w_up)
    normed, inv_rms = rms_norm(residual.astype(jnp.float32))
    normed_b = normed.astype(jnp.bfloat16)
    slot_index = slot_table(route_ids.reshape(-1), experts, capacity)
    placement = (
        slot_index[None, :] == jnp.arange(experts * capacity, dtype=jnp.int32)[:, None]
    ).astype(jnp.bfloat16)
    sent = jnp.dot(
        placement, jnp.repeat(normed_b, top_count, axis=0), preferred_element_type=jnp.float32
    ).astype(jnp.bfloat16)
    expert_rows = to_experts(sent, experts)
    gate_pre = jnp.dot(expert_rows, gate_w, preferred_element_type=jnp.float32)
    up_pre = jnp.dot(expert_rows, up_w, preferred_element_type=jnp.float32)
    hidden_b = (silu_parts(gate_pre)[0] * up_pre).astype(jnp.bfloat16)
    partial_value = down_part(hidden_b, down_w)
    summed = from_experts(partial_value, experts)
    picked = summed[slot_index]
    mixture = jnp.sum(
        picked.reshape(length, top_count, model_width) * gate_vals[:, :, None], axis=1
    )
    output = (residual.astype(jnp.float32) + mixture).astype(jnp.bfloat16)
    return (
        output,
        (kept_attn, normed, inv_rms, slot_index, placement, gate_vals, gate_pre, up_pre),
    )


def layer_backward(kept, upstream, weights):
    kept_attn, normed, inv_rms, slot_index, placement, gate_vals, gate_pre, up_pre = kept
    w_down, w_qk, w_up, gate_w, up_w, down_w = weights
    length, model_width = upstream.shape
    top_count = gate_vals.shape[1]
    experts = lax.axis_size("expert")
    scaled = (
        (upstream[:, None, :] * gate_vals[:, :, None])
        .reshape(length * top_count, model_width)
        .astype(jnp.bfloat16)
    )
    sent = jnp.dot(placement, scaled, preferred_element_type=jnp.float32).astype(jnp.bfloat16)
    expert_rows = to_experts(sent, experts)
    d_hidden = times_t(expert_rows, down_w)
    activated, slope = silu_parts(gate_pre)
    d_gate = (d_hidden * up_pre * slope).astype(jnp.bfloat16)
    d_up = (d_hidden * activated).astype(jnp.bfloat16)
    returned = back_part(d_gate, d_up, gate_w, up_w)
    summed = from_experts(returned, experts)
    d_normed = jnp.sum(summed[slot_index].reshape(length, top_count, model_width), axis=1)
    d_resid = upstream + rms_back(normed, inv_rms, d_normed)
    return attend_backward(kept_attn, d_resid, w_down, w_qk, w_up)


def body(x_in, dy_out, routes, gates, w_down, w_qk, w_up, e_gate, e_up, e_down):
    section_index = lax.axis_index("section")
    micro = x_in.shape[0]
    gate_w, up_w, down_w = (e_gate[0, 0], e_up[0, 0], e_down[0, 0])
    weights = (w_down[0], w_qk[0], w_up[0], gate_w, up_w, down_w)
    route_table = routes[0, :, 0]
    gate_table = gates[0, :, 0]
    forward_outs = []
    kept_list = []
    incoming = None
    for moment in range(micro + 1):
        micro_idx = jnp.clip(moment - section_index, 0, micro - 1)
        own_input = x_in[min(moment, micro - 1), 0]
        layer_in = (
            own_input if incoming is None else jnp.where(section_index == 0, own_input, incoming)
        )
        route_ids = lax.dynamic_index_in_dim(route_table, micro_idx, 0, keepdims=False)
        gate_vals = lax.dynamic_index_in_dim(gate_table, micro_idx, 0, keepdims=False)
        output, kept = layer_forward(layer_in, route_ids, gate_vals, weights)
        forward_outs.append(output)
        kept_list.append(kept)
        if moment < micro:
            incoming = pass_section(output)
    left_down, right_down, left_qk, right_qk, left_up, right_up = ([], [], [], [], [], [])
    backward_outs = []
    incoming = None
    for moment in range(micro + 1):
        later = kept_list[min(moment + 1, micro)]
        earlier = kept_list[max(moment - 1, 0)]
        kept = jax.tree.map(
            lambda upper, lower: jnp.where(section_index == 1, upper, lower), later, earlier
        )
        own_grad = dy_out[min(moment, micro - 1), 0].astype(jnp.float32)
        upstream = (
            own_grad
            if incoming is None
            else jnp.where(section_index == 1, own_grad, incoming.astype(jnp.float32))
        )
        valid = jnp.where(section_index == 1, moment < micro, moment >= 1).astype(jnp.bfloat16)
        d_input, factors = layer_backward(kept, upstream, weights)
        left_down.append(factors[0])
        right_down.append(factors[1] * valid)
        left_qk.append(factors[2])
        right_qk.append(factors[3] * valid)
        left_up.append(factors[4] * valid)
        right_up.append(factors[5])
        d_input_b = d_input.astype(jnp.bfloat16)
        backward_outs.append(d_input_b)
        if moment < micro:
            incoming = pass_section(d_input_b)
    total_down = t_times(jnp.concatenate(left_down, axis=0), jnp.concatenate(right_down, axis=0))
    total_qk = t_times(jnp.concatenate(left_qk, axis=0), jnp.concatenate(right_qk, axis=0))
    total_up = t_times(jnp.concatenate(left_up, axis=0), jnp.concatenate(right_up, axis=0))
    activations = lax.dynamic_slice_in_dim(jnp.stack(forward_outs), section_index, micro, 0)[
        None, :, None
    ]
    grads_in = lax.dynamic_slice_in_dim(jnp.stack(backward_outs), 1 - section_index, micro, 0)[
        None, :, None
    ]
    g_down, g_qk, g_up_t = (
        lax.psum_scatter(total_down[None], ("expert", "dp"), scatter_dimension=1, tiled=True),
        lax.psum_scatter(total_qk[None], ("expert", "dp"), scatter_dimension=1, tiled=True),
        lax.psum_scatter(total_up[None], ("expert", "dp"), scatter_dimension=1, tiled=True),
    )
    return (activations, grads_in, g_down, g_qk, g_up_t)


def solution(mesh):
    placed = (
        P(None, ("expert", "dp"), None, None),
        P(None, ("expert", "dp"), None, None),
        P("section", None, ("expert", "dp"), None, None),
        P("section", None, ("expert", "dp"), None, None),
        P("section", None, None),
        P("section", None, None),
        P("section", None, None),
        P("section", "expert", None, "dp"),
        P("section", "expert", None, "dp"),
        P("section", "expert", "dp", None),
    )
    return jax.shard_map(
        body,
        mesh=mesh,
        in_specs=placed,
        out_specs=(
            P("section", None, ("expert", "dp"), None, None),
            P("section", None, ("expert", "dp"), None, None),
            P("section", ("expert", "dp"), None),
            P("section", ("expert", "dp"), None),
            P("section", ("expert", "dp"), None),
        ),
        check_vma=False,
    )
```

profile of v0, /device:TPU:0, one launch (start us, length us, event | category | flops | bytes accessed | tf_op | source)
XLA Modules:
  0.0 1635.1 jit_solution(6646738025848384521)
XLA Ops:
  17.8 6.5 all_to_all.84
  24.3 99.2 %all_to_all.126 = bf16[128,3,3584]{2,1,0:T(4,128)(2,1)} all-to-all(bf16[128,3,3584]{2,1,0:T(4,128)(2,1)} %all_to_all.84), channel_id=1, replica_groups=mesh['section'=2,'expert'=32,'dp'=4] {'expert','dp'}, dimensions={0} | all-to-all | bytes 5505024 | tf_op jit(solution)/shard_map/all_to_all | solution.py:96
  123.5 7.1 all_to_all.86
  138.4 6.7 all_to_all.87
  145.2 9.3 all-to-all-start.1
  161.0 78.1 %all-to-all-done.1 = bf16[128,3,3584]{2,1,0:T(4,128)(2,1)} async-done(((bf16[128,3,3584]{2,1,0:T(4,128)(2,1)}), bf16[128,3,3584]{2,1,0:T(4,128)(2,1)}, u32[]{:S(2)}, u32[]{:S(2)}) %all-to-all-start.1) | async-done | bytes 2752544 | tf_op jit(solution)/shard_map/all_to_all | solution.py:96
  239.1 6.5 reshape.573
  255.6 6.5 all_to_all.99
  262.1 8.3 all-to-all-start.6
  279.0 6.5 all_to_all.89
  285.5 69.2 %all-to-all-done.6 = bf16[128,3,3584]{2,1,0:T(4,128)(2,1)} async-done(((bf16[128,3,3584]{2,1,0:T(4,128)(2,1)}), bf16[128,3,3584]{2,1,0:T(4,128)(2,1)}, u32[]{:S(2)}, u32[]{:S(2)}) %all-to-all-start.6) | async-done | bytes 2752544 | tf_op jit(solution)/shard_map/all_to_all | solution.py:96
  354.7 10.3 all-to-all-start.2
  365.0 7.1 all_to_all.101
  374.8 74.8 %all-to-all-done.2 = bf16[128,3,3584]{2,1,0:T(4,128)(2,1)} async-done(((bf16[128,3,3584]{2,1,0:T(4,128)(2,1)}), bf16[128,3,3584]{2,1,0:T(4,128)(2,1)}, u32[]{:S(2)}, u32[]{:S(2)}) %all-to-all-start.2) | async-done | bytes 2752544 | tf_op jit(solution)/shard_map/all_to_all | solution.py:96
  449.6 7.1 all_to_all.91
  465.8 6.7 all_to_all.102
  472.5 9.1 all-to-all-start.7
  484.1 6.7 all_to_all.92
  490.8 75.3 %all-to-all-done.7 = bf16[128,3,3584]{2,1,0:T(4,128)(2,1)} async-done(((bf16[128,3,3584]{2,1,0:T(4,128)(2,1)}), bf16[128,3,3584]{2,1,0:T(4,128)(2,1)}, u32[]{:S(2)}, u32[]{:S(2)}) %all-to-all-start.7) | async-done | bytes 2752544 | tf_op jit(solution)/shard_map/all_to_all | solution.py:96
  566.0 8.6 all-to-all-start.3
  587.5 71.2 %all-to-all-done.3 = bf16[128,3,3584]{2,1,0:T(4,128)(2,1)} async-done(((bf16[128,3,3584]{2,1,0:T(4,128)(2,1)}), bf16[128,3,3584]{2,1,0:T(4,128)(2,1)}, u32[]{:S(2)}, u32[]{:S(2)}) %all-to-all-start.3) | async-done | bytes 2752544 | tf_op jit(solution)/shard_map/all_to_all | solution.py:96
  658.7 6.4 reshape.577
  693.3 6.5 all_to_all.94
  699.8 8.2 all-to-all-start.4
  713.5 6.5 all_to_all.104
  720.0 72.3 %all-to-all-done.4 = bf16[128,3,3584]{2,1,0:T(4,128)(2,1)} async-done(((bf16[128,3,3584]{2,1,0:T(4,128)(2,1)}), bf16[128,3,3584]{2,1,0:T(4,128)(2,1)}, u32[]{:S(2)}, u32[]{:S(2)}) %all-to-all-start.4) | async-done | bytes 2752544 | tf_op jit(solution)/shard_map/all_to_all | solution.py:96
  792.4 9.9 all-to-all-start.8
  802.3 7.1 all_to_all.96
  814.0 72.9 %all-to-all-done.8 = bf16[128,3,3584]{2,1,0:T(4,128)(2,1)} async-done(((bf16[128,3,3584]{2,1,0:T(4,128)(2,1)}), bf16[128,3,3584]{2,1,0:T(4,128)(2,1)}, u32[]{:S(2)}, u32[]{:S(2)}) %all-to-all-start.8) | async-done | bytes 2752544 | tf_op jit(solution)/shard_map/all_to_all | solution.py:96
  886.9 7.1 all_to_all.106
  900.8 6.7 all_to_all.107
  907.5 9.4 all-to-all-start.9
  917.5 83.9 %all-to-all-done.9 = bf16[128,3,3584]{2,1,0:T(4,128)(2,1)} async-done(((bf16[128,3,3584]{2,1,0:T(4,128)(2,1)}), bf16[128,3,3584]{2,1,0:T(4,128)(2,1)}, u32[]{:S(2)}, u32[]{:S(2)}) %all-to-all-start.9) | async-done | bytes 2752544 | tf_op jit(solution)/shard_map/all_to_all | solution.py:96
  1001.4 6.5 reshape.587
  1031.7 6.5 all_to_all.109
  1038.2 8.4 all-to-all-start.10
  1049.1 6.7 all_to_all.97
  1055.8 75.4 %all-to-all-done.10 = bf16[128,3,3584]{2,1,0:T(4,128)(2,1)} async-done(((bf16[128,3,3584]{2,1,0:T(4,128)(2,1)}), bf16[128,3,3584]{2,1,0:T(4,128)(2,1)}, u32[]{:S(2)}, u32[]{:S(2)}) %all-to-all-start.10) | async-done | bytes 2752544 | tf_op jit(solution)/shard_map/all_to_all | solution.py:96
  1131.2 9.3 all-to-all-start.5
  1140.5 7.1 all_to_all.111
  1154.4 6.7 all_to_all.112
  1161.1 64.1 %all-to-all-done.5 = bf16[128,3,3584]{2,1,0:T(4,128)(2,1)} async-done(((bf16[128,3,3584]{2,1,0:T(4,128)(2,1)}), bf16[128,3,3584]{2,1,0:T(4,128)(2,1)}, u32[]{:S(2)}, u32[]{:S(2)}) %all-to-all-start.5) | async-done | bytes 2752544 | tf_op jit(solution)/shard_map/all_to_all | solution.py:96
  1225.2 8.7 all-to-all-start.11
  1249.5 68.6 %all-to-all-done.11 = bf16[128,3,3584]{2,1,0:T(4,128)(2,1)} async-done(((bf16[128,3,3584]{2,1,0:T(4,128)(2,1)}), bf16[128,3,3584]{2,1,0:T(4,128)(2,1)}, u32[]{:S(2)}, u32[]{:S(2)}) %all-to-all-start.11) | async-done | bytes 2752544 | tf_op jit(solution)/shard_map/all_to_all | solution.py:96
  1318.1 6.4 reshape.590
  1338.5 16.9 %copy.19 = f32[1,3584,256]{2,0,1:T(1,128)} copy(f32[1,3584,256]{2,1,0:T(8,128)S(1)} %convolution_bitcast_fusion.1) | data formatting | bytes 7340032 | tf_op jit(solution)/shard_map/broadcast_in_dim | solution.py:244
  1356.2 16.9 %copy.20 = f32[1,3584,256]{2,0,1:T(1,128)} copy(f32[1,3584,256]{2,1,0:T(8,128)S(1)} %convolution_bitcast_fusion) | data formatting | bytes 7340032 | tf_op jit(solution)/shard_map/broadcast_in_dim | solution.py:246
  1382.4 241.5 %all-reduce.6.cloned.1.call-done = (f32[1,3584,256]{2,0,1:T(1,128)}, f32[1,256,256]{2,1,0:T(8,128)}, f32[1,3584,256]{2,0,1:T(1,128)}) async-done(((f32[1,3584,256]{2,0,1:T(1,128)}, f32[1,256,256]{2,1,0:T(8,128)}, f32[1,3584,256]{2,0,1:T(1,128)}), (f32[1,3584,256]{2,0,1:T(1,128)}, f32[1,256,256]{2,1,0:T(8,128)}, f32[1,3584,256]{2,0,1:T(1,128)})) %all-reduce.6.cloned.1.call-update) | async-done | bytes 7602192
  (491 shorter events, 190.2 us)
Async XLA Ops:
  7.2 128.8 %copy-start = (bf16[1,1,256,3584]{3,2,1,0:T(8,128)(2,1)S(1)}, bf16[1,1,256,3584]{3,2,1,0:T(8,128)(2,1)}, u32[]{:S(2)}) copy-start(bf16[1,1,256,3584]{3,2,1,0:T(8,128)(2,1)} %param.19) | copy-start | bytes 5505028
  145.1 9.4 copy-start.127
  145.1 9.6 copy-start.129
  145.1 9.9 copy-start.137
  145.1 10.0 copy-start.141
  145.1 10.6 copy-start.139
  145.1 10.6 copy-start.42
  145.1 10.6 copy-start.119
  145.2 93.9 %all-to-all-start.1 = ((bf16[128,3,3584]{2,1,0:T(4,128)(2,1)}), bf16[128,3,3584]{2,1,0:T(4,128)(2,1)}, u32[]{:S(2)}, u32[]{:S(2)}) async-start(bf16[128,3,3584]{2,1,0:T(4,128)(2,1)} %all_to_all.87), calls=%async_computation.1 | async-start | bytes 7340032 | tf_op jit(solution)/shard_map/all_to_all | solution.py:96
  155.1 90.5 %copy-start.146 = (s32[64]{0:T(128)}, s32[64]{0:T(128)S(1)}, u32[]{:S(2)}) copy-start(s32[64]{0:T(128)S(1)} %get-tuple-element.104) | copy-start | bytes 772
  155.7 89.9 %copy-start.115 = (s32[64]{0:T(128)}, s32[64]{0:T(128)S(1)}, u32[]{:S(2)}) copy-start(s32[64]{0:T(128)S(1)} %multiply_add_fusion.3) | copy-start | bytes 772
  253.8 16.6 %collective-permute-start = (bf16[64,3584]{1,0:T(8,128)(2,1)S(1)}, bf16[64,3584]{1,0:T(8,128)(2,1)}, u32[]{:S(2)}, u32[]{:S(2)}) collective-permute-start(bf16[64,3584]{1,0:T(8,128)(2,1)S(1)} %add_convert_fusion.5), channel_id=1, source_target_pairs={{0,128},{128,0},{1,129},{129,1},{2,130},{130,2},{3,131},{131,3},{4... | collective-permute-start | bytes 1376264 | tf_op jit(solution)/shard_map/ppermute | solution.py:10
  262.1 92.6 %all-to-all-start.6 = ((bf16[128,3,3584]{2,1,0:T(4,128)(2,1)}), bf16[128,3,3584]{2,1,0:T(4,128)(2,1)}, u32[]{:S(2)}, u32[]{:S(2)}) async-start(bf16[128,3,3584]{2,1,0:T(4,128)(2,1)} %all_to_all.99), calls=%async_computation.6 | async-start | bytes 7340032 | tf_op jit(solution)/shard_map/all_to_all | solution.py:96
  276.3 402.8 %copy-start.94 = (f32[64]{0:T(128)}, f32[64]{0:T(128)S(1)}, u32[]{:S(2)}) copy-start(f32[64]{0:T(128)S(1)} %get-tuple-element.63) | copy-start | bytes 772
  354.7 94.9 %all-to-all-start.2 = ((bf16[128,3,3584]{2,1,0:T(4,128)(2,1)}), bf16[128,3,3584]{2,1,0:T(4,128)(2,1)}, u32[]{:S(2)}, u32[]{:S(2)}) async-start(bf16[128,3,3584]{2,1,0:T(4,128)(2,1)} %all_to_all.89), calls=%async_computation.2 | async-start | bytes 7340032 | tf_op jit(solution)/shard_map/all_to_all | solution.py:96
  460.4 21.2 %copy-start.54 = (f32[384,256]{1,0:T(8,128)}, f32[384,256]{1,0:T(8,128)S(1)}, u32[]{:S(2)}) copy-start(f32[384,256]{1,0:T(8,128)S(1)} %fusion.23) | copy-start | bytes 1179652
  461.7 19.9 %copy-start.38 = (f32[384,256]{1,0:T(8,128)}, f32[384,256]{1,0:T(8,128)S(1)}, u32[]{:S(2)}) copy-start(f32[384,256]{1,0:T(8,128)S(1)} %fusion.35) | copy-start | bytes 1179652
  472.5 93.5 %all-to-all-start.7 = ((bf16[128,3,3584]{2,1,0:T(4,128)(2,1)}), bf16[128,3,3584]{2,1,0:T(4,128)(2,1)}, u32[]{:S(2)}, u32[]{:S(2)}) async-start(bf16[128,3,3584]{2,1,0:T(4,128)(2,1)} %all_to_all.102), calls=%async_computation.7 | async-start | bytes 7340032 | tf_op jit(solution)/shard_map/all_to_all | solution.py:96
  490.7 83.9 %copy-start.156 = (s32[64]{0:T(128)S(1)}, s32[64]{0:T(128)}, u32[]{:S(2)}) copy-start(s32[64]{0:T(128)} %get-tuple-element.64) | copy-start | bytes 772
  490.7 84.5 %copy-start.155 = (s32[64]{0:T(128)S(1)}, s32[64]{0:T(128)}, u32[]{:S(2)}) copy-start(s32[64]{0:T(128)} %get-tuple-element.66) | copy-start | bytes 772
  490.7 85.1 %copy-start.128 = (s32[64]{0:T(128)S(1)}, s32[64]{0:T(128)}, u32[]{:S(2)}) copy-start(s32[64]{0:T(128)} %get-tuple-element.53) | copy-start | bytes 772
  490.7 85.1 %copy-start.147 = (s32[64]{0:T(128)S(1)}, s32[64]{0:T(128)}, u32[]{:S(2)}) copy-start(s32[64]{0:T(128)} %copy-done.146) | copy-start | bytes 772
  566.0 92.7 %all-to-all-start.3 = ((bf16[128,3,3584]{2,1,0:T(4,128)(2,1)}), bf16[128,3,3584]{2,1,0:T(4,128)(2,1)}, u32[]{:S(2)}, u32[]{:S(2)}) async-start(bf16[128,3,3584]{2,1,0:T(4,128)(2,1)} %all_to_all.92), calls=%async_computation.3 | async-start | bytes 7340032 | tf_op jit(solution)/shard_map/all_to_all | solution.py:96
  679.0 5.5 collective-permute-start.1
  686.0 22.1 %collective-permute-start.2 = (bf16[64,3584]{1,0:T(8,128)(2,1)}, bf16[64,3584]{1,0:T(8,128)(2,1)}, u32[]{:S(2)}, u32[]{:S(2)}) collective-permute-start(bf16[64,3584]{1,0:T(8,128)(2,1)} %get-tuple-element.43), channel_id=1, source_target_pairs={{0,128},{128,0},{1,129},{129,1},{2,130},{130,2},{3,131},{131,3},{4... | collective-permute-start | bytes 1376264 | tf_op jit(solution)/shard_map/ppermute | solution.py:10
  699.8 92.5 %all-to-all-start.4 = ((bf16[128,3,3584]{2,1,0:T(4,128)(2,1)}), bf16[128,3,3584]{2,1,0:T(4,128)(2,1)}, u32[]{:S(2)}, u32[]{:S(2)}) async-start(bf16[128,3,3584]{2,1,0:T(4,128)(2,1)} %all_to_all.94), calls=%async_computation.4 | async-start | bytes 7340032 | tf_op jit(solution)/shard_map/all_to_all | solution.py:96
  792.4 94.5 %all-to-all-start.8 = ((bf16[128,3,3584]{2,1,0:T(4,128)(2,1)}), bf16[128,3,3584]{2,1,0:T(4,128)(2,1)}, u32[]{:S(2)}, u32[]{:S(2)}) async-start(bf16[128,3,3584]{2,1,0:T(4,128)(2,1)} %all_to_all.104), calls=%async_computation.8 | async-start | bytes 7340032 | tf_op jit(solution)/shard_map/all_to_all | solution.py:96
  813.1 83.7 %copy-start.56 = (f32[384,256]{1,0:T(8,128)}, f32[384,256]{1,0:T(8,128)S(1)}, u32[]{:S(2)}) copy-start(f32[384,256]{1,0:T(8,128)S(1)} %fusion.21) | copy-start | bytes 1179652
  813.9 83.9 %copy-start.40 = (f32[384,256]{1,0:T(8,128)}, f32[384,256]{1,0:T(8,128)S(1)}, u32[]{:S(2)}) copy-start(f32[384,256]{1,0:T(8,128)S(1)} %fusion.33) | copy-start | bytes 1179652
  907.5 9.4 copy-start.158
  907.5 93.9 %all-to-all-start.9 = ((bf16[128,3,3584]{2,1,0:T(4,128)(2,1)}), bf16[128,3,3584]{2,1,0:T(4,128)(2,1)}, u32[]{:S(2)}, u32[]{:S(2)}) async-start(bf16[128,3,3584]{2,1,0:T(4,128)(2,1)} %all_to_all.107), calls=%async_computation.9 | async-start | bytes 7340032 | tf_op jit(solution)/shard_map/all_to_all | solution.py:96
  1022.3 1.9 collective-permute-start.3
  1038.2 93.0 %all-to-all-start.10 = ((bf16[128,3,3584]{2,1,0:T(4,128)(2,1)}), bf16[128,3,3584]{2,1,0:T(4,128)(2,1)}, u32[]{:S(2)}, u32[]{:S(2)}) async-start(bf16[128,3,3584]{2,1,0:T(4,128)(2,1)} %all_to_all.109), calls=%async_computation.10 | async-start | bytes 7340032 | tf_op jit(solution)/shard_map/all_to_all | solution.py:96
  1131.2 94.0 %all-to-all-start.5 = ((bf16[128,3,3584]{2,1,0:T(4,128)(2,1)}), bf16[128,3,3584]{2,1,0:T(4,128)(2,1)}, u32[]{:S(2)}, u32[]{:S(2)}) async-start(bf16[128,3,3584]{2,1,0:T(4,128)(2,1)} %all_to_all.97), calls=%async_computation.5 | async-start | bytes 7340032 | tf_op jit(solution)/shard_map/all_to_all | solution.py:96
  1161.1 73.0 %copy-start.154 = (s32[64]{0:T(128)S(1)}, s32[64]{0:T(128)}, u32[]{:S(2)}) copy-start(s32[64]{0:T(128)} %get-tuple-element.22) | copy-start | bytes 772
  1161.1 73.0 %copy-start.157 = (s32[64]{0:T(128)S(1)}, s32[64]{0:T(128)}, u32[]{:S(2)}) copy-start(s32[64]{0:T(128)} %get-tuple-element.67) | copy-start | bytes 772
  1161.1 73.1 %copy-start.18 = (bf16[64,3584]{1,0:T(8,128)(2,1)S(1)}, bf16[64,3584]{1,0:T(8,128)(2,1)}, u32[]{:S(2)}) copy-start(bf16[64,3584]{1,0:T(8,128)(2,1)} %copy-done.16) | copy-start | bytes 1376260
  1225.2 92.9 %all-to-all-start.11 = ((bf16[128,3,3584]{2,1,0:T(4,128)(2,1)}), bf16[128,3,3584]{2,1,0:T(4,128)(2,1)}, u32[]{:S(2)}, u32[]{:S(2)}) async-start(bf16[128,3,3584]{2,1,0:T(4,128)(2,1)} %all_to_all.112), calls=%async_computation.11 | async-start | bytes 7340032 | tf_op jit(solution)/shard_map/all_to_all | solution.py:96
  1233.9 390.0 %all-reduce.6.cloned.1.call-start = ((), (), s32[]{:S(2)}) async-start(), calls=%async_computation.12 | async-start | bytes 15204352
  1338.5 16.9 %copy-start.70 = (bf16[64,3584]{1,0:T(8,128)(2,1)S(1)}, bf16[64,3584]{1,0:T(8,128)(2,1)}, u32[]{:S(2)}) copy-start(bf16[64,3584]{1,0:T(8,128)(2,1)} %copy-done.69) | copy-start | bytes 1376260
  1338.5 16.9 %copy-start.74 = (bf16[64,3584]{1,0:T(8,128)(2,1)S(1)}, bf16[64,3584]{1,0:T(8,128)(2,1)}, u32[]{:S(2)}) copy-start(bf16[64,3584]{1,0:T(8,128)(2,1)} %get-tuple-element.18) | copy-start | bytes 1376260
  1338.5 16.9 %copy-start.160 = (bf16[64,256]{1,0:T(8,128)(2,1)S(1)}, bf16[64,256]{1,0:T(8,128)(2,1)}, u32[]{:S(2)}) copy-start(bf16[64,256]{1,0:T(8,128)(2,1)} %get-tuple-element.46) | copy-start | bytes 98308
  1338.5 16.9 %copy-start.161 = (bf16[64,256]{1,0:T(8,128)(2,1)S(1)}, bf16[64,256]{1,0:T(8,128)(2,1)}, u32[]{:S(2)}) copy-start(bf16[64,256]{1,0:T(8,128)(2,1)} %get-tuple-element.47) | copy-start | bytes 98308
  1338.5 16.9 %copy-start.162 = (bf16[64,256]{1,0:T(8,128)(2,1)S(1)}, bf16[64,256]{1,0:T(8,128)(2,1)}, u32[]{:S(2)}) copy-start(bf16[64,256]{1,0:T(8,128)(2,1)} %get-tuple-element.48) | copy-start | bytes 98308
  1356.1 16.9 %copy-start.79 = (bf16[64,256]{1,0:T(8,128)(2,1)S(1)}, bf16[64,256]{1,0:T(8,128)(2,1)}, u32[]{:S(2)}) copy-start(bf16[64,256]{1,0:T(8,128)(2,1)} %get-tuple-element.76) | copy-start | bytes 98308
  1356.2 16.9 %copy-start.82 = (bf16[64,256]{1,0:T(8,128)(2,1)S(1)}, bf16[64,256]{1,0:T(8,128)(2,1)}, u32[]{:S(2)}) copy-start(bf16[64,256]{1,0:T(8,128)(2,1)} %get-tuple-element.50) | copy-start | bytes 98308
  1356.2 16.9 %copy-start.84 = (bf16[64,256]{1,0:T(8,128)(2,1)S(1)}, bf16[64,256]{1,0:T(8,128)(2,1)}, u32[]{:S(2)}) copy-start(bf16[64,256]{1,0:T(8,128)(2,1)} %copy-done.83) | copy-start | bytes 98308
  1356.2 16.9 %copy-start.89 = (bf16[64,256]{1,0:T(8,128)(2,1)S(1)}, bf16[64,256]{1,0:T(8,128)(2,1)}, u32[]{:S(2)}) copy-start(bf16[64,256]{1,0:T(8,128)(2,1)} %get-tuple-element.101) | copy-start | bytes 98308
  (131 other events, 409.4 us)
Sparse Core Ops, SparseCore 0:
  1374.2 249.6 all-reduce.5
where the time goes:
time: 1650 us; the launch traced here: 1640 us
  waiting for transfers between devices  1050 us (64%)
  local copies, waits for them, and re-layouts  239 us (14%)
  starting transfers between devices  100 us (6%)
  blocking collectives  99.2 us (6%)
  matrix products  67.9 us (4%)
  other arithmetic  61.9 us (4%)
  between operations  17.9 us (1%)
    all_to_all x11, waiting for transfers between devices, trade(): lax.all_to_all(block, ('expert', 'dp'), split_axis=0, concat_axis=0, tile...  806 us
    unnamed x2, waiting for transfers between devices  242 us
    all_to_all x18, local copies, waits for them, and re-layouts, trade(): lax.all_to_all(block, ('expert', 'dp'), split_axis=0, concat_axis=0, tile...  122 us
    all_to_all x11, starting transfers between devices, trade(): lax.all_to_all(block, ('expert', 'dp'), split_axis=0, concat_axis=0, tile...  99.4 us
    all_to_all x1, blocking collectives, trade(): lax.all_to_all(block, ('expert', 'dp'), split_axis=0, concat_axis=0, tile...  99.2 us
    reshape x6, local copies, waits for them, and re-layouts, from_experts(): flat = returned.reshape(experts, dp_count * width)  38.5 us
  transfers between devices with their start and end apart: 16, of which 13 were waited for; matrix products, arithmetic and copies ran while one was open for 5% of the time, Pallas kernels for 0%

commit v1 on v0

v1 whole, which is shorter than its diff:
```python
import functools

import jax
import jax.numpy as jnp
from jax import lax
from jax.experimental import pallas as pl
from jax.experimental.pallas import tpu as pltpu
from jax.sharding import PartitionSpec as P

epsilon = 1e-06
WIDTH = 3584
LAT = 256
FF = 256
SEQ = 64
EXPERTS = 32
DP = 4
CAP = 3
NZ = 8
NY = 4
PIECE = 512
PIECES = 7
BLOCK = (8, CAP * PIECE)
PACKED = PIECES * EXPERTS
ORDER = (0, 1, 7, 2, 6, 3, 5, 4)
MESH = pl.DeviceIdType.MESH
VMEM = pl.BlockSpec(memory_space=pltpu.VMEM)
ANY = pl.BlockSpec(memory_space=pl.ANY)
bf16 = jnp.bfloat16
f32 = jnp.float32


def dot(left, right):
    return jnp.dot(left, right, preferred_element_type=f32)


def times_t(left, right):
    return lax.dot_general(left, right, (((1,), (1,)), ((), ())), preferred_element_type=f32)


def t_times(left, right):
    return lax.dot_general(left, right, (((0,), (0,)), ((), ())), preferred_element_type=f32)


def rms_norm(values):
    inv_rms = lax.rsqrt(jnp.mean(values * values, axis=-1, keepdims=True) + epsilon)
    return (values * inv_rms, inv_rms)


def rms_back(normed, inv_rms, upstream):
    return inv_rms * (upstream - normed * jnp.mean(upstream * normed, axis=-1, keepdims=True))


def silu_parts(gate_pre):
    sigmoid = jax.nn.sigmoid(gate_pre)
    return (gate_pre * sigmoid, sigmoid * (1.0 + gate_pre * (1.0 - sigmoid)))


def spread_matrix():
    rows = lax.broadcasted_iota(jnp.int32, (EXPERTS * 8, PACKED), 0)
    cols = lax.broadcasted_iota(jnp.int32, (EXPERTS * 8, PACKED), 1)
    return ((rows % 8) * EXPERTS + rows // 8 == cols).astype(f32).astype(bf16)


def gather_matrix():
    rows = lax.broadcasted_iota(jnp.int32, (PACKED, EXPERTS * 8), 0)
    cols = lax.broadcasted_iota(jnp.int32, (PACKED, EXPERTS * 8), 1)
    return ((cols % 8) * EXPERTS + cols // 8 == rows).astype(f32).astype(bf16)


def slot_rows(route_row):
    experts = lax.broadcasted_iota(jnp.int32, (EXPERTS, SEQ), 0)
    hot = (experts == route_row).astype(f32)
    before = lax.broadcasted_iota(jnp.int32, (SEQ, SEQ), 0) < lax.broadcasted_iota(
        jnp.int32, (SEQ, SEQ), 1
    )
    rank = dot(hot.astype(bf16), before.astype(f32).astype(bf16))
    return jnp.concatenate(
        [(hot * (rank == float(s)).astype(f32)).astype(bf16) for s in range(CAP)], axis=0
    )


def slot_columns(route_col):
    experts = lax.broadcasted_iota(jnp.int32, (SEQ, EXPERTS), 1)
    hot = (experts == route_col).astype(f32)
    before = lax.broadcasted_iota(jnp.int32, (SEQ, SEQ), 0) > lax.broadcasted_iota(
        jnp.int32, (SEQ, SEQ), 1
    )
    rank = dot(before.astype(f32).astype(bf16), hot.astype(bf16))
    return jnp.concatenate(
        [(hot * (rank == float(s)).astype(f32)).astype(bf16) for s in range(CAP)], axis=1
    )


def pack_tokens(values_b, route_row, packed_ref, blocks_ref):
    picked = dot(slot_rows(route_row), values_b).astype(bf16)
    for s in range(CAP):
        for r in range(PIECES):
            packed_ref[r * EXPERTS : (r + 1) * EXPERTS, s * PIECE : (s + 1) * PIECE] = picked[
                s * EXPERTS : (s + 1) * EXPERTS, r * PIECE : (r + 1) * PIECE
            ]
    blocks_ref[...] = dot(spread_matrix(), packed_ref[...]).astype(bf16)


def unpack_tokens(blocks_ref, route_col, token_ref):
    packed = dot(gather_matrix(), blocks_ref[...]).astype(bf16)
    columns = slot_columns(route_col)
    for r in range(PIECES):
        stacked = jnp.concatenate(
            [
                packed[r * EXPERTS : (r + 1) * EXPERTS, s * PIECE : (s + 1) * PIECE]
                for s in range(CAP)
            ],
            axis=0,
        )
        token_ref[:, r * PIECE : (r + 1) * PIECE] = dot(columns, stacked)


def places():
    e = lax.axis_index("expert")
    d = lax.axis_index("dp")
    return e, d, e // NY, e % NY, (d + 1) % DP, (d + DP - 1) % DP, (d + 2) % DP


def meet(e, right, left):
    barrier = pltpu.get_barrier_semaphore()
    for k in range(1, EXPERTS):
        pl.semaphore_signal(
            barrier, inc=1, device_id={"expert": (e + k) % EXPERTS}, device_id_type=MESH
        )
    for side in (right, left):
        pl.semaphore_signal(barrier, inc=1, device_id={"dp": side}, device_id_type=MESH)
    pl.semaphore_wait(barrier, EXPERTS + 1)


def remote(src, dst, send, recv, where):
    return pltpu.make_async_remote_copy(
        src_ref=src, dst_ref=dst, send_sem=send, recv_sem=recv, device_id=where, device_id_type=MESH
    )


def dispatch_kernel(blk, rows, s1, sx, r1, rl, rr, ro):
    e, d, z, y, right, left, opp = places()
    meet(e, right, left)
    for j in ORDER:
        for dy in range(NY):
            if j == 0 and dy == 0:
                pltpu.make_async_copy(blk.at[e], rows.at[d * EXPERTS + e], r1.at[0]).start()
            else:
                peer = ((z + j) % NZ) * NY + (y + dy) % NY
                remote(
                    blk.at[peer],
                    rows.at[d * EXPERTS + e],
                    s1,
                    r1.at[(NZ - j) % NZ],
                    {"expert": peer},
                ).start()

    def group(owner, j):
        return rows.at[pl.ds(owner * EXPERTS + ((z + j) % NZ) * NY, NY)]

    def arrived(ref, sem):
        remote(ref, ref, s1, sem, {"dp": right}).wait_recv()

    def relay(i):
        j = ORDER[i]
        if i % 2 == 0:
            arrived(group(left, j), rl.at[j])
            remote(group(left, j), group(left, j), sx, ro.at[j], {"dp": right}).start()
        else:
            arrived(group(right, j), rr.at[j])
            remote(group(right, j), group(right, j), sx, ro.at[j], {"dp": left}).start()

    for i, j in enumerate(ORDER):
        arrived(group(d, j), r1.at[j])
        remote(group(d, j), group(d, j), sx, rl.at[j], {"dp": right}).start()
        remote(group(d, j), group(d, j), sx, rr.at[j], {"dp": left}).start()
        if i >= 2:
            relay(i - 2)
    relay(NZ - 2)
    relay(NZ - 1)
    for i, j in enumerate(ORDER):
        if i % 2 == 0:
            arrived(group(right, j), rr.at[j])
        else:
            arrived(group(left, j), rl.at[j])
        arrived(group(opp, j), ro.at[j])
    sent = blk.at[pl.ds(0, EXPERTS - 1)]
    remote(sent, sent, s1, r1.at[0], {"dp": right}).wait_send()
    sent = rows.at[pl.ds(0, 3 * EXPERTS)]
    remote(sent, sent, sx, r1.at[0], {"dp": right}).wait_send()


def dispatch(blocks):
    return pl.pallas_call(
        dispatch_kernel,
        name="dispatch",
        out_shape=jax.ShapeDtypeStruct((DP * EXPERTS, *BLOCK), bf16),
        in_specs=[VMEM],
        out_specs=VMEM,
        scratch_shapes=[
            pltpu.SemaphoreType.DMA,
            pltpu.SemaphoreType.DMA,
            pltpu.SemaphoreType.DMA((NZ,)),
            pltpu.SemaphoreType.DMA((NZ,)),
            pltpu.SemaphoreType.DMA((NZ,)),
            pltpu.SemaphoreType.DMA((NZ,)),
        ],
        compiler_params=pltpu.CompilerParams(collective_id=0, has_side_effects=True),
    )(blocks)


def combine_kernel(
    part, out, relayed, relay_sum, from_left, from_right, final, sx, s1, ra, rl, rr, rh
):
    e, d, z, y, right, left, opp = places()
    meet(e, right, left)

    def group(owner, j):
        return part.at[pl.ds(owner * EXPERTS + ((z + j) % NZ) * NY, NY)]

    def spot(ref, i):
        return ref.at[pl.ds(i * NY, NY)]

    def arrived(ref, sem):
        remote(ref, ref, s1, sem, {"dp": right}).wait_recv()

    for i, j in enumerate(ORDER):
        side = right if i % 2 == 0 else left
        remote(group(opp, j), spot(relayed, i), sx, ra.at[i], {"dp": side}).start()
    for i, j in enumerate(ORDER):
        if i % 2 == 0:
            remote(group(left, j), spot(from_right, i), sx, rr.at[i], {"dp": left}).start()
        else:
            remote(group(right, j), spot(from_left, i), sx, rl.at[i], {"dp": right}).start()

    def relay(i):
        j = ORDER[i]
        arrived(spot(relayed, i), ra.at[i])
        side = right if i % 2 == 0 else left
        spot(relay_sum, i)[...] = (
            spot(relayed, i)[...].astype(f32) + group(side, j)[...].astype(f32)
        ).astype(bf16)
        if i % 2 == 0:
            remote(spot(relay_sum, i), spot(from_left, i), sx, rl.at[i], {"dp": right}).start()
        else:
            remote(spot(relay_sum, i), spot(from_right, i), sx, rr.at[i], {"dp": left}).start()

    def finish(i):
        j = ORDER[i]
        arrived(spot(from_left, i), rl.at[i])
        arrived(spot(from_right, i), rr.at[i])
        spot(final, i)[...] = (
            group(d, j)[...].astype(f32)
            + spot(from_left, i)[...].astype(f32)
            + spot(from_right, i)[...].astype(f32)
        ).astype(bf16)
        for dy in range(NY):
            yy = (y + dy) % NY
            if j == 0 and dy == 0:
                pltpu.make_async_copy(final.at[i * NY + yy], out.at[e], rh).start()
            else:
                peer = ((z + j) % NZ) * NY + yy
                remote(final.at[i * NY + yy], out.at[e], s1, rh, {"expert": peer}).start()

    for i in range(NZ):
        relay(i)
    for i in range(NZ):
        finish(i)
    arrived(out, rh)
    sent = part.at[pl.ds(0, 3 * EXPERTS)]
    remote(sent, sent, sx, rh, {"dp": right}).wait_send()
    sent = part.at[pl.ds(0, EXPERTS - 1)]
    remote(sent, sent, s1, rh, {"dp": right}).wait_send()


def combine(partials):
    return pl.pallas_call(
        combine_kernel,
        name="combine",
        out_shape=jax.ShapeDtypeStruct((EXPERTS, *BLOCK), bf16),
        in_specs=[VMEM],
        out_specs=VMEM,
        scratch_shapes=[pltpu.VMEM((EXPERTS, *BLOCK), bf16)] * 5
        + [
            pltpu.SemaphoreType.DMA,
            pltpu.SemaphoreType.DMA,
            pltpu.SemaphoreType.DMA((NZ,)),
            pltpu.SemaphoreType.DMA((NZ,)),
            pltpu.SemaphoreType.DMA((NZ,)),
            pltpu.SemaphoreType.DMA,
        ],
        compiler_params=pltpu.CompilerParams(collective_id=1, has_side_effects=True),
    )(partials)


def fetch(layer, pairs, sems):
    mine = lax.axis_index("section") == layer
    for k, (own, other, dst) in enumerate(pairs):

        @pl.when(mine)
        def _():
            pltpu.make_async_copy(own, dst, sems.at[k]).start()

        @pl.when(jnp.logical_not(mine))
        def _():
            pltpu.make_async_copy(other, dst, sems.at[k]).start()

    def wait(k):
        own, _, dst = pairs[k]
        pltpu.make_async_copy(own, dst, sems.at[k]).wait()

    return wait


def attend(
    inputs, route_row, wd, wq, wu, wait, packed, blocks, residual, latent_o, queries_o, probs_o, mixed_o
):
    normed, _ = rms_norm(inputs.astype(f32))
    wait(0)
    latent = dot(normed.astype(bf16), wd[...]).astype(bf16)
    wait(1)
    queries = dot(latent, wq[...]).astype(bf16)
    scores = times_t(queries, latent) * (LAT ** (-0.5))
    causal = lax.broadcasted_iota(jnp.int32, (SEQ, SEQ), 0) >= lax.broadcasted_iota(
        jnp.int32, (SEQ, SEQ), 1
    )
    scores = jnp.where(causal, scores, -1e30)
    exponent = jnp.exp(scores - jnp.max(scores, axis=-1, keepdims=True))
    probs = exponent / jnp.sum(exponent, axis=-1, keepdims=True)
    mixed = dot(probs.astype(bf16), latent).astype(bf16)
    wait(2)
    resid = (inputs.astype(f32) + dot(mixed, wu[...])).astype(bf16)
    residual[...] = resid
    latent_o[...] = latent
    queries_o[...] = queries
    probs_o[...] = probs
    mixed_o[...] = mixed
    normed2, _ = rms_norm(resid.astype(f32))
    pack_tokens(normed2.astype(bf16), route_row, packed, blocks)


ATTN_SCRATCH = [
    pltpu.VMEM((WIDTH, LAT), bf16),
    pltpu.VMEM((LAT, LAT), bf16),
    pltpu.VMEM((LAT, WIDTH), bf16),
    pltpu.SemaphoreType.DMA((3,)),
]
ATTN_OUT = [
    jax.ShapeDtypeStruct((EXPERTS * 8, BLOCK[1]), bf16),
    jax.ShapeDtypeStruct((SEQ, WIDTH), bf16),
    jax.ShapeDtypeStruct((SEQ, LAT), bf16),
    jax.ShapeDtypeStruct((SEQ, LAT), bf16),
    jax.ShapeDtypeStruct((SEQ, SEQ), f32),
    jax.ShapeDtypeStruct((SEQ, LAT), bf16),
]
PACK_SCRATCH = [pltpu.VMEM((PACKED, BLOCK[1]), bf16)]
TOKEN_SCRATCH = [pltpu.VMEM((SEQ, WIDTH), f32)]


def first_kernel(
    x, route_row, wd0, wq0, wu0, wd1, wq1, wu1, blocks, residual, latent, queries, probs, mixed,
    packed, wd, wq, wu, sems,
):
    wait = fetch(0, ((wd0, wd1, wd), (wq0, wq1, wq), (wu0, wu1, wu)), sems)
    attend(
        x[...], route_row[...], wd, wq, wu, wait, packed, blocks, residual, latent, queries, probs,
        mixed,
    )


def first(x, route_row, attn):
    return pl.pallas_call(
        first_kernel,
        name="first",
        out_shape=ATTN_OUT,
        in_specs=[VMEM] * 2 + [ANY] * 6,
        out_specs=[VMEM] * 6,
        scratch_shapes=PACK_SCRATCH + ATTN_SCRATCH,
    )(x, route_row, *attn)


def second_kernel(
    back, resid_in, gate_col, route_col, route_row, wd0, wq0, wu0, wd1, wq1, wu1,
    act, blocks, residual, latent, queries, probs, mixed, tokens, packed, wd, wq, wu, sems,
):
    wait = fetch(1, ((wd0, wd1, wd), (wq0, wq1, wq), (wu0, wu1, wu)), sems)
    unpack_tokens(back, route_col[...], tokens)
    hidden = (resid_in[...].astype(f32) + gate_col[...] * tokens[...]).astype(bf16)
    act[...] = hidden
    attend(
        hidden, route_row[...], wd, wq, wu, wait, packed, blocks, residual, latent, queries, probs,
        mixed,
    )


def second(back, residual, gate_col, route_col, route_row, attn):
    return pl.pallas_call(
        second_kernel,
        name="second",
        out_shape=[jax.ShapeDtypeStruct((SEQ, WIDTH), bf16)] + ATTN_OUT,
        in_specs=[VMEM] * 5 + [ANY] * 6,
        out_specs=[VMEM] * 7,
        scratch_shapes=TOKEN_SCRATCH + PACK_SCRATCH + ATTN_SCRATCH,
    )(back, residual, gate_col, route_col, route_row, *attn)


def third_kernel(
    back, resid_in, gate_col, route_col, route_row, upstream, act, blocks, tokens, packed
):
    scaled = (gate_col[...] * upstream[...].astype(f32)).astype(bf16)
    pack_tokens(scaled, route_row[...], packed, blocks)
    unpack_tokens(back, route_col[...], tokens)
    act[...] = (resid_in[...].astype(f32) + gate_col[...] * tokens[...]).astype(bf16)


def third(back, residual, gate_col, route_col, route_row, upstream):
    return pl.pallas_call(
        third_kernel,
        name="third",
        out_shape=[jax.ShapeDtypeStruct((SEQ, WIDTH), bf16), ATTN_OUT[0]],
        in_specs=[VMEM] * 6,
        out_specs=[VMEM] * 2,
        scratch_shapes=TOKEN_SCRATCH + PACK_SCRATCH,
    )(back, residual, gate_col, route_col, route_row, upstream)


def back_kernel(
    layer, last, back, resid_in, inputs, upstream, route_col, gate_col, route_row, latent_i,
    queries_i, probs_i, mixed_i, wd0, wq0, wu0, wd1, wq1, wu1, *rest,
):
    if last:
        grad, normed_o, d_latent_o, d_queries_o, d_resid_o, tokens, wd, wq, wu, sems = rest
    else:
        grad, normed_o, d_latent_o, d_queries_o, d_resid_o, blocks, tokens, packed, wd, wq, wu, sems = rest
    wait = fetch(layer, ((wd0, wd1, wd), (wq0, wq1, wq), (wu0, wu1, wu)), sems)
    unpack_tokens(back, route_col[...], tokens)
    normed2, inv2 = rms_norm(resid_in[...].astype(f32))
    d_resid = upstream[...].astype(f32) + rms_back(normed2, inv2, tokens[...])
    d_resid_b = d_resid.astype(bf16)
    d_resid_o[...] = d_resid_b
    tokens[...] = d_resid
    latent, probs = latent_i[...], probs_i[...]
    wait(2)
    d_mixed = times_t(d_resid_b, wu[...]).astype(bf16)
    d_probs = times_t(d_mixed, latent)
    d_scores = (
        probs * (d_probs - jnp.sum(d_probs * probs, axis=-1, keepdims=True)) * (LAT ** (-0.5))
    ).astype(bf16)
    d_queries = dot(d_scores, latent).astype(bf16)
    wait(1)
    d_latent = (
        t_times(probs.astype(bf16), d_mixed)
        + t_times(d_scores, queries_i[...])
        + times_t(d_queries, wq[...])
    ).astype(bf16)
    wait(0)
    d_normed = times_t(d_latent, wd[...])
    normed, inv = rms_norm(inputs[...].astype(f32))
    normed_o[...] = normed.astype(bf16)
    d_latent_o[...] = d_latent
    d_queries_o[...] = d_queries
    d_input = (tokens[...] + rms_back(normed, inv, d_normed)).astype(bf16)
    grad[...] = d_input
    if not last:
        scaled = (gate_col[...] * d_input.astype(f32)).astype(bf16)
        pack_tokens(scaled, route_row[...], packed, blocks)


def backward(layer, back, residual, inputs, upstream, route_col, gate_col, route_row, kept, attn):
    last = layer == 0
    outs = [
        jax.ShapeDtypeStruct((SEQ, WIDTH), bf16),
        jax.ShapeDtypeStruct((SEQ, WIDTH), bf16),
        jax.ShapeDtypeStruct((SEQ, LAT), bf16),
        jax.ShapeDtypeStruct((SEQ, LAT), bf16),
        jax.ShapeDtypeStruct((SEQ, WIDTH), bf16),
    ] + ([] if last else [ATTN_OUT[0]])
    return pl.pallas_call(
        functools.partial(back_kernel, layer, last),
        name=f"backward{layer}",
        out_shape=outs,
        in_specs=[VMEM] * 11 + [ANY] * 6,
        out_specs=[VMEM] * len(outs),
        scratch_shapes=TOKEN_SCRATCH + ([] if last else PACK_SCRATCH) + ATTN_SCRATCH,
    )(back, residual, inputs, upstream, route_col, gate_col, route_row, *kept, *attn)


def unpack_rows(rows, wide):
    gather = gather_matrix()

    @pl.loop(0, DP)
    def _(g):
        start = pl.multiple_of(g * EXPERTS * 8, EXPERTS * 8)
        packed = dot(gather, rows[pl.ds(start, EXPERTS * 8), :]).astype(bf16)
        for s in range(CAP):
            at = pl.multiple_of(g * EXPERTS + s * DP * EXPERTS, EXPERTS)
            for r in range(PIECES):
                wide[pl.ds(at, EXPERTS), r * PIECE : (r + 1) * PIECE] = packed[
                    r * EXPERTS : (r + 1) * EXPERTS, s * PIECE : (s + 1) * PIECE
                ]


def pack_rows(wide, packed, out):
    spread = spread_matrix()

    @pl.loop(0, DP)
    def _(g):
        for s in range(CAP):
            at = pl.multiple_of(g * EXPERTS + s * DP * EXPERTS, EXPERTS)
            for r in range(PIECES):
                packed[r * EXPERTS : (r + 1) * EXPERTS, s * PIECE : (s + 1) * PIECE] = wide[
                    pl.ds(at, EXPERTS), r * PIECE : (r + 1) * PIECE
                ]
        start = pl.multiple_of(g * EXPERTS * 8, EXPERTS * 8)
        out[pl.ds(start, EXPERTS * 8), :] = dot(spread, packed[...]).astype(bf16)


def expert_forward_kernel(
    layer, rows, gw0, uw0, dw0, gw1, uw1, dw1, part, gate_o, up_o, wide, packed, gw, uw, dw, sems
):
    wait = fetch(layer, ((gw0, gw1, gw), (uw0, uw1, uw), (dw0, dw1, dw)), sems)
    unpack_rows(rows, wide)
    wait(0)
    gate_o[...] = dot(wide[...], gw[...])
    wait(1)
    up_o[...] = dot(wide[...], uw[...])
    hidden = (silu_parts(gate_o[...])[0] * up_o[...]).astype(bf16)
    wait(2)
    for c in range(PIECES):
        wide[:, c * PIECE : (c + 1) * PIECE] = dot(
            hidden, dw[:, c * PIECE : (c + 1) * PIECE]
        ).astype(bf16)
    pack_rows(wide, packed, part)


def expert_backward_kernel(
    layer, rows, gate_i, up_i, gw0, uw0, dw0, gw1, uw1, dw1, part, wide, packed, gw, uw, dw, sems
):
    wait = fetch(layer, ((gw0, gw1, gw), (uw0, uw1, uw), (dw0, dw1, dw)), sems)
    unpack_rows(rows, wide)
    wait(2)
    d_hidden = times_t(wide[...], dw[...])
    activated, slope = silu_parts(gate_i[...])
    d_gate = (d_hidden * up_i[...] * slope).astype(bf16)
    d_up = (d_hidden * activated).astype(bf16)
    wait(0)
    wait(1)
    for c in range(PIECES):
        wide[:, c * PIECE : (c + 1) * PIECE] = (
            times_t(d_gate, gw[c * PIECE : (c + 1) * PIECE, :])
            + times_t(d_up, uw[c * PIECE : (c + 1) * PIECE, :])
        ).astype(bf16)
    pack_rows(wide, packed, part)


EXPERT_SCRATCH = [
    pltpu.VMEM((CAP * DP * EXPERTS, WIDTH), bf16),
    pltpu.VMEM((PACKED, BLOCK[1]), bf16),
    pltpu.VMEM((WIDTH, FF), bf16),
    pltpu.VMEM((WIDTH, FF), bf16),
    pltpu.VMEM((FF, WIDTH), bf16),
    pltpu.SemaphoreType.DMA((3,)),
]
PARTS = jax.ShapeDtypeStruct((DP * EXPERTS * 8, BLOCK[1]), bf16)
PRE = jax.ShapeDtypeStruct((CAP * DP * EXPERTS, FF), f32)


def expert_forward(layer, rows, experts):
    return pl.pallas_call(
        functools.partial(expert_forward_kernel, layer),
        name=f"expert_forward{layer}",
        out_shape=[PARTS, PRE, PRE],
        in_specs=[VMEM] + [ANY] * 6,
        out_specs=[VMEM] * 3,
        scratch_shapes=EXPERT_SCRATCH,
    )(rows, *experts)


def expert_backward(layer, rows, gate_pre, up_pre, experts):
    return pl.pallas_call(
        functools.partial(expert_backward_kernel, layer),
        name=f"expert_backward{layer}",
        out_shape=PARTS,
        in_specs=[VMEM] * 3 + [ANY] * 6,
        out_specs=VMEM,
        scratch_shapes=EXPERT_SCRATCH,
    )(rows, gate_pre, up_pre, *experts)


def flat(blocks):
    return blocks.reshape(-1, BLOCK[1])


def blocked(rows):
    return rows.reshape(-1, *BLOCK)


def swap(value):
    return lax.ppermute(value, "section", [(0, 1), (1, 0)])


def spaced(values, per):
    rows, width = values.shape
    wide = (per + 7) // 8 * 8
    return jnp.pad(values.reshape(rows, width // per, per), ((0, 0), (0, 0), (0, wide - per))).reshape(
        rows, width // per * wide
    )


def body(x_in, dy_out, routes, gates, w_down, w_qk, w_up, e_gate, e_up, e_down):
    section = lax.axis_index("section")
    attn_own = (w_down[0], w_qk[0], w_up[0])
    experts_own = (e_gate[0, 0], e_up[0, 0], e_down[0, 0])
    attn = attn_own + tuple(swap(w) for w in attn_own)
    experts = experts_own + tuple(swap(w) for w in experts_own)
    x = lax.dynamic_index_in_dim(x_in[:, 0], section, 0, keepdims=False)
    dy = lax.dynamic_index_in_dim(dy_out[:, 0], section, 0, keepdims=False)

    def both_layers(table):
        other = swap(lax.dynamic_index_in_dim(table, 1 - section, 0, keepdims=False))
        own = lax.dynamic_index_in_dim(table, section, 0, keepdims=False)
        return (jnp.where(section == 0, own, other), jnp.where(section == 0, other, own))

    route_cols = both_layers(routes[0, :, 0])
    gate_cols = both_layers(gates[0, :, 0])
    route_rows = tuple(r.reshape(1, SEQ) for r in route_cols)

    blocks, resid0, *kept0 = first(x, route_rows[0], attn)
    rows = flat(dispatch(blocked(blocks)))
    parts, gate0, up0 = expert_forward(0, rows, experts)
    back = flat(combine(blocked(parts)))
    act0, blocks, resid1, *kept1 = second(
        back, resid0, gate_cols[0], route_cols[0], route_rows[1], attn
    )
    rows = flat(dispatch(blocked(blocks)))
    parts, gate1, up1 = expert_forward(1, rows, experts)
    back = flat(combine(blocked(parts)))
    act1, blocks = third(back, resid1, gate_cols[1], route_cols[1], route_rows[1], dy)
    rows = flat(dispatch(blocked(blocks)))
    parts = expert_backward(1, rows, gate1, up1, experts)
    back = flat(combine(blocked(parts)))
    grad1, n1, dl1, dq1, dr1, blocks = backward(
        1, back, resid1, act0, dy, route_cols[1], gate_cols[0], route_rows[0], kept1, attn
    )
    rows = flat(dispatch(blocked(blocks)))
    parts = expert_backward(0, rows, gate0, up0, experts)
    back = flat(combine(blocked(parts)))
    grad0, n0, dl0, dq0, dr0 = backward(
        0, back, resid0, x, grad1, route_cols[0], gate_cols[0], route_rows[0], kept0, attn
    )
    layer0 = (n0, dl0, kept0[0], dq0, dr0, kept0[3], act0, grad0)
    layer1 = (n1, dl1, kept1[0], dq1, dr1, kept1[3], act1, grad1)
    own = [jnp.where(section == 0, a, b) for a, b in zip(layer0, layer1)]
    other = [swap(jnp.where(section == 0, b, a)) for a, b in zip(layer0, layer1)]
    n1b, d_latent, latent, d_queries, d_resid, mixed = (
        jnp.concatenate([a, b], axis=0) for a, b in zip(own[:6], other[:6])
    )

    def in_order(a, b):
        return jnp.stack([jnp.where(section == 0, a, b), jnp.where(section == 0, b, a)])[
            None, :, None
        ]

    activations = in_order(own[6], other[6])
    grads_in = in_order(own[7], other[7])

    def scattered(left, right, per):
        total = t_times(spaced(left, per), right)
        mine = lax.psum_scatter(total, ("expert", "dp"), scatter_dimension=0, tiled=True)
        return mine[None, :per]

    g_down = scattered(n1b, d_latent, 28)
    g_qk = scattered(latent, d_queries, 2)
    g_up_t = scattered(d_resid, mixed, 28)
    return (activations, grads_in, g_down, g_qk, g_up_t)


def solution(mesh):
    placed = (
        P(None, ("expert", "dp"), None, None),
        P(None, ("expert", "dp"), None, None),
        P("section", None, ("expert", "dp"), None, None),
        P("section", None, ("expert", "dp"), None, None),
        P("section", None, None),
        P("section", None, None),
        P("section", None, None),
        P("section", "expert", None, "dp"),
        P("section", "expert", None, "dp"),
        P("section", "expert", "dp", None),
    )
    return jax.shard_map(
        body,
        mesh=mesh,
        in_specs=placed,
        out_specs=(
            P("section", None, ("expert", "dp"), None, None),
            P("section", None, ("expert", "dp"), None, None),
            P("section", ("expert", "dp"), None),
            P("section", ("expert", "dp"), None),
            P("section", ("expert", "dp"), None),
        ),
        check_vma=False,
    )
```

time: 1650 us -> 2530 us (1.53)
  waiting for transfers between devices: 1050 us -> 2100 us
  Pallas kernels: 0 us -> 389 us
  local copies, waits for them, and re-layouts: 239 us -> 14.3 us
  blocking collectives: 99.2 us -> 0 us
  starting transfers between devices: 100 us -> 4.84 us
  matrix products: 67.9 us -> 6.63 us
  other arithmetic: 61.9 us -> 5.29 us
    reduce_scatter x0 -> x3, waiting for transfers between devices: none -> 2090 us  [scattered(): lax.psum_scatter(total, ('expert', 'dp'), scatter_dimension=0, tiled=True)]
    all_to_all x11 -> x0, waiting for transfers between devices: 806 us -> none  [trade(): lax.all_to_all(block, ('expert', 'dp'), split_axis=0, concat_axis=0, tile...]
    pallas_call x0 -> x17, Pallas kernels: none -> 389 us  [the longest x4 162 us: combine(): pl.pallas_call(combine_kernel, name='combine', out_shape=jax.ShapeDtypeSt...]
    unnamed x2 -> x3, waiting for transfers between devices: 242 us -> 0.05 us
    all_to_all x18 -> x0, local copies, waits for them, and re-layouts: 122 us -> none  [trade(): lax.all_to_all(block, ('expert', 'dp'), split_axis=0, concat_axis=0, tile...]
    all_to_all x11 -> x0, starting transfers between devices: 99.4 us -> none  [trade(): lax.all_to_all(block, ('expert', 'dp'), split_axis=0, concat_axis=0, tile...]
    all_to_all x1 -> x0, blocking collectives: 99.2 us -> none  [trade(): lax.all_to_all(block, ('expert', 'dp'), split_axis=0, concat_axis=0, tile...]
    dot_general x54 -> x0, matrix products: 64.7 us -> none  [the longest x24 27 us: times_t(): lax.dot_general(left, right, (((left.ndim - 1,), (right.ndim - 1,)), ((),...]
  transfers between devices with their start and end apart: 16 -> 19, of which waited for: 13 -> 8; matrix products, arithmetic and copies ran while one was open for 5% -> 1% of each run, Pallas kernels for 0% -> 2%
where the time goes in v1:
time: 2530 us
  waiting for transfers between devices  2100 us (83%)
  Pallas kernels  389 us (15%)
    reduce_scatter x3, waiting for transfers between devices, scattered(): lax.psum_scatter(total, ('expert', 'dp'), scatter_dimension=0, tiled=True)  2090 us
    pallas_call x4, Pallas kernels, combine(): pl.pallas_call(combine_kernel, name='combine', out_shape=jax.ShapeDtypeSt...  162 us
    pallas_call x4, Pallas kernels, dispatch(): pl.pallas_call(dispatch_kernel, name='dispatch', out_shape=jax.ShapeDtype...  150 us
  transfers between devices with their start and end apart: 19, of which 8 were waited for; matrix products, arithmetic and copies ran while one was open for 1% of the time, Pallas kernels for 2%

profile of v1, /device:TPU:0, one launch (start us, length us, event | category | flops | bytes accessed | tf_op | source)
XLA Modules:
  0.0 2532.0 jit_solution(2505838560843391802)
XLA Ops:
  7.3 0.8 fusion.15
  8.8 0.7 fusion.17
  10.5 2.3 collective-permute-done.7
  13.5 0.8 dynamic-slice_bitcast_fusion.1.x.inputs
  14.3 1.8 dynamic-slice_bitcast_fusion.upstream
  16.1 1.3 fusion.22
  17.4 0.6 broadcast_select_fusion.16
  18.0 6.0 first.1
  24.0 45.0 %dispatch.4 = bf16[128,8,1536]{2,1,0:T(8,128)(2,1)} custom-call(bf16[32,8,1536]{2,1,0:T(8,128)(2,1)} %bitcast.116), custom_call_target="tpu_custom_call" | custom-call | tf_op jit(solution)/shard_map/dispatch/pallas_call | solution.py:194
  69.1 1.2 copy-done.2
  70.4 10.6 expert_forward0.1
  80.9 41.7 %combine.4 = bf16[32,8,1536]{2,1,0:T(8,128)(2,1)} custom-call(bf16[128,8,1536]{2,1,0:T(8,128)(2,1)} %bitcast.103), custom_call_target="tpu_custom_call" | custom-call | tf_op jit(solution)/shard_map/combine/pallas_call | solution.py:277
  122.6 7.0 second.1
  129.6 36.3 %dispatch.5 = bf16[128,8,1536]{2,1,0:T(8,128)(2,1)} custom-call(bf16[32,8,1536]{2,1,0:T(8,128)(2,1)} %bitcast.115), custom_call_target="tpu_custom_call" | custom-call | tf_op jit(solution)/shard_map/dispatch/pallas_call | solution.py:194
  165.9 10.5 expert_forward1.1
  176.4 40.2 %combine.5 = bf16[32,8,1536]{2,1,0:T(8,128)(2,1)} custom-call(bf16[128,8,1536]{2,1,0:T(8,128)(2,1)} %bitcast.104), custom_call_target="tpu_custom_call" | custom-call | tf_op jit(solution)/shard_map/combine/pallas_call | solution.py:277
  216.7 3.5 third.1
  220.2 34.5 %dispatch.6 = bf16[128,8,1536]{2,1,0:T(8,128)(2,1)} custom-call(bf16[32,8,1536]{2,1,0:T(8,128)(2,1)} %bitcast.117), custom_call_target="tpu_custom_call" | custom-call | tf_op jit(solution)/shard_map/dispatch/pallas_call | solution.py:194
  254.7 11.5 expert_backward1.1
  266.3 41.4 %combine.6 = bf16[32,8,1536]{2,1,0:T(8,128)(2,1)} custom-call(bf16[128,8,1536]{2,1,0:T(8,128)(2,1)} %bitcast.100), custom_call_target="tpu_custom_call" | custom-call | tf_op jit(solution)/shard_map/combine/pallas_call | solution.py:277
  307.7 8.2 backward1.1
  315.9 33.7 %dispatch.7 = bf16[128,8,1536]{2,1,0:T(8,128)(2,1)} custom-call(bf16[32,8,1536]{2,1,0:T(8,128)(2,1)} %bitcast.114), custom_call_target="tpu_custom_call" | custom-call | tf_op jit(solution)/shard_map/dispatch/pallas_call | solution.py:194
  349.6 11.5 expert_backward0.1
  361.2 39.0 %combine.7 = bf16[32,8,1536]{2,1,0:T(8,128)(2,1)} custom-call(bf16[128,8,1536]{2,1,0:T(8,128)(2,1)} %bitcast.98), custom_call_target="tpu_custom_call" | custom-call | tf_op jit(solution)/shard_map/combine/pallas_call | solution.py:277
  400.4 7.7 backward0.1
  408.1 0.8 broadcast_select_fusion.11
  409.0 0.5 collective-permute-start.13
  409.6 0.7 collective-permute-done.13
  410.3 1.3 fusion
  412.4 1.2 collective-permute-done.14
  413.7 0.6 copy.33
  414.7 2.7 fusion.10
  417.4 0.9 copy-done.8
  419.3 1.2 collective-permute-done.10
  420.5 0.9 copy.31
  421.8 2.7 fusion.3
  424.5 1.0 copy-done.4
  426.4 1.2 collective-permute-done.9
  427.7 1.0 maximum_bitcast_fusion.1
  428.8 1.0 maximum_bitcast_fusion
  429.8 682.9 %reduce-scatter.6.cloned.1.call-done = f32[8,256]{1,0:T(8,128)} async-done(((f32[1024,256]{1,0:T(8,128)}), f32[8,256]{1,0:T(8,128)}) %reduce-scatter.6.cloned.1.call-update) | async-done | bytes 8208 | tf_op jit(solution)/shard_map/reduce_scatter | solution.py:669
  1112.7 1.3 slice_bitcast_fusion.2
  1114.0 704.8 %reduce-scatter.8.cloned.1.call-done = f32[32,256]{1,0:T(8,128)} async-done(((f32[4096,256]{1,0:T(8,128)}), f32[32,256]{1,0:T(8,128)}) %reduce-scatter.8.cloned.1.call-update) | async-done | bytes 32784 | tf_op jit(solution)/shard_map/reduce_scatter | solution.py:669
  1818.7 0.8 slice_bitcast_fusion
  1819.5 0.6 copy.37
  1820.1 703.4 %reduce-scatter.4.cloned.1.call-done = f32[32,256]{1,0:T(8,128)} async-done(((f32[4096,256]{1,0:T(8,128)}), f32[32,256]{1,0:T(8,128)}) %reduce-scatter.4.cloned.1.call-update) | async-done | bytes 32784 | tf_op jit(solution)/shard_map/reduce_scatter | solution.py:669
  2523.5 0.8 slice_bitcast_fusion.1
  2524.3 0.6 copy.36
  (88 shorter events, 6.4 us)
Async XLA Ops:
  7.2 6.3 copy-start
  7.2 1105.5 %reduce-scatter.6.cloned.1.call-start = ((), (), s32[]{:S(2)}) async-start(), calls=%async_computation.4 | async-start | bytes 1056768 | tf_op jit(solution)/shard_map/reduce_scatter | solution.py:669
  7.2 5.7 collective-permute-start.2
  8.2 1.9 collective-permute-start
  8.6 9.4 collective-permute-start.1
  9.5 3.2 collective-permute-start.7
  10.0 8.0 collective-permute-start.3
  10.1 59.0 %collective-permute-start.4 = (bf16[3584,256]{1,0:T(8,128)(2,1)}, bf16[3584,256]{1,0:T(8,128)(2,1)S(1)}, u32[]{:S(2)}, u32[]{:S(2)}) collective-permute-start(bf16[3584,256]{1,0:T(8,128)(2,1)} %bitcast.70), channel_id=1, source_target_pairs={{0,128},{128,0},{1,129},{129,1},{2,130},{130,2},{3,131},{131,3},{4... | collective-permute-start | bytes 5505032 | tf_op jit(solution)/shard_map/ppermute | solution.py:599
  12.8 56.3 %collective-permute-start.5 = (bf16[3584,256]{1,0:T(8,128)(2,1)}, bf16[3584,256]{1,0:T(8,128)(2,1)}, u32[]{:S(2)}, u32[]{:S(2)}) collective-permute-start(bf16[3584,256]{1,0:T(8,128)(2,1)} %bitcast.75), channel_id=1, source_target_pairs={{0,128},{128,0},{1,129},{129,1},{2,130},{130,2},{3,131},{131,3},{4... | collective-permute-start | bytes 5505032 | tf_op jit(solution)/shard_map/ppermute | solution.py:599
  12.9 5.1 copy-start.5
  12.9 56.2 %collective-permute-start.6 = (bf16[256,3584]{1,0:T(8,128)(2,1)}, bf16[256,3584]{1,0:T(8,128)(2,1)}, u32[]{:S(2)}, u32[]{:S(2)}) collective-permute-start(bf16[256,3584]{1,0:T(8,128)(2,1)} %bitcast.80), channel_id=1, source_target_pairs={{0,128},{128,0},{1,129},{129,1},{2,130},{130,2},{3,131},{131,3},{4... | collective-permute-start | bytes 5505032 | tf_op jit(solution)/shard_map/ppermute | solution.py:599
  69.1 1.3 copy-start.2
  361.2 39.1 %copy-start.14 = (bf16[64,256]{1,0:T(8,128)(2,1)S(1)}, bf16[64,256]{1,0:T(8,128)(2,1)}, u32[]{:S(2)}) copy-start(bf16[64,256]{1,0:T(8,128)(2,1)} %get-tuple-element.56.latent_i) | copy-start | bytes 98308
  361.2 39.1 %copy-start.15 = (bf16[64,256]{1,0:T(8,128)(2,1)S(1)}, bf16[64,256]{1,0:T(8,128)(2,1)}, u32[]{:S(2)}) copy-start(bf16[64,256]{1,0:T(8,128)(2,1)} %get-tuple-element.48.latent_i) | copy-start | bytes 98308
  400.3 9.2 collective-permute-start.12
  400.4 7.7 copy-start.18
  408.1 3.6 copy-start.10
  408.1 3.6 copy-start.11
  409.0 1.3 collective-permute-start.13
  410.3 1.9 copy-start.12
  410.3 1.9 copy-start.13
  411.6 1407.1 %reduce-scatter.8.cloned.1.call-start = ((), (), s32[]{:S(2)}) async-start(), calls=%async_computation.5 | async-start | bytes 4227072 | tf_op jit(solution)/shard_map/reduce_scatter | solution.py:669
  411.7 1.9 collective-permute-start.14
  412.2 2.5 collective-permute-start.15
  417.3 1.0 copy-start.8
  417.3 1.2 copy-start.9
  417.4 1.6 copy-start.16
  417.4 1.6 copy-start.17
  417.4 2106.1 %reduce-scatter.4.cloned.1.call-start = ((), (), s32[]{:S(2)}) async-start(), calls=%async_computation.3 | async-start | bytes 4227072 | tf_op jit(solution)/shard_map/reduce_scatter | solution.py:669
  418.5 1.9 collective-permute-start.10
  419.0 2.8 collective-permute-start.11
  424.5 1.0 copy-start.4
  424.5 1.2 copy-start.7
  424.5 1.6 copy-start.3
  424.5 1.6 copy-start.6
  425.7 1.9 collective-permute-start.9
  426.2 2.5 collective-permute-start.8
  427.7 2097.2 %copy-start.1 = (bf16[2,1,64,3584]{3,2,1,0:T(8,128)(2,1)S(1)}, bf16[2,1,64,3584]{3,2,1,0:T(8,128)(2,1)}, u32[]{:S(2)}) copy-start(bf16[2,1,64,3584]{3,2,1,0:T(8,128)(2,1)} %param.10) | copy-start | bytes 2752516
Sparse Core Ops, SparseCore 0:
  411.7 700.9 reduce-scatter.5
  1115.2 703.4 reduce-scatter.7
  1821.2 702.2 reduce-scatter.3

commit v2 on v1

--- a/solution.py
+++ b/solution.py
@@ -599,12 +599,271 @@
     return lax.ppermute(value, "section", [(0, 1), (1, 0)])
 
 
-def spaced(values, per):
-    rows, width = values.shape
-    wide = (per + 7) // 8 * 8
-    return jnp.pad(values.reshape(rows, width // per, per), ((0, 0), (0, 0), (0, wide - per))).reshape(
-        rows, width // per * wide
-    )
+ROUND = 1792
+SIDE = 1280
+
+
+def quarter_matrix(first_is_dp):
+    out = lax.broadcasted_iota(jnp.int32, (1, 1024), 1)
+    one, two, zz, i = out // 256, (out // 64) % 4, (out // 32) % 2, out % 32
+    y, x = (two, one) if first_is_dp else (one, two)
+    source = jnp.where(i < 28, zz * 448 + y * 112 + x * 28 + i, -1)
+    return (lax.broadcasted_iota(jnp.int32, (896, 1024), 0) == source).astype(f32).astype(bf16)
+
+
+def small_matrix():
+    out = lax.broadcasted_iota(jnp.int32, (1, 1024), 1)
+    x, y, z, i = out // 256, (out // 64) % 4, (out // 8) % 8, out % 8
+    source = jnp.where(i < 2, z * 32 + y * 8 + x * 2 + i, -1)
+    return (lax.broadcasted_iota(jnp.int32, (LAT, 1024), 0) == source).astype(f32).astype(bf16)
+
+
+def lay_out(factor, matrix, sent, layer):
+    stacked = jnp.concatenate([factor[:, c * 896 : (c + 1) * 896] for c in range(4)], axis=0)
+    moved = dot(stacked, matrix).astype(bf16)
+    for q in range(4):
+        for c in range(4):
+            sent[layer, q, :, c * 256 : (c + 1) * 256] = moved[
+                c * SEQ : (c + 1) * SEQ, q * 256 : (q + 1) * 256
+            ]
+
+
+class Ring:
+    def __init__(self, section, position, near, sent, got, relay, ssem, fsem, rsem):
+        self.section, self.position, self.near = section, position, near
+        self.sent, self.got, self.relay_buf = sent, got, relay
+        self.ssem, self.fsem, self.rsem = ssem, fsem, rsem
+
+    def start(self, layer):
+        pos, s = self.position, self.section
+        way = 1 if layer == 0 else 3
+        remote(
+            self.sent.at[layer, (pos + 2) % 4],
+            self.relay_buf.at[layer],
+            self.ssem,
+            self.rsem.at[layer],
+            self.near(way),
+        ).start()
+        for step, back in ((1, 1), (3, 0)):
+            remote(
+                self.sent.at[layer, (pos + step) % 4],
+                self.got.at[s, pos],
+                self.ssem,
+                self.fsem.at[s, back],
+                {**self.near(step), "section": layer},
+            ).start()
+
+    def own(self):
+        pos, s = self.position, self.section
+        pltpu.make_async_copy(self.sent.at[s, pos], self.got.at[s, pos], self.fsem.at[s, 3]).start()
+        remote(
+            self.sent.at[1 - s, pos],
+            self.got.at[s, pos],
+            self.ssem,
+            self.fsem.at[s, 3],
+            {"section": 1 - s},
+        ).start()
+
+    def relay(self):
+        for layer, way in ((0, 1), (1, 3)):
+            buf = self.relay_buf.at[layer]
+            remote(buf, buf, self.ssem, self.rsem.at[layer], self.near(1)).wait_recv()
+            origin = (self.position + 4 - way) % 4
+            remote(
+                buf,
+                self.got.at[self.section, origin],
+                self.ssem,
+                self.fsem.at[self.section, 2],
+                {**self.near(way), "section": layer},
+            ).start()
+
+    def arrive(self):
+        for m in range(2):
+            for k, step in enumerate((1, 3, 2, 0)):
+                ref = self.got.at[m, (self.position + step) % 4]
+                remote(ref, ref, self.ssem, self.fsem.at[m, k], self.near(1)).wait_recv()
+
+    def drain(self):
+        for layer in range(2):
+            ref = self.sent.at[layer]
+            remote(ref, ref, self.ssem, self.rsem.at[0], self.near(1)).wait_send()
+        ref = self.sent.at[0, 0]
+        remote(ref, ref, self.ssem, self.rsem.at[0], self.near(1)).wait_send()
+
+
+def fold(pieces):
+    total = pieces[0].astype(f32)
+    for piece in pieces[1:]:
+        total = total + piece.astype(f32)
+    return total
+
+
+def grads_kernel(
+    n0, dl0, la0, dq0, dr0, mx0, act0, grad0, n1, dl1, la1, dq1, dr1, mx1, act1, grad1,
+    act_o, grad_o, down_o, qk_o, up_o,
+    xs, xg, xr, ys, yg, yr, td, sd, zd, zr, tu, su, zu, zv,
+    xssem, xfsem, xrsem, yssem, yfsem, yrsem, psem, qsem, asem, dsem, dr, usem, ur, zsem, zrecv,
+):
+    s = lax.axis_index("section")
+    e, d, z, y, right, left, opp = places()
+
+    def near_x(k):
+        return {"dp": (d + k) % 4}
+
+    def near_y(k):
+        return {"expert": z * NY + (y + k) % 4}
+
+    def near_z(k):
+        return {"expert": ((z + k) % NZ) * NY + y}
+
+    barrier = pltpu.get_barrier_semaphore()
+    peers = [{"section": 1 - s}]
+    for near in (near_x, near_y):
+        for k in (1, 3):
+            peers += [{**near(k), "section": 0}, {**near(k), "section": 1}]
+        peers.append(near(2))
+    peers += [near_z(k) for k in range(1, NZ)]
+    for peer in peers:
+        pl.semaphore_signal(barrier, inc=1, device_id=peer, device_id_type=MESH)
+    x_ring = Ring(s, d, near_x, xs, xg, xr, xssem, xfsem, xrsem)
+    y_ring = Ring(s, y, near_y, ys, yg, yr, yssem, yfsem, yrsem)
+    factors = ((n0, dl0, la0, dq0, dr0, mx0), (n1, dl1, la1, dq1, dr1, mx1))
+    by_x, by_y, small = quarter_matrix(True), quarter_matrix(False), small_matrix()
+    for layer, (n, dl, la, dq, _, _) in enumerate(factors):
+        lay_out(n[...], by_x, xs, layer)
+        moved = dot(la[...], small).astype(bf16)
+        for q in range(4):
+            xs[layer, q, :, 1024:1280] = dl[...]
+            xs[layer, q, :, 1280:1536] = moved[:, q * 256 : (q + 1) * 256]
+            xs[layer, q, :, 1536:1792] = dq[...]
+    pl.semaphore_wait(barrier, len(peers))
+    x_ring.start(0)
+    x_ring.start(1)
+    for layer, (_, _, _, _, dres, mx) in enumerate(factors):
+        lay_out(dres[...], by_y, ys, layer)
+        for q in range(4):
+            ys[layer, q, :, 1024:1280] = mx[...]
+    y_ring.start(0)
+    y_ring.start(1)
+    x_ring.own()
+    y_ring.own()
+
+    for k, (out, first_layer, second_layer) in enumerate(((act_o, act0, act1), (grad_o, grad0, grad1))):
+        for here, keep, give in ((0, first_layer, second_layer), (1, second_layer, first_layer)):
+
+            @pl.when(s == here)
+            def _():
+                pltpu.make_async_copy(keep, out.at[s], asem.at[k]).start()
+                remote(give, out.at[s], psem, qsem.at[k], {"section": 1 - s}).start()
+
+    x_ring.relay()
+    y_ring.relay()
+
+    def rows(ring, start, width):
+        got = ring.got
+        return jnp.concatenate(
+            [got[m, q, :, start : start + width] for m in range(2) for q in range(4)], axis=0
+        )
+
+    x_ring.arrive()
+    total = t_times(rows(x_ring, 0, 1024), rows(x_ring, 1024, 256)).astype(bf16)
+    total_qk = t_times(rows(x_ring, 1280, 256), rows(x_ring, 1536, 256)).astype(bf16)
+    for q in range(4):
+        for c in range(4):
+            td[q, c * 64 : (c + 1) * 64, :] = total[c * 256 + q * 64 : c * 256 + (q + 1) * 64]
+        td[q, 256:320, :] = total_qk[q * 64 : (q + 1) * 64]
+    for k in (2, 1, 3):
+        remote(td.at[(y + k) % 4], sd.at[y], dsem, dr.at[4 - k - 1], near_y(k)).start()
+    y_ring.arrive()
+    total = t_times(rows(y_ring, 0, 1024), rows(y_ring, 1024, 256)).astype(bf16)
+    for q in range(4):
+        for c in range(4):
+            tu[q, c * 64 : (c + 1) * 64, :] = total[c * 256 + q * 64 : c * 256 + (q + 1) * 64]
+    for k in (2, 1, 3):
+        remote(tu.at[(d + k) % 4], su.at[d], usem, ur.at[4 - k - 1], near_x(k)).start()
+
+    def gathered(buf, recv, position):
+        for k in (1, 2, 3):
+            ref = buf.at[(position + k) % 4]
+            remote(ref, ref, dsem, recv.at[k - 1], near_x(1)).wait_recv()
+        return [buf[(position + k) % 4] for k in (1, 2, 3)]
+
+    summed = fold([td[y]] + gathered(sd, dr, y)).astype(bf16)
+    for k in range(NZ):
+        zd[k, 0:32, :] = summed[k * 32 : (k + 1) * 32]
+        zd[k, 32:40, :] = summed[256 + k * 8 : 264 + k * 8]
+    for k in range(1, NZ):
+        remote(zd.at[(z + k) % NZ], zr.at[z], zsem.at[0], zrecv.at[0, NZ - k - 1], near_z(k)).start()
+    summed = fold([tu[d]] + gathered(su, ur, d)).astype(bf16)
+    for k in range(NZ):
+        zu[k] = summed[k * 32 : (k + 1) * 32]
+    for k in range(1, NZ):
+        remote(zu.at[(z + k) % NZ], zv.at[z], zsem.at[1], zrecv.at[1, NZ - k - 1], near_z(k)).start()
+
+    def last(own, buf, which):
+        for k in range(1, NZ):
+            ref = buf.at[(z + k) % NZ]
+            remote(ref, ref, zsem.at[0], zrecv.at[which, k - 1], near_z(1)).wait_recv()
+        return fold([own[z]] + [buf[(z + k) % NZ] for k in range(1, NZ)])
+
+    mine = last(zd, zr, 0)
+    down_o[...] = mine[0:28]
+    qk_o[...] = mine[32:34]
+    mine = last(zu, zv, 1)
+    up_o[...] = mine[0:28]
+
+    x_ring.drain()
+    y_ring.drain()
+    for k, (out, some) in enumerate(((act_o, act0), (grad_o, grad0))):
+        pltpu.make_async_copy(some, out.at[s], asem.at[k]).wait()
+        remote(some, out.at[1 - s], psem, qsem.at[k], {"section": 1 - s}).wait_recv()
+    whole = act_o
+    remote(whole, whole, psem, qsem.at[0], {"section": 1 - s}).wait_send()
+    ref = td.at[pl.ds(0, 3)]
+    remote(ref, ref, dsem, dr.at[0], near_x(1)).wait_send()
+    ref = tu.at[pl.ds(0, 3)]
+    remote(ref, ref, usem, ur.at[0], near_x(1)).wait_send()
+    ref = zd.at[pl.ds(0, NZ - 1)]
+    remote(ref, ref, zsem.at[0], dr.at[0], near_x(1)).wait_send()
+    ref = zu.at[pl.ds(0, NZ - 1)]
+    remote(ref, ref, zsem.at[1], dr.at[0], near_x(1)).wait_send()
+
+
+def weight_grads(layer0, layer1):
+    dma = pltpu.SemaphoreType.DMA
+    ring_sems = [dma, dma((2, 4)), dma((2,))]
+    return pl.pallas_call(
+        grads_kernel,
+        name="weight_grads",
+        out_shape=[
+            jax.ShapeDtypeStruct((2, SEQ, WIDTH), bf16),
+            jax.ShapeDtypeStruct((2, SEQ, WIDTH), bf16),
+            jax.ShapeDtypeStruct((28, LAT), f32),
+            jax.ShapeDtypeStruct((2, LAT), f32),
+            jax.ShapeDtypeStruct((28, LAT), f32),
+        ],
+        in_specs=[VMEM] * 16,
+        out_specs=[VMEM] * 5,
+        scratch_shapes=[
+            pltpu.VMEM((2, 4, SEQ, ROUND), bf16),
+            pltpu.VMEM((2, 4, SEQ, ROUND), bf16),
+            pltpu.VMEM((2, SEQ, ROUND), bf16),
+            pltpu.VMEM((2, 4, SEQ, SIDE), bf16),
+            pltpu.VMEM((2, 4, SEQ, SIDE), bf16),
+            pltpu.VMEM((2, SEQ, SIDE), bf16),
+            pltpu.VMEM((4, 320, LAT), bf16),
+            pltpu.VMEM((4, 320, LAT), bf16),
+            pltpu.VMEM((NZ, 40, LAT), bf16),
+            pltpu.VMEM((NZ, 40, LAT), bf16),
+            pltpu.VMEM((4, 256, LAT), bf16),
+            pltpu.VMEM((4, 256, LAT), bf16),
+            pltpu.VMEM((NZ, 32, LAT), bf16),
+            pltpu.VMEM((NZ, 32, LAT), bf16),
+        ]
+        + ring_sems * 2
+        + [dma, dma((2,)), dma((2,)), dma, dma((3,)), dma, dma((3,)), dma((2,)), dma((2, NZ - 1))],
+        compiler_params=pltpu.CompilerParams(collective_id=2, has_side_effects=True),
+    )(*layer0, *layer1)
 
 
 def body(x_in, dy_out, routes, gates, w_down, w_qk, w_up, e_gate, e_up, e_down):
@@ -650,29 +909,14 @@
     )
     layer0 = (n0, dl0, kept0[0], dq0, dr0, kept0[3], act0, grad0)
     layer1 = (n1, dl1, kept1[0], dq1, dr1, kept1[3], act1, grad1)
-    own = [jnp.where(section == 0, a, b) for a, b in zip(layer0, layer1)]
-    other = [swap(jnp.where(section == 0, b, a)) for a, b in zip(layer0, layer1)]
-    n1b, d_latent, latent, d_queries, d_resid, mixed = (
-        jnp.concatenate([a, b], axis=0) for a, b in zip(own[:6], other[:6])
-    )
-
-    def in_order(a, b):
-        return jnp.stack([jnp.where(section == 0, a, b), jnp.where(section == 0, b, a)])[
-            None, :, None
-        ]
-
-    activations = in_order(own[6], other[6])
-    grads_in = in_order(own[7], other[7])
-
-    def scattered(left, right, per):
-        total = t_times(spaced(left, per), right)
-        mine = lax.psum_scatter(total, ("expert", "dp"), scatter_dimension=0, tiled=True)
-        return mine[None, :per]
-
-    g_down = scattered(n1b, d_latent, 28)
-    g_qk = scattered(latent, d_queries, 2)
-    g_up_t = scattered(d_resid, mixed, 28)
-    return (activations, grads_in, g_down, g_qk, g_up_t)
+    activations, grads_in, g_down, g_qk, g_up_t = weight_grads(layer0, layer1)
+    return (
+        activations[None, :, None],
+        grads_in[None, :, None],
+        g_down[None],
+        g_qk[None],
+        g_up_t[None],
+    )
 
 
 def solution(mesh):

time: 2530 us -> 457 us (0.18)
  the two profiles are of different devices: /device:TPU:0 before, /device:TPU:1 now
where the time goes in v2:
time: 457 us; the launch traced here: 448 us
  Pallas kernels  427 us (93%)
  local copies, waits for them, and re-layouts  12.1 us (3%)
  starting transfers between devices  5 us (1%)
    pallas_call x4, Pallas kernels, combine(): pl.pallas_call(combine_kernel, name='combine', out_shape=jax.ShapeDtypeSt...  149 us
    pallas_call x4, Pallas kernels, dispatch(): pl.pallas_call(dispatch_kernel, name='dispatch', out_shape=jax.ShapeDtype...  138 us
    pallas_call x1, Pallas kernels, weight_grads(): pl.pallas_call(grads_kernel, name='weight_grads', out_shape=[jax.ShapeDty...  63.6 us
    pallas_call x2, Pallas kernels, expert_backward(): pl.pallas_call(functools.partial(expert_backward_kernel, layer), name=f'e...  23.1 us
    pallas_call x2, Pallas kernels, expert_forward(): pl.pallas_call(functools.partial(expert_forward_kernel, layer), name=f'ex...  21.1 us
    pallas_call x2, Pallas kernels, backward(): pl.pallas_call(functools.partial(back_kernel, layer, last), name=f'backwa...  15.9 us
  transfers between devices with their start and end apart: 8, of which 2 were waited for; matrix products, arithmetic and copies ran while one was open for 1% of the time, Pallas kernels for 11%

profile of v2, /device:TPU:1, one launch (start us, length us, event | category | flops | bytes accessed | tf_op | source)
XLA Modules:
  0.0 448.1 jit_solution(11869194406792931534)
XLA Ops:
  0.6 0.0 copy-start
  0.6 3.3 collective-permute-start.2
  3.9 0.7 fusion.1
  4.6 0.1 copy.25
  4.7 0.1 collective-permute-start
  4.8 0.7 fusion.3
  5.5 0.1 copy.27
  5.6 0.5 collective-permute-start.7
  6.1 0.1 collective-permute-start.1
  6.2 0.4 collective-permute-start.3
  6.6 0.0 collective-permute-done
  6.6 0.1 collective-permute-start.4
  6.7 0.2 collective-permute-done.7
  6.9 0.3 collective-permute-start.5
  7.3 0.2 collective-permute-start.6
  7.4 0.1 copy.28
  7.5 0.1 copy.26
  7.6 0.8 dynamic-slice_bitcast_fusion.1.x.inputs
  8.4 1.8 dynamic-slice_bitcast_fusion.upstream
  10.3 1.2 fusion.4
  11.5 0.6 broadcast_select_fusion
  12.1 0.0 collective-permute-done.1.wd1
  12.1 0.7 collective-permute-done.3.wu1
  12.8 6.0 %first.1 = (bf16[256,1536]{1,0:T(8,128)(2,1)}, bf16[64,3584]{1,0:T(8,128)(2,1)}, bf16[64,256]{1,0:T(8,128)(2,1)}, bf16[64,256]{1,0:T(8,128)(2,1)}, f32[64,64]{1,0:T(8,128)}, /*index=5*/bf16[64,256]{1,0:T(8,128)(2,1)}) custom-call(bf16[64,3584]{1,0:T(8,128)(2,1)} %dynamic-slice_bitcast_fusion.1.x.inputs, s32[1,64]{1,0:T(1,128)} %bitcast.95, ...), custom_call_target="tpu_custom_call" | custom-call | tf_op jit(solution)/shard_map/first/pallas_call | solution.py:372
  18.9 43.9 %dispatch.4 = bf16[128,8,1536]{2,1,0:T(8,128)(2,1)} custom-call(bf16[32,8,1536]{2,1,0:T(8,128)(2,1)} %bitcast.91), custom_call_target="tpu_custom_call" | custom-call | tf_op jit(solution)/shard_map/dispatch/pallas_call | solution.py:194
  62.8 0.0 collective-permute-done.4.gw1
  62.8 1.2 copy-done.1
  64.0 10.6 %expert_forward0.1 = (bf16[1024,1536]{1,0:T(8,128)(2,1)}, f32[384,256]{1,0:T(8,128)}, f32[384,256]{1,0:T(8,128)}) custom-call(bf16[1024,1536]{1,0:T(8,128)(2,1)} %bitcast.70, bf16[3584,256]{1,0:T(8,128)(2,1)} %bitcast.46, bf16[3584,256]{1,0:T(8,128)(2,1)} %bitcast.51, bf16[256,3584]{1,0:T(8,128)(2,1)} %bitcast.56, bf16[3584,256]{1,0:T(8,128)(2,1)} %copy-done.1, ...), custom_call_target="tpu_custom_call" | custom-call | tf_op jit(solution)/shard_map/expert_forward0/pallas_call | solution.py:569
  74.6 42.4 %combine.4 = bf16[32,8,1536]{2,1,0:T(8,128)(2,1)} custom-call(bf16[128,8,1536]{2,1,0:T(8,128)(2,1)} %bitcast.76), custom_call_target="tpu_custom_call" | custom-call | tf_op jit(solution)/shard_map/combine/pallas_call | solution.py:277
  117.0 6.9 %second.1 = (bf16[64,3584]{1,0:T(8,128)(2,1)}, bf16[256,1536]{1,0:T(8,128)(2,1)}, bf16[64,3584]{1,0:T(8,128)(2,1)}, bf16[64,256]{1,0:T(8,128)(2,1)}, bf16[64,256...) custom-call(bf16[256,1536]{1,0:T(8,128)(2,1)} %bitcast.80, bf16[64,3584]{1,0:T(8,128)(2,1)} %get-tuple-element.44.resid_in, ...), custom_call_target="tpu_custom_call" | custom-call | tf_op jit(solution)/shard_map/second/pallas_call | solution.py:397
  124.0 31.9 %dispatch.5 = bf16[128,8,1536]{2,1,0:T(8,128)(2,1)} custom-call(bf16[32,8,1536]{2,1,0:T(8,128)(2,1)} %bitcast.90), custom_call_target="tpu_custom_call" | custom-call | tf_op jit(solution)/shard_map/dispatch/pallas_call | solution.py:194
  155.9 10.5 %expert_forward1.1 = (bf16[1024,1536]{1,0:T(8,128)(2,1)}, f32[384,256]{1,0:T(8,128)}, f32[384,256]{1,0:T(8,128)}) custom-call(bf16[1024,1536]{1,0:T(8,128)(2,1)} %bitcast.71, bf16[3584,256]{1,0:T(8,128)(2,1)} %bitcast.47, bf16[3584,256]{1,0:T(8,128)(2,1)} %bitcast.52, bf16[256,3584]{1,0:T(8,128)(2,1)} %bitcast.57, bf16[3584,256]{1,0:T(8,128)(2,1)} %copy-done.1, ...), custom_call_target="tpu_custom_call" | custom-call | tf_op jit(solution)/shard_map/expert_forward1/pallas_call | solution.py:569
  166.4 37.4 %combine.5 = bf16[32,8,1536]{2,1,0:T(8,128)(2,1)} custom-call(bf16[128,8,1536]{2,1,0:T(8,128)(2,1)} %bitcast.77), custom_call_target="tpu_custom_call" | custom-call | tf_op jit(solution)/shard_map/combine/pallas_call | solution.py:277
  203.9 3.5 third.1
  207.4 33.3 %dispatch.6 = bf16[128,8,1536]{2,1,0:T(8,128)(2,1)} custom-call(bf16[32,8,1536]{2,1,0:T(8,128)(2,1)} %bitcast.92), custom_call_target="tpu_custom_call" | custom-call | tf_op jit(solution)/shard_map/dispatch/pallas_call | solution.py:194
  240.7 11.5 %expert_backward1.1 = bf16[1024,1536]{1,0:T(8,128)(2,1)} custom-call(bf16[1024,1536]{1,0:T(8,128)(2,1)} %bitcast.74, f32[384,256]{1,0:T(8,128)} %get-tuple-element.49.gate_i, f32[384,256]{1,0:T(8,128)} %get-tuple-element.50.up_i, bf16[3584,256]{1,0:T(8,128)(2,1)} %bitcast.48, bf16[3584,256]{1,0:T(8,128)(2,1)} %bitcast.53, bf16[256,3584]{1,0:T(8,128)(2,1)} %bitcast.58, ...), custom_call_target="tpu_custom_call" | custom-call | tf_op jit(solution)/shard_map/expert_backward1/pallas_call | solution.py:580
  252.3 35.1 %combine.6 = bf16[32,8,1536]{2,1,0:T(8,128)(2,1)} custom-call(bf16[128,8,1536]{2,1,0:T(8,128)(2,1)} %bitcast.75), custom_call_target="tpu_custom_call" | custom-call | tf_op jit(solution)/shard_map/combine/pallas_call | solution.py:277
  287.4 8.2 %backward1.1 = (bf16[64,3584]{1,0:T(8,128)(2,1)}, bf16[64,3584]{1,0:T(8,128)(2,1)}, bf16[64,256]{1,0:T(8,128)(2,1)}, bf16[64,256]{1,0:T(8,128)(2,1)}, bf16[64,35...) custom-call(bf16[256,1536]{1,0:T(8,128)(2,1)} %bitcast.79, bf16[64,3584]{1,0:T(8,128)(2,1)} %get-tuple-element.47.resid_in, ...), custom_call_target="tpu_custom_call" | custom-call | tf_op jit(solution)/shard_map/backward1/pallas_call | solution.py:478
  295.6 29.0 %dispatch.7 = bf16[128,8,1536]{2,1,0:T(8,128)(2,1)} custom-call(bf16[32,8,1536]{2,1,0:T(8,128)(2,1)} %bitcast.89), custom_call_target="tpu_custom_call" | custom-call | tf_op jit(solution)/shard_map/dispatch/pallas_call | solution.py:194
  324.7 11.5 %expert_backward0.1 = bf16[1024,1536]{1,0:T(8,128)(2,1)} custom-call(bf16[1024,1536]{1,0:T(8,128)(2,1)} %bitcast.72, f32[384,256]{1,0:T(8,128)} %get-tuple-element.57.gate_i, f32[384,256]{1,0:T(8,128)} %get-tuple-element.58.up_i, bf16[3584,256]{1,0:T(8,128)(2,1)} %bitcast.49, bf16[3584,256]{1,0:T(8,128)(2,1)} %bitcast.54, bf16[256,3584]{1,0:T(8,128)(2,1)} %bitcast.59, ...), custom_call_target="tpu_custom_call" | custom-call | tf_op jit(solution)/shard_map/expert_backward0/pallas_call | solution.py:580
  336.3 33.6 %combine.7 = bf16[32,8,1536]{2,1,0:T(8,128)(2,1)} custom-call(bf16[128,8,1536]{2,1,0:T(8,128)(2,1)} %bitcast.73), custom_call_target="tpu_custom_call" | custom-call | tf_op jit(solution)/shard_map/combine/pallas_call | solution.py:277
  369.8 7.7 %backward0.1 = (bf16[64,3584]{1,0:T(8,128)(2,1)}, bf16[64,3584]{1,0:T(8,128)(2,1)}, bf16[64,256]{1,0:T(8,128)(2,1)}, bf16[64,256]{1,0:T(8,128)(2,1)}, bf16[64,3584]{1,0:T(8,128)(2,1)}) custom-call(bf16[256,1536]{1,0:T(8,128)(2,1)} %bitcast.78, bf16[64,3584]{1,0:T(8,128)(2,1)} %get-tuple-element.44.resid_in, ...), custom_call_target="tpu_custom_call" | custom-call | tf_op jit(solution)/shard_map/backward0/pallas_call | solution.py:478
  377.5 63.6 %weight_grads.1 = (bf16[2,64,3584]{2,1,0:T(8,128)(2,1)}, bf16[2,64,3584]{2,1,0:T(8,128)(2,1)}, f32[28,256]{1,0:T(8,128)}, f32[2,256]{1,0:T(2,128)}, f32[28,256]{1,0:T(8,128)}) custom-call(bf16[64,3584]{1,0:T(8,128)(2,1)} %get-tuple-element.64.n0, bf16[64,256]{1,0:T(8,128)(2,1)} %get-tuple-element.65.dl0, bf16[64,256]{1,0:T(8,128)(2,1)} %get-tuple-element.60.latent_i.la0, ...), custom_call_target="tpu_custom_call" | custom-call | tf_op jit(solution)/shard_map/weight_grads/pallas_call | solution.py:835
  441.1 1.5 copy.33
  442.6 1.4 copy.34
  444.0 2.2 copy.38
  446.1 0.9 copy.39
  447.0 0.6 copy.40
  (11 shorter events, 0.0 us)
Async XLA Ops:
  0.6 7.0 %copy-start = (bf16[2,1,64,3584]{3,2,1,0:T(8,128)(2,1)S(1)}, bf16[2,1,64,3584]{3,2,1,0:T(8,128)(2,1)}, u32[]{:S(2)}) copy-start(bf16[2,1,64,3584]{3,2,1,0:T(8,128)(2,1)} %param.10) | copy-start | bytes 2752516
  0.6 6.6 %collective-permute-start.2 = (bf16[256,256]{1,0:T(8,128)(2,1)}, bf16[256,256]{1,0:T(8,128)(2,1)S(1)}, u32[]{:S(2)}, u32[]{:S(2)}) collective-permute-start(bf16[256,256]{1,0:T(8,128)(2,1)} %bitcast.82), channel_id=1, source_target_pairs={{0,128},{128,0},{1,129},{129,1},{2,130},{130,2},{3,131},{131,3},{4... | collective-permute-start | bytes 393224 | tf_op jit(solution)/shard_map/ppermute | solution.py:599
  4.7 1.9 collective-permute-start
  5.6 1.3 collective-permute-start.7
  6.1 6.1 %collective-permute-start.1 = (bf16[3584,256]{1,0:T(8,128)(2,1)}, bf16[3584,256]{1,0:T(8,128)(2,1)}, u32[]{:S(2)}, u32[]{:S(2)}) collective-permute-start(bf16[3584,256]{1,0:T(8,128)(2,1)} %bitcast.60), channel_id=1, source_target_pairs={{0,128},{128,0},{1,129},{129,1},{2,130},{130,2},{3,131},{131,3},{4... | collective-permute-start | bytes 5505032 | tf_op jit(solution)/shard_map/ppermute | solution.py:599
  6.2 6.7 %collective-permute-start.3 = (bf16[256,3584]{1,0:T(8,128)(2,1)}, bf16[256,3584]{1,0:T(8,128)(2,1)}, u32[]{:S(2)}, u32[]{:S(2)}) collective-permute-start(bf16[256,3584]{1,0:T(8,128)(2,1)} %bitcast.65), channel_id=1, source_target_pairs={{0,128},{128,0},{1,129},{129,1},{2,130},{130,2},{3,131},{131,3},{4... | collective-permute-start | bytes 5505032 | tf_op jit(solution)/shard_map/ppermute | solution.py:599
  6.6 56.2 %collective-permute-start.4 = (bf16[3584,256]{1,0:T(8,128)(2,1)}, bf16[3584,256]{1,0:T(8,128)(2,1)S(1)}, u32[]{:S(2)}, u32[]{:S(2)}) collective-permute-start(bf16[3584,256]{1,0:T(8,128)(2,1)} %bitcast.45), channel_id=1, source_target_pairs={{0,128},{128,0},{1,129},{129,1},{2,130},{130,2},{3,131},{131,3},{4... | collective-permute-start | bytes 5505032 | tf_op jit(solution)/shard_map/ppermute | solution.py:599
  6.9 55.9 %collective-permute-start.5 = (bf16[3584,256]{1,0:T(8,128)(2,1)}, bf16[3584,256]{1,0:T(8,128)(2,1)}, u32[]{:S(2)}, u32[]{:S(2)}) collective-permute-start(bf16[3584,256]{1,0:T(8,128)(2,1)} %bitcast.50), channel_id=1, source_target_pairs={{0,128},{128,0},{1,129},{129,1},{2,130},{130,2},{3,131},{131,3},{4... | collective-permute-start | bytes 5505032 | tf_op jit(solution)/shard_map/ppermute | solution.py:599
  7.3 5.5 %copy-start.2 = (bf16[256,256]{1,0:T(8,128)(2,1)}, bf16[256,256]{1,0:T(8,128)(2,1)S(1)}, u32[]{:S(2)}) copy-start(bf16[256,256]{1,0:T(8,128)(2,1)S(1)} %collective-permute-done.2.wq1) | copy-start | bytes 393220
  7.3 55.5 %collective-permute-start.6 = (bf16[256,3584]{1,0:T(8,128)(2,1)}, bf16[256,3584]{1,0:T(8,128)(2,1)}, u32[]{:S(2)}, u32[]{:S(2)}) collective-permute-start(bf16[256,3584]{1,0:T(8,128)(2,1)} %bitcast.55), channel_id=1, source_target_pairs={{0,128},{128,0},{1,129},{129,1},{2,130},{130,2},{3,131},{131,3},{4... | collective-permute-start | bytes 5505032 | tf_op jit(solution)/shard_map/ppermute | solution.py:599
  62.8 1.2 copy-start.1
  441.1 5.0 %copy-start.3 = (bf16[2,64,3584]{2,1,0:T(8,128)(2,1)S(1)}, bf16[2,64,3584]{2,1,0:T(8,128)(2,1)}, u32[]{:S(2)}) copy-start(bf16[2,64,3584]{2,1,0:T(8,128)(2,1)} %get-tuple-element.75) | copy-start | bytes 2752516
  444.0 3.1 copy-start.4

commit v3 on v2

--- a/solution.py
+++ b/solution.py
@@ -98,11 +98,11 @@
             packed_ref[r * EXPERTS : (r + 1) * EXPERTS, s * PIECE : (s + 1) * PIECE] = picked[
                 s * EXPERTS : (s + 1) * EXPERTS, r * PIECE : (r + 1) * PIECE
             ]
-    blocks_ref[...] = dot(spread_matrix(), packed_ref[...]).astype(bf16)
+    blocks_ref[...] = dot(spread_matrix(), packed_ref[...]).astype(bf16).reshape(HOME)
 
 
 def unpack_tokens(blocks_ref, route_col, token_ref):
-    packed = dot(gather_matrix(), blocks_ref[...]).astype(bf16)
+    packed = dot(gather_matrix(), blocks_ref[...].reshape(EXPERTS * 8, BLOCK[1])).astype(bf16)
     columns = slot_columns(route_col)
     for r in range(PIECES):
         stacked = jnp.concatenate(
@@ -121,7 +121,7 @@
     return e, d, e // NY, e % NY, (d + 1) % DP, (d + DP - 1) % DP, (d + 2) % DP
 
 
-def meet(e, right, left):
+def greet(e, right, left):
     barrier = pltpu.get_barrier_semaphore()
     for k in range(1, EXPERTS):
         pl.semaphore_signal(
@@ -129,7 +129,10 @@
         )
     for side in (right, left):
         pl.semaphore_signal(barrier, inc=1, device_id={"dp": side}, device_id_type=MESH)
-    pl.semaphore_wait(barrier, EXPERTS + 1)
+
+
+def greeted():
+    pl.semaphore_wait(pltpu.get_barrier_semaphore(), EXPERTS + 1)
 
 
 def remote(src, dst, send, recv, where):
@@ -138,159 +141,160 @@
     )
 
 
-def dispatch_kernel(blk, rows, s1, sx, r1, rl, rr, ro):
-    e, d, z, y, right, left, opp = places()
-    meet(e, right, left)
-    for j in ORDER:
-        for dy in range(NY):
-            if j == 0 and dy == 0:
-                pltpu.make_async_copy(blk.at[e], rows.at[d * EXPERTS + e], r1.at[0]).start()
+class Dispatch:
+    sems = (
+        pltpu.SemaphoreType.DMA,
+        pltpu.SemaphoreType.DMA,
+        pltpu.SemaphoreType.DMA((NZ,)),
+        pltpu.SemaphoreType.DMA((NZ,)),
+        pltpu.SemaphoreType.DMA((NZ,)),
+        pltpu.SemaphoreType.DMA((NZ,)),
+    )
+
+    def __init__(self, blk, rows, sems):
+        self.blk, self.rows = blk, rows
+        self.s1, self.sx, self.r1, self.rl, self.rr, self.ro = sems
+        self.e, self.d, self.z, self.y, self.right, self.left, self.opp = places()
+
+    def start(self):
+        for j in ORDER:
+            for dy in range(NY):
+                spot = self.rows.at[self.d * EXPERTS + self.e]
+                if j == 0 and dy == 0:
+                    pltpu.make_async_copy(self.blk.at[self.e], spot, self.r1.at[0]).start()
+                else:
+                    peer = ((self.z + j) % NZ) * NY + (self.y + dy) % NY
+                    remote(
+                        self.blk.at[peer], spot, self.s1, self.r1.at[(NZ - j) % NZ], {"expert": peer}
+                    ).start()
+
+    def group(self, owner, j):
+        return self.rows.at[pl.ds(owner * EXPERTS + ((self.z + j) % NZ) * NY, NY)]
+
+    def arrived(self, ref, sem):
+        remote(ref, ref, self.s1, sem, {"dp": self.right}).wait_recv()
+
+    def forward(self, i):
+        j = ORDER[i]
+        mine = self.group(self.d, j)
+        self.arrived(mine, self.r1.at[j])
+        remote(mine, mine, self.sx, self.rl.at[j], {"dp": self.right}).start()
+        remote(mine, mine, self.sx, self.rr.at[j], {"dp": self.left}).start()
+
+    def relay(self, i):
+        j = ORDER[i]
+        owner, sem, to = (
+            (self.left, self.rl, self.right) if i % 2 == 0 else (self.right, self.rr, self.left)
+        )
+        ref = self.group(owner, j)
+        self.arrived(ref, sem.at[j])
+        remote(ref, ref, self.sx, self.ro.at[j], {"dp": to}).start()
+
+    def rest(self, use):
+        use(self.d)
+        for i, j in enumerate(ORDER):
+            if i % 2 == 0:
+                self.arrived(self.group(self.right, j), self.rr.at[j])
+        use(self.right)
+        for i, j in enumerate(ORDER):
+            if i % 2 == 1:
+                self.arrived(self.group(self.left, j), self.rl.at[j])
+        use(self.left)
+        for j in ORDER:
+            self.arrived(self.group(self.opp, j), self.ro.at[j])
+        use(self.opp)
+
+    def drain(self):
+        sent = self.blk.at[pl.ds(0, EXPERTS - 1)]
+        remote(sent, sent, self.s1, self.r1.at[0], {"dp": self.right}).wait_send()
+        sent = self.rows.at[pl.ds(0, 3 * EXPERTS)]
+        remote(sent, sent, self.sx, self.r1.at[0], {"dp": self.right}).wait_send()
+
+
+class Combine:
+    sems = (
+        pltpu.SemaphoreType.DMA,
+        pltpu.SemaphoreType.DMA,
+        pltpu.SemaphoreType.DMA((NZ,)),
+        pltpu.SemaphoreType.DMA((NZ,)),
+        pltpu.SemaphoreType.DMA((NZ,)),
+        pltpu.SemaphoreType.DMA,
+    )
+    buffers = (pltpu.VMEM((EXPERTS, *BLOCK), bf16),) * 5
+
+    def __init__(self, part, out, buffers, sems):
+        self.part, self.out = part, out
+        self.relayed, self.relay_sum, self.from_left, self.from_right, self.final = buffers
+        self.sx, self.s1, self.ra, self.rl, self.rr, self.rh = sems
+        self.e, self.d, self.z, self.y, self.right, self.left, self.opp = places()
+
+    def group(self, owner, j):
+        return self.part.at[pl.ds(owner * EXPERTS + ((self.z + j) % NZ) * NY, NY)]
+
+    def spot(self, ref, i):
+        return ref.at[pl.ds(i * NY, NY)]
+
+    def arrived(self, ref, sem):
+        remote(ref, ref, self.s1, sem, {"dp": self.right}).wait_recv()
+
+    def start_far(self):
+        for i, j in enumerate(ORDER):
+            side = self.right if i % 2 == 0 else self.left
+            remote(
+                self.group(self.opp, j), self.spot(self.relayed, i), self.sx, self.ra.at[i], {"dp": side}
+            ).start()
+
+    def start_near(self):
+        for i, j in enumerate(ORDER):
+            if i % 2 == 0:
+                ref, to, sem, side = self.left, self.from_right, self.rr, self.left
             else:
-                peer = ((z + j) % NZ) * NY + (y + dy) % NY
-                remote(
-                    blk.at[peer],
-                    rows.at[d * EXPERTS + e],
-                    s1,
-                    r1.at[(NZ - j) % NZ],
-                    {"expert": peer},
-                ).start()
-
-    def group(owner, j):
-        return rows.at[pl.ds(owner * EXPERTS + ((z + j) % NZ) * NY, NY)]
-
-    def arrived(ref, sem):
-        remote(ref, ref, s1, sem, {"dp": right}).wait_recv()
-
-    def relay(i):
+                ref, to, sem, side = self.right, self.from_left, self.rl, self.right
+            remote(self.group(ref, j), self.spot(to, i), self.sx, sem.at[i], {"dp": side}).start()
+
+    def relay(self, i):
         j = ORDER[i]
-        if i % 2 == 0:
-            arrived(group(left, j), rl.at[j])
-            remote(group(left, j), group(left, j), sx, ro.at[j], {"dp": right}).start()
-        else:
-            arrived(group(right, j), rr.at[j])
-            remote(group(right, j), group(right, j), sx, ro.at[j], {"dp": left}).start()
-
-    for i, j in enumerate(ORDER):
-        arrived(group(d, j), r1.at[j])
-        remote(group(d, j), group(d, j), sx, rl.at[j], {"dp": right}).start()
-        remote(group(d, j), group(d, j), sx, rr.at[j], {"dp": left}).start()
-        if i >= 2:
-            relay(i - 2)
-    relay(NZ - 2)
-    relay(NZ - 1)
-    for i, j in enumerate(ORDER):
-        if i % 2 == 0:
-            arrived(group(right, j), rr.at[j])
-        else:
-            arrived(group(left, j), rl.at[j])
-        arrived(group(opp, j), ro.at[j])
-    sent = blk.at[pl.ds(0, EXPERTS - 1)]
-    remote(sent, sent, s1, r1.at[0], {"dp": right}).wait_send()
-    sent = rows.at[pl.ds(0, 3 * EXPERTS)]
-    remote(sent, sent, sx, r1.at[0], {"dp": right}).wait_send()
-
-
-def dispatch(blocks):
-    return pl.pallas_call(
-        dispatch_kernel,
-        name="dispatch",
-        out_shape=jax.ShapeDtypeStruct((DP * EXPERTS, *BLOCK), bf16),
-        in_specs=[VMEM],
-        out_specs=VMEM,
-        scratch_shapes=[
-            pltpu.SemaphoreType.DMA,
-            pltpu.SemaphoreType.DMA,
-            pltpu.SemaphoreType.DMA((NZ,)),
-            pltpu.SemaphoreType.DMA((NZ,)),
-            pltpu.SemaphoreType.DMA((NZ,)),
-            pltpu.SemaphoreType.DMA((NZ,)),
-        ],
-        compiler_params=pltpu.CompilerParams(collective_id=0, has_side_effects=True),
-    )(blocks)
-
-
-def combine_kernel(
-    part, out, relayed, relay_sum, from_left, from_right, final, sx, s1, ra, rl, rr, rh
-):
-    e, d, z, y, right, left, opp = places()
-    meet(e, right, left)
-
-    def group(owner, j):
-        return part.at[pl.ds(owner * EXPERTS + ((z + j) % NZ) * NY, NY)]
-
-    def spot(ref, i):
-        return ref.at[pl.ds(i * NY, NY)]
-
-    def arrived(ref, sem):
-        remote(ref, ref, s1, sem, {"dp": right}).wait_recv()
-
-    for i, j in enumerate(ORDER):
-        side = right if i % 2 == 0 else left
-        remote(group(opp, j), spot(relayed, i), sx, ra.at[i], {"dp": side}).start()
-    for i, j in enumerate(ORDER):
-        if i % 2 == 0:
-            remote(group(left, j), spot(from_right, i), sx, rr.at[i], {"dp": left}).start()
-        else:
-            remote(group(right, j), spot(from_left, i), sx, rl.at[i], {"dp": right}).start()
-
-    def relay(i):
+        self.arrived(self.spot(self.relayed, i), self.ra.at[i])
+        side, to, sem = (
+            (self.right, self.from_left, self.rl)
+            if i % 2 == 0
+            else (self.left, self.from_right, self.rr)
+        )
+        self.spot(self.relay_sum, i)[...] = (
+            self.spot(self.relayed, i)[...].astype(f32) + self.group(side, j)[...].astype(f32)
+        ).astype(bf16)
+        remote(
+            self.spot(self.relay_sum, i), self.spot(to, i), self.sx, sem.at[i], {"dp": side}
+        ).start()
+
+    def finish(self, i):
         j = ORDER[i]
-        arrived(spot(relayed, i), ra.at[i])
-        side = right if i % 2 == 0 else left
-        spot(relay_sum, i)[...] = (
-            spot(relayed, i)[...].astype(f32) + group(side, j)[...].astype(f32)
-        ).astype(bf16)
-        if i % 2 == 0:
-            remote(spot(relay_sum, i), spot(from_left, i), sx, rl.at[i], {"dp": right}).start()
-        else:
-            remote(spot(relay_sum, i), spot(from_right, i), sx, rr.at[i], {"dp": left}).start()
-
-    def finish(i):
-        j = ORDER[i]
-        arrived(spot(from_left, i), rl.at[i])
-        arrived(spot(from_right, i), rr.at[i])
-        spot(final, i)[...] = (
-            group(d, j)[...].astype(f32)
-            + spot(from_left, i)[...].astype(f32)
-            + spot(from_right, i)[...].astype(f32)
+        self.arrived(self.spot(self.from_left, i), self.rl.at[i])
+        self.arrived(self.spot(self.from_right, i), self.rr.at[i])
+        self.spot(self.final, i)[...] = (
+            self.group(self.d, j)[...].astype(f32)
+            + self.spot(self.from_left, i)[...].astype(f32)
+            + self.spot(self.from_right, i)[...].astype(f32)
         ).astype(bf16)
         for dy in range(NY):
-            yy = (y + dy) % NY
+            yy = (self.y + dy) % NY
+            spot = self.out.at[self.e]
             if j == 0 and dy == 0:
-                pltpu.make_async_copy(final.at[i * NY + yy], out.at[e], rh).start()
+                pltpu.make_async_copy(self.final.at[i * NY + yy], spot, self.rh).start()
             else:
-                peer = ((z + j) % NZ) * NY + yy
-                remote(final.at[i * NY + yy], out.at[e], s1, rh, {"expert": peer}).start()
-
-    for i in range(NZ):
-        relay(i)
-    for i in range(NZ):
-        finish(i)
-    arrived(out, rh)
-    sent = part.at[pl.ds(0, 3 * EXPERTS)]
-    remote(sent, sent, sx, rh, {"dp": right}).wait_send()
-    sent = part.at[pl.ds(0, EXPERTS - 1)]
-    remote(sent, sent, s1, rh, {"dp": right}).wait_send()
-
-
-def combine(partials):
-    return pl.pallas_call(
-        combine_kernel,
-        name="combine",
-        out_shape=jax.ShapeDtypeStruct((EXPERTS, *BLOCK), bf16),
-        in_specs=[VMEM],
-        out_specs=VMEM,
-        scratch_shapes=[pltpu.VMEM((EXPERTS, *BLOCK), bf16)] * 5
-        + [
-            pltpu.SemaphoreType.DMA,
-            pltpu.SemaphoreType.DMA,
-            pltpu.SemaphoreType.DMA((NZ,)),
-            pltpu.SemaphoreType.DMA((NZ,)),
-            pltpu.SemaphoreType.DMA((NZ,)),
-            pltpu.SemaphoreType.DMA,
-        ],
-        compiler_params=pltpu.CompilerParams(collective_id=1, has_side_effects=True),
-    )(partials)
+                peer = ((self.z + j) % NZ) * NY + yy
+                remote(
+                    self.final.at[i * NY + yy], spot, self.s1, self.rh, {"expert": peer}
+                ).start()
+
+    def arrive(self):
+        self.arrived(self.out, self.rh)
+
+    def drain(self):
+        sent = self.part.at[pl.ds(0, 3 * EXPERTS)]
+        remote(sent, sent, self.sx, self.rh, {"dp": self.right}).wait_send()
+        sent = self.part.at[pl.ds(0, EXPERTS - 1)]
+        remote(sent, sent, self.s1, self.rh, {"dp": self.right}).wait_send()
 
 
 def fetch(layer, pairs, sems):
@@ -339,107 +343,16 @@
     pack_tokens(normed2.astype(bf16), route_row, packed, blocks)
 
 
-ATTN_SCRATCH = [
-    pltpu.VMEM((WIDTH, LAT), bf16),
-    pltpu.VMEM((LAT, LAT), bf16),
-    pltpu.VMEM((LAT, WIDTH), bf16),
-    pltpu.SemaphoreType.DMA((3,)),
-]
-ATTN_OUT = [
-    jax.ShapeDtypeStruct((EXPERTS * 8, BLOCK[1]), bf16),
-    jax.ShapeDtypeStruct((SEQ, WIDTH), bf16),
-    jax.ShapeDtypeStruct((SEQ, LAT), bf16),
-    jax.ShapeDtypeStruct((SEQ, LAT), bf16),
-    jax.ShapeDtypeStruct((SEQ, SEQ), f32),
-    jax.ShapeDtypeStruct((SEQ, LAT), bf16),
-]
-PACK_SCRATCH = [pltpu.VMEM((PACKED, BLOCK[1]), bf16)]
-TOKEN_SCRATCH = [pltpu.VMEM((SEQ, WIDTH), f32)]
-
-
-def first_kernel(
-    x, route_row, wd0, wq0, wu0, wd1, wq1, wu1, blocks, residual, latent, queries, probs, mixed,
-    packed, wd, wq, wu, sems,
+def attend_back(
+    upstream, inputs, resid, latent, queries, probs, mixed, w, wait, tokens, normed_o, d_latent_o,
+    d_queries_o, d_resid_o, grad,
 ):
-    wait = fetch(0, ((wd0, wd1, wd), (wq0, wq1, wq), (wu0, wu1, wu)), sems)
-    attend(
-        x[...], route_row[...], wd, wq, wu, wait, packed, blocks, residual, latent, queries, probs,
-        mixed,
-    )
-
-
-def first(x, route_row, attn):
-    return pl.pallas_call(
-        first_kernel,
-        name="first",
-        out_shape=ATTN_OUT,
-        in_specs=[VMEM] * 2 + [ANY] * 6,
-        out_specs=[VMEM] * 6,
-        scratch_shapes=PACK_SCRATCH + ATTN_SCRATCH,
-    )(x, route_row, *attn)
-
-
-def second_kernel(
-    back, resid_in, gate_col, route_col, route_row, wd0, wq0, wu0, wd1, wq1, wu1,
-    act, blocks, residual, latent, queries, probs, mixed, tokens, packed, wd, wq, wu, sems,
-):
-    wait = fetch(1, ((wd0, wd1, wd), (wq0, wq1, wq), (wu0, wu1, wu)), sems)
-    unpack_tokens(back, route_col[...], tokens)
-    hidden = (resid_in[...].astype(f32) + gate_col[...] * tokens[...]).astype(bf16)
-    act[...] = hidden
-    attend(
-        hidden, route_row[...], wd, wq, wu, wait, packed, blocks, residual, latent, queries, probs,
-        mixed,
-    )
-
-
-def second(back, residual, gate_col, route_col, route_row, attn):
-    return pl.pallas_call(
-        second_kernel,
-        name="second",
-        out_shape=[jax.ShapeDtypeStruct((SEQ, WIDTH), bf16)] + ATTN_OUT,
-        in_specs=[VMEM] * 5 + [ANY] * 6,
-        out_specs=[VMEM] * 7,
-        scratch_shapes=TOKEN_SCRATCH + PACK_SCRATCH + ATTN_SCRATCH,
-    )(back, residual, gate_col, route_col, route_row, *attn)
-
-
-def third_kernel(
-    back, resid_in, gate_col, route_col, route_row, upstream, act, blocks, tokens, packed
-):
-    scaled = (gate_col[...] * upstream[...].astype(f32)).astype(bf16)
-    pack_tokens(scaled, route_row[...], packed, blocks)
-    unpack_tokens(back, route_col[...], tokens)
-    act[...] = (resid_in[...].astype(f32) + gate_col[...] * tokens[...]).astype(bf16)
-
-
-def third(back, residual, gate_col, route_col, route_row, upstream):
-    return pl.pallas_call(
-        third_kernel,
-        name="third",
-        out_shape=[jax.ShapeDtypeStruct((SEQ, WIDTH), bf16), ATTN_OUT[0]],
-        in_specs=[VMEM] * 6,
-        out_specs=[VMEM] * 2,
-        scratch_shapes=TOKEN_SCRATCH + PACK_SCRATCH,
-    )(back, residual, gate_col, route_col, route_row, upstream)
-
-
-def back_kernel(
-    layer, last, back, resid_in, inputs, upstream, route_col, gate_col, route_row, latent_i,
-    queries_i, probs_i, mixed_i, wd0, wq0, wu0, wd1, wq1, wu1, *rest,
-):
-    if last:
-        grad, normed_o, d_latent_o, d_queries_o, d_resid_o, tokens, wd, wq, wu, sems = rest
-    else:
-        grad, normed_o, d_latent_o, d_queries_o, d_resid_o, blocks, tokens, packed, wd, wq, wu, sems = rest
-    wait = fetch(layer, ((wd0, wd1, wd), (wq0, wq1, wq), (wu0, wu1, wu)), sems)
-    unpack_tokens(back, route_col[...], tokens)
-    normed2, inv2 = rms_norm(resid_in[...].astype(f32))
-    d_resid = upstream[...].astype(f32) + rms_back(normed2, inv2, tokens[...])
+    normed2, inv2 = rms_norm(resid.astype(f32))
+    d_resid = upstream.astype(f32) + rms_back(normed2, inv2, tokens[...])
     d_resid_b = d_resid.astype(bf16)
     d_resid_o[...] = d_resid_b
     tokens[...] = d_resid
-    latent, probs = latent_i[...], probs_i[...]
+    wd, wq, wu = w
     wait(2)
     d_mixed = times_t(d_resid_b, wu[...]).astype(bf16)
     d_probs = times_t(d_mixed, latent)
@@ -450,153 +363,325 @@
     wait(1)
     d_latent = (
         t_times(probs.astype(bf16), d_mixed)
-        + t_times(d_scores, queries_i[...])
+        + t_times(d_scores, queries)
         + times_t(d_queries, wq[...])
     ).astype(bf16)
     wait(0)
     d_normed = times_t(d_latent, wd[...])
-    normed, inv = rms_norm(inputs[...].astype(f32))
+    normed, inv = rms_norm(inputs.astype(f32))
     normed_o[...] = normed.astype(bf16)
     d_latent_o[...] = d_latent
     d_queries_o[...] = d_queries
-    d_input = (tokens[...] + rms_back(normed, inv, d_normed)).astype(bf16)
-    grad[...] = d_input
-    if not last:
-        scaled = (gate_col[...] * d_input.astype(f32)).astype(bf16)
-        pack_tokens(scaled, route_row[...], packed, blocks)
-
-
-def backward(layer, back, residual, inputs, upstream, route_col, gate_col, route_row, kept, attn):
-    last = layer == 0
-    outs = [
-        jax.ShapeDtypeStruct((SEQ, WIDTH), bf16),
-        jax.ShapeDtypeStruct((SEQ, WIDTH), bf16),
-        jax.ShapeDtypeStruct((SEQ, LAT), bf16),
-        jax.ShapeDtypeStruct((SEQ, LAT), bf16),
-        jax.ShapeDtypeStruct((SEQ, WIDTH), bf16),
-    ] + ([] if last else [ATTN_OUT[0]])
-    return pl.pallas_call(
-        functools.partial(back_kernel, layer, last),
-        name=f"backward{layer}",
-        out_shape=outs,
-        in_specs=[VMEM] * 11 + [ANY] * 6,
+    grad[...] = (tokens[...] + rms_back(normed, inv, d_normed)).astype(bf16)
+
+
+def unpack_rows(rows, wide, g):
+    packed = dot(
+        gather_matrix(), rows[pl.ds(g * EXPERTS, EXPERTS)].reshape(EXPERTS * 8, BLOCK[1])
+    ).astype(bf16)
+    for s in range(CAP):
+        at = pl.multiple_of(g * EXPERTS + s * DP * EXPERTS, EXPERTS)
+        for r in range(PIECES):
+            wide[pl.ds(at, EXPERTS), r * PIECE : (r + 1) * PIECE] = packed[
+                r * EXPERTS : (r + 1) * EXPERTS, s * PIECE : (s + 1) * PIECE
+            ]
+
+
+def pack_rows(wide, packed, out, g):
+    for s in range(CAP):
+        at = pl.multiple_of(g * EXPERTS + s * DP * EXPERTS, EXPERTS)
+        for r in range(PIECES):
+            packed[r * EXPERTS : (r + 1) * EXPERTS, s * PIECE : (s + 1) * PIECE] = wide[
+                pl.ds(at, EXPERTS), r * PIECE : (r + 1) * PIECE
+            ]
+    out[pl.ds(g * EXPERTS, EXPERTS)] = (
+        dot(spread_matrix(), packed[...]).astype(bf16).reshape(EXPERTS, *BLOCK)
+    )
+
+
+def send_back(combine, wide, packed):
+    pack_rows(wide, packed, combine.part, combine.opp)
+    combine.start_far()
+    pack_rows(wide, packed, combine.part, combine.left)
+    pack_rows(wide, packed, combine.part, combine.right)
+    combine.start_near()
+    pack_rows(wide, packed, combine.part, combine.d)
+
+
+def expert_out(hidden, dw, wide):
+    for c in range(PIECES):
+        cols = slice(c * PIECE, (c + 1) * PIECE)
+        wide[:, cols] = dot(hidden, dw[:, cols]).astype(bf16)
+
+
+def expert_back(wide, gate_pre, up_pre, gw, uw, dw):
+    d_hidden = times_t(wide[...], dw[...])
+    activated, slope = silu_parts(gate_pre)
+    d_gate = (d_hidden * up_pre * slope).astype(bf16)
+    d_up = (d_hidden * activated).astype(bf16)
+    for c in range(PIECES):
+        cols = slice(c * PIECE, (c + 1) * PIECE)
+        wide[:, cols] = (times_t(d_gate, gw[cols, :]) + times_t(d_up, uw[cols, :])).astype(bf16)
+
+
+class Refs:
+    def __init__(self, names, refs):
+        for name, ref in zip(names, refs, strict=True):
+            setattr(self, name, ref)
+
+    def some(self, prefix, count):
+        return tuple(getattr(self, f"{prefix}{k}") for k in range(count))
+
+
+def named(prefix, items):
+    return {f"{prefix}{k}": item for k, item in enumerate(items)}
+
+
+def fused(run, name, ins, outs, scratch, number):
+    names = [*ins, *outs, *scratch]
+
+    def kernel(*refs):
+        run(Refs(names, refs))
+
+    results = pl.pallas_call(
+        kernel,
+        name=name,
+        out_shape=list(outs.values()),
+        in_specs=[spec for _, spec in ins.values()],
         out_specs=[VMEM] * len(outs),
-        scratch_shapes=TOKEN_SCRATCH + ([] if last else PACK_SCRATCH) + ATTN_SCRATCH,
-    )(back, residual, inputs, upstream, route_col, gate_col, route_row, *kept, *attn)
-
-
-def unpack_rows(rows, wide):
-    gather = gather_matrix()
-
-    @pl.loop(0, DP)
-    def _(g):
-        start = pl.multiple_of(g * EXPERTS * 8, EXPERTS * 8)
-        packed = dot(gather, rows[pl.ds(start, EXPERTS * 8), :]).astype(bf16)
-        for s in range(CAP):
-            at = pl.multiple_of(g * EXPERTS + s * DP * EXPERTS, EXPERTS)
-            for r in range(PIECES):
-                wide[pl.ds(at, EXPERTS), r * PIECE : (r + 1) * PIECE] = packed[
-                    r * EXPERTS : (r + 1) * EXPERTS, s * PIECE : (s + 1) * PIECE
-                ]
-
-
-def pack_rows(wide, packed, out):
-    spread = spread_matrix()
-
-    @pl.loop(0, DP)
-    def _(g):
-        for s in range(CAP):
-            at = pl.multiple_of(g * EXPERTS + s * DP * EXPERTS, EXPERTS)
-            for r in range(PIECES):
-                packed[r * EXPERTS : (r + 1) * EXPERTS, s * PIECE : (s + 1) * PIECE] = wide[
-                    pl.ds(at, EXPERTS), r * PIECE : (r + 1) * PIECE
-                ]
-        start = pl.multiple_of(g * EXPERTS * 8, EXPERTS * 8)
-        out[pl.ds(start, EXPERTS * 8), :] = dot(spread, packed[...]).astype(bf16)
-
-
-def expert_forward_kernel(
-    layer, rows, gw0, uw0, dw0, gw1, uw1, dw1, part, gate_o, up_o, wide, packed, gw, uw, dw, sems
-):
-    wait = fetch(layer, ((gw0, gw1, gw), (uw0, uw1, uw), (dw0, dw1, dw)), sems)
-    unpack_rows(rows, wide)
-    wait(0)
-    gate_o[...] = dot(wide[...], gw[...])
-    wait(1)
-    up_o[...] = dot(wide[...], uw[...])
-    hidden = (silu_parts(gate_o[...])[0] * up_o[...]).astype(bf16)
-    wait(2)
-    for c in range(PIECES):
-        wide[:, c * PIECE : (c + 1) * PIECE] = dot(
-            hidden, dw[:, c * PIECE : (c + 1) * PIECE]
-        ).astype(bf16)
-    pack_rows(wide, packed, part)
-
-
-def expert_backward_kernel(
-    layer, rows, gate_i, up_i, gw0, uw0, dw0, gw1, uw1, dw1, part, wide, packed, gw, uw, dw, sems
-):
-    wait = fetch(layer, ((gw0, gw1, gw), (uw0, uw1, uw), (dw0, dw1, dw)), sems)
-    unpack_rows(rows, wide)
-    wait(2)
-    d_hidden = times_t(wide[...], dw[...])
-    activated, slope = silu_parts(gate_i[...])
-    d_gate = (d_hidden * up_i[...] * slope).astype(bf16)
-    d_up = (d_hidden * activated).astype(bf16)
-    wait(0)
-    wait(1)
-    for c in range(PIECES):
-        wide[:, c * PIECE : (c + 1) * PIECE] = (
-            times_t(d_gate, gw[c * PIECE : (c + 1) * PIECE, :])
-            + times_t(d_up, uw[c * PIECE : (c + 1) * PIECE, :])
-        ).astype(bf16)
-    pack_rows(wide, packed, part)
-
-
-EXPERT_SCRATCH = [
-    pltpu.VMEM((CAP * DP * EXPERTS, WIDTH), bf16),
-    pltpu.VMEM((PACKED, BLOCK[1]), bf16),
-    pltpu.VMEM((WIDTH, FF), bf16),
-    pltpu.VMEM((WIDTH, FF), bf16),
-    pltpu.VMEM((FF, WIDTH), bf16),
-    pltpu.SemaphoreType.DMA((3,)),
-]
-PARTS = jax.ShapeDtypeStruct((DP * EXPERTS * 8, BLOCK[1]), bf16)
-PRE = jax.ShapeDtypeStruct((CAP * DP * EXPERTS, FF), f32)
-
-
-def expert_forward(layer, rows, experts):
-    return pl.pallas_call(
-        functools.partial(expert_forward_kernel, layer),
-        name=f"expert_forward{layer}",
-        out_shape=[PARTS, PRE, PRE],
-        in_specs=[VMEM] + [ANY] * 6,
-        out_specs=[VMEM] * 3,
-        scratch_shapes=EXPERT_SCRATCH,
-    )(rows, *experts)
-
-
-def expert_backward(layer, rows, gate_pre, up_pre, experts):
-    return pl.pallas_call(
-        functools.partial(expert_backward_kernel, layer),
-        name=f"expert_backward{layer}",
-        out_shape=PARTS,
-        in_specs=[VMEM] * 3 + [ANY] * 6,
-        out_specs=VMEM,
-        scratch_shapes=EXPERT_SCRATCH,
-    )(rows, gate_pre, up_pre, *experts)
-
-
-def flat(blocks):
-    return blocks.reshape(-1, BLOCK[1])
-
-
-def blocked(rows):
-    return rows.reshape(-1, *BLOCK)
-
-
-def swap(value):
-    return lax.ppermute(value, "section", [(0, 1), (1, 0)])
+        scratch_shapes=list(scratch.values()),
+        compiler_params=pltpu.CompilerParams(
+            collective_id=number, has_side_effects=True, vmem_limit_bytes=60 * 1024 * 1024
+        ),
+    )(*[array for array, _ in ins.values()])
+    return dict(zip(outs, results))
+
+
+def shaped(*shape, dtype=bf16):
+    return jax.ShapeDtypeStruct(shape, dtype)
+
+
+TOKENS = (SEQ, WIDTH)
+ROWS = (DP * EXPERTS, *BLOCK)
+HOME = (EXPERTS, *BLOCK)
+PRE = (CAP * DP * EXPERTS, FF)
+COMMON = {
+    "tokens": pltpu.VMEM(TOKENS, f32),
+    "wide": pltpu.VMEM((CAP * DP * EXPERTS, WIDTH), bf16),
+    "packed": pltpu.VMEM((PACKED, BLOCK[1]), bf16),
+    "w0": pltpu.VMEM((WIDTH, LAT), bf16),
+    "w1": pltpu.VMEM((LAT, LAT), bf16),
+    "w2": pltpu.VMEM((LAT, WIDTH), bf16),
+    "wsem": pltpu.SemaphoreType.DMA((3,)),
+    "v0": pltpu.VMEM((WIDTH, FF), bf16),
+    "v1": pltpu.VMEM((WIDTH, FF), bf16),
+    "v2": pltpu.VMEM((FF, WIDTH), bf16),
+    "vsem": pltpu.SemaphoreType.DMA((3,)),
+}
+
+
+def fetch_attn(refs, layer):
+    attn = refs.some("attn", 6)
+    return fetch(layer, [(attn[k], attn[3 + k], getattr(refs, f"w{k}")) for k in range(3)], refs.wsem)
+
+
+def fetch_expert(refs, layer):
+    expert = refs.some("expert", 6)
+    return fetch(
+        layer, [(expert[k], expert[3 + k], getattr(refs, f"v{k}")) for k in range(3)], refs.vsem
+    )
+
+
+def dispatch_of(refs, tag):
+    return Dispatch(
+        getattr(refs, "blk" + tag), getattr(refs, "rows" + tag), refs.some("ds" + tag + "_", 6)
+    )
+
+
+def dispatch_scratch(tag):
+    return {
+        "blk" + tag: pltpu.VMEM(HOME, bf16),
+        "rows" + tag: pltpu.VMEM(ROWS, bf16),
+        **named("ds" + tag + "_", Dispatch.sems),
+    }
+
+
+def combine_of(refs, tag):
+    return Combine(
+        getattr(refs, "part" + tag),
+        getattr(refs, "home" + tag),
+        refs.some("cb" + tag + "_", 5),
+        refs.some("cs" + tag + "_", 6),
+    )
+
+
+def combine_scratch(tag, skip=()):
+    whole = {
+        "part" + tag: pltpu.VMEM(ROWS, bf16),
+        "home" + tag: pltpu.VMEM(HOME, bf16),
+        **named("cb" + tag + "_", Combine.buffers),
+        **named("cs" + tag + "_", Combine.sems),
+    }
+    return {k: v for k, v in whole.items() if k not in skip}
+
+
+def kept_shapes(layer):
+    return {
+        f"resid{layer}": shaped(*TOKENS),
+        f"latent{layer}": shaped(SEQ, LAT),
+        f"queries{layer}": shaped(SEQ, LAT),
+        f"probs{layer}": shaped(SEQ, SEQ, dtype=f32),
+        f"mixed{layer}": shaped(SEQ, LAT),
+    }
+
+
+def kept_refs(refs, layer):
+    return [getattr(refs, f"{k}{layer}") for k in ("resid", "latent", "queries", "probs", "mixed")]
+
+
+def forward_run(refs):
+    e, _, _, _, right, left, _ = places()
+    greet(e, right, left)
+    wait_w = fetch_attn(refs, 0)
+    wait_v = fetch_expert(refs, 0)
+    first, early, second = (dispatch_of(refs, tag) for tag in ("a", "b", "c"))
+    out0, back1 = combine_of(refs, "a"), combine_of(refs, "b")
+    w = refs.some("w", 3)
+
+    attend(
+        refs.x[...], refs.route_row0[...], *w, wait_w, refs.packed, refs.blka, *kept_refs(refs, 0)
+    )
+    wait_w = fetch_attn(refs, 1)
+    greeted()
+    first.start()
+    scaled = (refs.gate_col1[...] * refs.dy[...].astype(f32)).astype(bf16)
+    pack_tokens(scaled, refs.route_row1[...], refs.packed, refs.blkb)
+    for i in range(NZ):
+        first.forward(i)
+        if i >= 2:
+            first.relay(i - 2)
+        if i == 5:
+            early.start()
+    first.relay(6)
+    first.relay(7)
+    first.rest(lambda g: unpack_rows(refs.rowsa, refs.wide, g))
+
+    wait_v(0)
+    refs.gate0[...] = dot(refs.wide[...], refs.v0[...])
+    wait_v(1)
+    refs.up0[...] = dot(refs.wide[...], refs.v1[...])
+    hidden = (silu_parts(refs.gate0[...])[0] * refs.up0[...]).astype(bf16)
+    wait_v(2)
+    expert_out(hidden, refs.v2, refs.wide)
+    wait_v = fetch_expert(refs, 1)
+    send_back(out0, refs.wide, refs.packed)
+    for i in range(NZ):
+        out0.relay(i)
+    for i in range(NZ):
+        early.forward(i)
+    for i in range(NZ):
+        out0.finish(i)
+    out0.arrive()
+
+    unpack_tokens(refs.homea, refs.route_col0[...], refs.tokens)
+    act0 = (refs.resid0[...].astype(f32) + refs.gate_col0[...] * refs.tokens[...]).astype(bf16)
+    refs.act0[...] = act0
+    attend(act0, refs.route_row1[...], *w, wait_w, refs.packed, refs.blkc, *kept_refs(refs, 1))
+    second.start()
+    for i in range(NZ):
+        early.relay(i)
+    for i in range(NZ):
+        second.forward(i)
+        if i >= 2:
+            second.relay(i - 2)
+    second.relay(6)
+    second.relay(7)
+    second.rest(lambda g: unpack_rows(refs.rowsc, refs.wide, g))
+
+    wait_v(0)
+    refs.gate1[...] = dot(refs.wide[...], refs.v0[...])
+    wait_v(1)
+    refs.up1[...] = dot(refs.wide[...], refs.v1[...])
+    early.rest(lambda g: unpack_rows(refs.rowsb, refs.wide, g))
+    wait_v(2)
+    expert_back(refs.wide, refs.gate1[...], refs.up1[...], refs.v0, refs.v1, refs.v2)
+    send_back(back1, refs.wide, refs.packed)
+    hidden = (silu_parts(refs.gate1[...])[0] * refs.up1[...]).astype(bf16)
+    expert_out(hidden, refs.v2, refs.wide)
+    for i in range(NZ):
+        back1.relay(i)
+    for g in range(DP):
+        pack_rows(refs.wide, refs.packed, refs.part1, g)
+    for i in range(NZ):
+        back1.finish(i)
+    back1.arrive()
+    for each in (first, early, second, out0, back1):
+        each.drain()
+
+
+def backward_run(refs):
+    e, _, _, _, right, left, _ = places()
+    greet(e, right, left)
+    wait_w = fetch_attn(refs, 1)
+    wait_v = fetch_expert(refs, 0)
+    again = dispatch_of(refs, "a")
+    out1, back0 = combine_of(refs, "a"), combine_of(refs, "b")
+    w = refs.some("w", 3)
+
+    unpack_tokens(refs.back1, refs.route_col1[...], refs.tokens)
+    greeted()
+    out1.start_far()
+    out1.start_near()
+    attend_back(
+        refs.dy[...], refs.act0[...], *[ref[...] for ref in kept_refs(refs, 1)], w, wait_w,
+        refs.tokens, refs.n1, refs.dl1, refs.dq1, refs.dr1, refs.grad1,
+    )
+    wait_w = fetch_attn(refs, 0)
+    scaled = (refs.gate_col0[...] * refs.grad1[...].astype(f32)).astype(bf16)
+    pack_tokens(scaled, refs.route_row0[...], refs.packed, refs.blka)
+    again.start()
+    for i in range(NZ):
+        out1.relay(i)
+    for i in range(NZ):
+        again.forward(i)
+        if i >= 2:
+            again.relay(i - 2)
+    again.relay(6)
+    again.relay(7)
+    for i in range(NZ):
+        out1.finish(i)
+    again.rest(lambda g: unpack_rows(refs.rowsa, refs.wide, g))
+    for k in range(3):
+        wait_v(k)
+    expert_back(refs.wide, refs.gate0[...], refs.up0[...], refs.v0, refs.v1, refs.v2)
+    send_back(back0, refs.wide, refs.packed)
+    for i in range(NZ):
+        back0.relay(i)
+    out1.arrive()
+    unpack_tokens(refs.homea, refs.route_col1[...], refs.tokens)
+    refs.act1[...] = (
+        refs.resid1[...].astype(f32) + refs.gate_col1[...] * refs.tokens[...]
+    ).astype(bf16)
+    for i in range(NZ):
+        back0.finish(i)
+    back0.arrive()
+    unpack_tokens(refs.homeb, refs.route_col0[...], refs.tokens)
+    attend_back(
+        refs.grad1[...], refs.x[...], *[ref[...] for ref in kept_refs(refs, 0)], w, wait_w,
+        refs.tokens, refs.n0, refs.dl0, refs.dq0, refs.dr0, refs.grad0,
+    )
+    for each in (again, out1, back0):
+        each.drain()
+
+
+def factor_shapes(layer):
+    return {
+        f"n{layer}": shaped(*TOKENS),
+        f"dl{layer}": shaped(SEQ, LAT),
+        f"dq{layer}": shaped(SEQ, LAT),
+        f"dr{layer}": shaped(*TOKENS),
+        f"grad{layer}": shaped(*TOKENS),
+    }
 
 
 ROUND = 1792
@@ -866,6 +951,10 @@
     )(*layer0, *layer1)
 
 
+def swap(value):
+    return lax.ppermute(value, "section", [(0, 1), (1, 0)])
+
+
 def body(x_in, dy_out, routes, gates, w_down, w_qk, w_up, e_gate, e_up, e_down):
     section = lax.axis_index("section")
     attn_own = (w_down[0], w_qk[0], w_up[0])
@@ -884,32 +973,64 @@
     gate_cols = both_layers(gates[0, :, 0])
     route_rows = tuple(r.reshape(1, SEQ) for r in route_cols)
 
-    blocks, resid0, *kept0 = first(x, route_rows[0], attn)
-    rows = flat(dispatch(blocked(blocks)))
-    parts, gate0, up0 = expert_forward(0, rows, experts)
-    back = flat(combine(blocked(parts)))
-    act0, blocks, resid1, *kept1 = second(
-        back, resid0, gate_cols[0], route_cols[0], route_rows[1], attn
-    )
-    rows = flat(dispatch(blocked(blocks)))
-    parts, gate1, up1 = expert_forward(1, rows, experts)
-    back = flat(combine(blocked(parts)))
-    act1, blocks = third(back, resid1, gate_cols[1], route_cols[1], route_rows[1], dy)
-    rows = flat(dispatch(blocked(blocks)))
-    parts = expert_backward(1, rows, gate1, up1, experts)
-    back = flat(combine(blocked(parts)))
-    grad1, n1, dl1, dq1, dr1, blocks = backward(
-        1, back, resid1, act0, dy, route_cols[1], gate_cols[0], route_rows[0], kept1, attn
-    )
-    rows = flat(dispatch(blocked(blocks)))
-    parts = expert_backward(0, rows, gate0, up0, experts)
-    back = flat(combine(blocked(parts)))
-    grad0, n0, dl0, dq0, dr0 = backward(
-        0, back, resid0, x, grad1, route_cols[0], gate_cols[0], route_rows[0], kept0, attn
-    )
-    layer0 = (n0, dl0, kept0[0], dq0, dr0, kept0[3], act0, grad0)
-    layer1 = (n1, dl1, kept1[0], dq1, dr1, kept1[3], act1, grad1)
-    activations, grads_in, g_down, g_qk, g_up_t = weight_grads(layer0, layer1)
+    whole = {
+        "x": (x, VMEM),
+        "dy": (dy, VMEM),
+        **{f"route_row{k}": (route_rows[k], VMEM) for k in range(2)},
+        **{f"route_col{k}": (route_cols[k], VMEM) for k in range(2)},
+        **{f"gate_col{k}": (gate_cols[k], VMEM) for k in range(2)},
+        **named("attn", [(w, ANY) for w in attn]),
+        **named("expert", [(w, ANY) for w in experts]),
+    }
+    kept = fused(
+        forward_run,
+        "forward",
+        whole,
+        {
+            "act0": shaped(*TOKENS),
+            **kept_shapes(0),
+            **kept_shapes(1),
+            "gate0": shaped(*PRE, dtype=f32),
+            "up0": shaped(*PRE, dtype=f32),
+            "part1": shaped(*ROWS),
+            "homeb": shaped(*HOME),
+        },
+        {
+            **COMMON,
+            "gate1": pltpu.VMEM(PRE, f32),
+            "up1": pltpu.VMEM(PRE, f32),
+            **dispatch_scratch("a"),
+            **dispatch_scratch("b"),
+            **dispatch_scratch("c"),
+            **combine_scratch("a"),
+            **combine_scratch("b", skip=("homeb",)),
+        },
+        0,
+    )
+    part1, back1 = kept.pop("part1"), kept.pop("homeb")
+    done = fused(
+        backward_run,
+        "backward",
+        {
+            **whole,
+            **{k: (v, VMEM) for k, v in kept.items()},
+            "parta": (part1, VMEM),
+            "back1": (back1, VMEM),
+        },
+        {"act1": shaped(*TOKENS), **factor_shapes(1), **factor_shapes(0)},
+        {
+            **COMMON,
+            **dispatch_scratch("a"),
+            **combine_scratch("a", skip=("parta",)),
+            **combine_scratch("b"),
+        },
+        1,
+    )
+    layers = [
+        tuple({**kept, **done}[f"{k}{layer}"] for k in ("n", "dl", "latent", "dq", "dr", "mixed", "act", "grad"))
+        for layer in range(2)
+    ]
+    activations, grads_in, g_down, g_qk, g_up_t = weight_grads(*layers)
     return (
         activations[None, :, None],
         grads_in[None, :, None],

time: 457 us -> 366 us (0.80)
  the two profiles are of different devices: /device:TPU:1 before, /device:TPU:0 now
where the time goes in v3:
time: 366 us; the launch traced here: 360 us
  Pallas kernels  335 us (92%)
  local copies, waits for them, and re-layouts  10.4 us (3%)
  waiting for transfers between devices  8.73 us (2%)
    pallas_call x2, Pallas kernels, fused(): pl.pallas_call(kernel, name=name, out_shape=list(outs.values()), in_specs...  287 us
    pallas_call x1, Pallas kernels, weight_grads(): pl.pallas_call(grads_kernel, name='weight_grads', out_shape=[jax.ShapeDty...  48.6 us
    ppermute x8, waiting for transfers between devices, swap(): return lax.ppermute(value, 'section', [(0, 1), (1, 0)])  8.73 us
  transfers between devices with their start and end apart: 8, of which 5 were waited for; matrix products, arithmetic and copies ran while one was open for 2% of the time, Pallas kernels for 0%

profile of v3, /device:TPU:0, one launch (start us, length us, event | category | flops | bytes accessed | tf_op | source)
XLA Modules:
  0.0 359.6 jit_solution(3468520894910177039)
XLA Ops:
  0.6 0.1 collective-permute-start.3
  0.7 0.7 fusion.1
  1.4 0.1 copy.25
  1.5 0.5 collective-permute-start
  2.0 0.7 fusion.3
  2.7 0.1 copy.28
  2.8 0.1 collective-permute-start.1
  2.9 0.5 collective-permute-start.2
  3.4 0.1 collective-permute-start.4
  3.5 0.0 collective-permute-done
  3.5 0.4 collective-permute-start.5
  3.9 0.2 collective-permute-done.1
  4.1 0.2 collective-permute-start.6
  4.2 0.0 collective-permute-done.3.refs_12_
  4.2 0.0 copy-start.2
  4.2 0.6 collective-permute-start.7
  4.9 0.1 copy.29
  4.9 0.1 copy.26
  5.0 2.1 dynamic-slice_bitcast_fusion
  7.2 1.3 fusion.4
  8.4 0.6 broadcast_select_fusion
  9.1 0.0 collective-permute-done.2.refs_11_
  9.1 0.0 copy-start
  9.1 0.7 collective-permute-done.4.refs_13_
  9.7 2.6 collective-permute-done.5.refs_17_
  12.4 2.6 collective-permute-done.6.refs_18_
  15.0 2.6 collective-permute-done.7.refs_19_
  17.6 0.0 copy-done.2
  17.6 0.0 copy-done
  17.6 179.2 %forward.1 = (bf16[64,3584]{1,0:T(8,128)(2,1)}, bf16[64,3584]{1,0:T(8,128)(2,1)}, bf16[64,256]{1,0:T(8,128)(2,1)}, bf16[64,256]{1,0:T(8,128)(2,1)}, f32[64,64]{1...) custom-call(bf16[64,3584]{1,0:T(8,128)(2,1)} %get-tuple-element.90.r, ...), custom_call_target="tpu_custom_call" | custom-call | tf_op jit(solution)/shard_map/forward/pallas_call | solution.py:446
  196.9 107.3 %backward.1 = (bf16[64,3584]{1,0:T(8,128)(2,1)}, bf16[64,3584]{1,0:T(8,128)(2,1)}, bf16[64,256]{1,0:T(8,128)(2,1)}, bf16[64,256]{1,0:T(8,128)(2,1)}, bf16[64,358...) custom-call(bf16[64,3584]{1,0:T(8,128)(2,1)} %get-tuple-element.90.r, ...), custom_call_target="tpu_custom_call" | custom-call | tf_op jit(solution)/shard_map/backward/pallas_call | solution.py:446
  304.2 48.6 %weight_grads.1 = (bf16[2,64,3584]{2,1,0:T(8,128)(2,1)}, bf16[2,64,3584]{2,1,0:T(8,128)(2,1)}, f32[28,256]{1,0:T(8,128)}, f32[2,256]{1,0:T(2,128)}, f32[28,256]{1,0:T(8,128)}) custom-call(bf16[64,3584]{1,0:T(8,128)(2,1)} %get-tuple-element.51.n0, bf16[64,256]{1,0:T(8,128)(2,1)} %get-tuple-element.52.dl0, bf16[64,256]{1,0:T(8,128)(2,1)} %get-tuple-element.38.refs_22_.la0, ...), custom_call_target="tpu_custom_call" | custom-call | tf_op jit(solution)/shard_map/weight_grads/pallas_call | solution.py:920
  352.8 0.0 copy-start.1
  352.8 1.5 copy.33
  354.3 1.4 copy.34
  355.7 0.0 copy-start.3
  355.7 2.2 copy.38
  357.9 0.0 copy-done.1
  357.9 0.9 copy.39
  358.8 0.0 copy-done.3
  358.8 0.6 copy.40
Async XLA Ops:
  0.6 3.6 %collective-permute-start.3 = (bf16[256,256]{1,0:T(8,128)(2,1)}, bf16[256,256]{1,0:T(8,128)(2,1)S(1)}, u32[]{:S(2)}, u32[]{:S(2)}) collective-permute-start(bf16[256,256]{1,0:T(8,128)(2,1)} %bitcast.46), channel_id=1, source_target_pairs={{0,128},{128,0},{1,129},{129,1},{2,130},{130,2},{3,131},{131,3},{4... | collective-permute-start | bytes 393224 | tf_op jit(solution)/shard_map/ppermute | solution.py:955
  1.5 2.0 collective-permute-start
  2.8 1.2 collective-permute-start.1
  2.9 6.2 %collective-permute-start.2 = (bf16[3584,256]{1,0:T(8,128)(2,1)}, bf16[3584,256]{1,0:T(8,128)(2,1)S(1)}, u32[]{:S(2)}, u32[]{:S(2)}) collective-permute-start(bf16[3584,256]{1,0:T(8,128)(2,1)} %bitcast.29), channel_id=1, source_target_pairs={{0,128},{128,0},{1,129},{129,1},{2,130},{130,2},{3,131},{131,3},{4... | collective-permute-start | bytes 5505032 | tf_op jit(solution)/shard_map/ppermute | solution.py:955
  3.4 6.4 %collective-permute-start.4 = (bf16[256,3584]{1,0:T(8,128)(2,1)}, bf16[256,3584]{1,0:T(8,128)(2,1)}, u32[]{:S(2)}, u32[]{:S(2)}) collective-permute-start(bf16[256,3584]{1,0:T(8,128)(2,1)} %bitcast.32), channel_id=1, source_target_pairs={{0,128},{128,0},{1,129},{129,1},{2,130},{130,2},{3,131},{131,3},{4... | collective-permute-start | bytes 5505032 | tf_op jit(solution)/shard_map/ppermute | solution.py:955
  3.5 8.9 %collective-permute-start.5 = (bf16[3584,256]{1,0:T(8,128)(2,1)}, bf16[3584,256]{1,0:T(8,128)(2,1)}, u32[]{:S(2)}, u32[]{:S(2)}) collective-permute-start(bf16[3584,256]{1,0:T(8,128)(2,1)} %bitcast.35), channel_id=1, source_target_pairs={{0,128},{128,0},{1,129},{129,1},{2,130},{130,2},{3,131},{131,3},{4... | collective-permute-start | bytes 5505032 | tf_op jit(solution)/shard_map/ppermute | solution.py:955
  4.1 10.9 %collective-permute-start.6 = (bf16[3584,256]{1,0:T(8,128)(2,1)}, bf16[3584,256]{1,0:T(8,128)(2,1)}, u32[]{:S(2)}, u32[]{:S(2)}) collective-permute-start(bf16[3584,256]{1,0:T(8,128)(2,1)} %bitcast.38), channel_id=1, source_target_pairs={{0,128},{128,0},{1,129},{129,1},{2,130},{130,2},{3,131},{131,3},{4... | collective-permute-start | bytes 5505032 | tf_op jit(solution)/shard_map/ppermute | solution.py:955
  4.2 13.4 %copy-start.2 = (bf16[256,256]{1,0:T(8,128)(2,1)}, bf16[256,256]{1,0:T(8,128)(2,1)S(1)}, u32[]{:S(2)}) copy-start(bf16[256,256]{1,0:T(8,128)(2,1)S(1)} %collective-permute-done.3.refs_12_) | copy-start | bytes 393220
  4.2 13.4 %collective-permute-start.7 = (bf16[256,3584]{1,0:T(8,128)(2,1)}, bf16[256,3584]{1,0:T(8,128)(2,1)}, u32[]{:S(2)}, u32[]{:S(2)}) collective-permute-start(bf16[256,3584]{1,0:T(8,128)(2,1)} %bitcast.41), channel_id=1, source_target_pairs={{0,128},{128,0},{1,129},{129,1},{2,130},{130,2},{3,131},{131,3},{4... | collective-permute-start | bytes 5505032 | tf_op jit(solution)/shard_map/ppermute | solution.py:955
  9.1 8.6 %copy-start = (bf16[3584,256]{1,0:T(8,128)(2,1)}, bf16[3584,256]{1,0:T(8,128)(2,1)S(1)}, u32[]{:S(2)}) copy-start(bf16[3584,256]{1,0:T(8,128)(2,1)S(1)} %collective-permute-done.2.refs_11_) | copy-start | bytes 5505028
  352.8 5.0 %copy-start.1 = (bf16[2,64,3584]{2,1,0:T(8,128)(2,1)S(1)}, bf16[2,64,3584]{2,1,0:T(8,128)(2,1)}, u32[]{:S(2)}) copy-start(bf16[2,64,3584]{2,1,0:T(8,128)(2,1)} %get-tuple-element.63) | copy-start | bytes 2752516
  355.7 3.1 copy-start.3

commit v4 on v3

--- a/solution.py
+++ b/solution.py
@@ -129,10 +129,12 @@
         )
     for side in (right, left):
         pl.semaphore_signal(barrier, inc=1, device_id={"dp": side}, device_id_type=MESH)
+    partner = {"section": 1 - lax.axis_index("section")}
+    pl.semaphore_signal(barrier, inc=1, device_id=partner, device_id_type=MESH)
 
 
 def greeted():
-    pl.semaphore_wait(pltpu.get_barrier_semaphore(), EXPERTS + 1)
+    pl.semaphore_wait(pltpu.get_barrier_semaphore(), EXPERTS + 2)
 
 
 def remote(src, dst, send, recv, where):
@@ -190,19 +192,28 @@
         self.arrived(ref, sem.at[j])
         remote(ref, ref, self.sx, self.ro.at[j], {"dp": to}).start()
 
-    def rest(self, use):
-        use(self.d)
+    def wait_right(self):
         for i, j in enumerate(ORDER):
             if i % 2 == 0:
                 self.arrived(self.group(self.right, j), self.rr.at[j])
-        use(self.right)
+
+    def wait_left(self):
         for i, j in enumerate(ORDER):
             if i % 2 == 1:
                 self.arrived(self.group(self.left, j), self.rl.at[j])
-        use(self.left)
+
+    def wait_far(self):
         for j in ORDER:
             self.arrived(self.group(self.opp, j), self.ro.at[j])
-        use(self.opp)
+
+    def chunks(self, use, near):
+        @pl.loop(0, DP)
+        def _(k):
+            pl.when(k == 1)(self.wait_right)
+            pl.when(k == 2)(self.wait_left)
+            pl.when(k == 3)(self.wait_far)
+            use((self.d + k + k // 2 - 2 * (k // 3)) % DP)
+            pl.when(k == 2)(near)
 
     def drain(self):
         sent = self.blk.at[pl.ds(0, EXPERTS - 1)]
@@ -375,53 +386,47 @@
     grad[...] = (tokens[...] + rms_back(normed, inv, d_normed)).astype(bf16)
 
 
+CHUNK = CAP * EXPERTS
+
+
 def unpack_rows(rows, wide, g):
     packed = dot(
         gather_matrix(), rows[pl.ds(g * EXPERTS, EXPERTS)].reshape(EXPERTS * 8, BLOCK[1])
     ).astype(bf16)
     for s in range(CAP):
-        at = pl.multiple_of(g * EXPERTS + s * DP * EXPERTS, EXPERTS)
         for r in range(PIECES):
-            wide[pl.ds(at, EXPERTS), r * PIECE : (r + 1) * PIECE] = packed[
+            wide[s * EXPERTS : (s + 1) * EXPERTS, r * PIECE : (r + 1) * PIECE] = packed[
                 r * EXPERTS : (r + 1) * EXPERTS, s * PIECE : (s + 1) * PIECE
             ]
-
-
-def pack_rows(wide, packed, out, g):
-    for s in range(CAP):
-        at = pl.multiple_of(g * EXPERTS + s * DP * EXPERTS, EXPERTS)
-        for r in range(PIECES):
-            packed[r * EXPERTS : (r + 1) * EXPERTS, s * PIECE : (s + 1) * PIECE] = wide[
-                pl.ds(at, EXPERTS), r * PIECE : (r + 1) * PIECE
+    return wide[...]
+
+
+def pack_rows(piece, packed, out, g):
+    for r in range(PIECES):
+        rows = piece(slice(r * PIECE, (r + 1) * PIECE)).astype(bf16)
+        for s in range(CAP):
+            packed[r * EXPERTS : (r + 1) * EXPERTS, s * PIECE : (s + 1) * PIECE] = rows[
+                s * EXPERTS : (s + 1) * EXPERTS
             ]
     out[pl.ds(g * EXPERTS, EXPERTS)] = (
         dot(spread_matrix(), packed[...]).astype(bf16).reshape(EXPERTS, *BLOCK)
     )
 
 
-def send_back(combine, wide, packed):
-    pack_rows(wide, packed, combine.part, combine.opp)
-    combine.start_far()
-    pack_rows(wide, packed, combine.part, combine.left)
-    pack_rows(wide, packed, combine.part, combine.right)
-    combine.start_near()
-    pack_rows(wide, packed, combine.part, combine.d)
-
-
-def expert_out(hidden, dw, wide):
-    for c in range(PIECES):
-        cols = slice(c * PIECE, (c + 1) * PIECE)
-        wide[:, cols] = dot(hidden, dw[:, cols]).astype(bf16)
-
-
-def expert_back(wide, gate_pre, up_pre, gw, uw, dw):
-    d_hidden = times_t(wide[...], dw[...])
+def chunk_rows(g):
+    return pl.ds(pl.multiple_of(g * CHUNK, CHUNK), CHUNK)
+
+
+def expert_out(hidden, dw):
+    return lambda cols: dot(hidden, dw[:, cols])
+
+
+def expert_back(rows, gate_pre, up_pre, gw, uw, dw):
+    d_hidden = times_t(rows, dw[...])
     activated, slope = silu_parts(gate_pre)
     d_gate = (d_hidden * up_pre * slope).astype(bf16)
     d_up = (d_hidden * activated).astype(bf16)
-    for c in range(PIECES):
-        cols = slice(c * PIECE, (c + 1) * PIECE)
-        wide[:, cols] = (times_t(d_gate, gw[cols, :]) + times_t(d_up, uw[cols, :])).astype(bf16)
+    return lambda cols: times_t(d_gate, gw[cols, :]) + times_t(d_up, uw[cols, :])
 
 
 class Refs:
@@ -467,17 +472,14 @@
 PRE = (CAP * DP * EXPERTS, FF)
 COMMON = {
     "tokens": pltpu.VMEM(TOKENS, f32),
-    "wide": pltpu.VMEM((CAP * DP * EXPERTS, WIDTH), bf16),
+    "wide": pltpu.VMEM((CHUNK, WIDTH), bf16),
     "packed": pltpu.VMEM((PACKED, BLOCK[1]), bf16),
     "w0": pltpu.VMEM((WIDTH, LAT), bf16),
     "w1": pltpu.VMEM((LAT, LAT), bf16),
     "w2": pltpu.VMEM((LAT, WIDTH), bf16),
     "wsem": pltpu.SemaphoreType.DMA((3,)),
-    "v0": pltpu.VMEM((WIDTH, FF), bf16),
-    "v1": pltpu.VMEM((WIDTH, FF), bf16),
-    "v2": pltpu.VMEM((FF, WIDTH), bf16),
-    "vsem": pltpu.SemaphoreType.DMA((3,)),
 }
+EXPERT_WEIGHTS = ((WIDTH, FF), (WIDTH, FF), (FF, WIDTH))
 
 
 def fetch_attn(refs, layer):
@@ -485,11 +487,63 @@
     return fetch(layer, [(attn[k], attn[3 + k], getattr(refs, f"w{k}")) for k in range(3)], refs.wsem)
 
 
-def fetch_expert(refs, layer):
-    expert = refs.some("expert", 6)
-    return fetch(
-        layer, [(expert[k], expert[3 + k], getattr(refs, f"v{k}")) for k in range(3)], refs.vsem
-    )
+class Experts:
+    @staticmethod
+    def scratch(layers):
+        return {
+            **named("v", [pltpu.VMEM((layers, *shape), bf16) for shape in EXPERT_WEIGHTS]),
+            "vsem": pltpu.SemaphoreType.DMA((layers, 3)),
+            "vsent": pltpu.SemaphoreType.DMA((3,)),
+        }
+
+    def __init__(self, refs, layers):
+        self.s = lax.axis_index("section")
+        self.own = refs.some("expert", 3)
+        self.v = refs.some("v", 3)
+        self.sem, self.sent, self.layers = refs.vsem, refs.vsent, layers
+
+    def each(self, act):
+        def run():
+            for k in range(3):
+                act(k)
+
+        if self.layers == 1:
+            pl.when(self.s == 0)(run)
+        else:
+            run()
+
+    def place(self):
+        return self.s if self.layers == 2 else 0
+
+    def copy(self, k):
+        return pltpu.make_async_copy(
+            self.own[k], self.v[k].at[self.place()], self.sem.at[self.place(), k]
+        )
+
+    def give(self, k):
+        return remote(
+            self.own[k],
+            self.v[k].at[self.place()],
+            self.sent.at[k],
+            self.sem.at[self.place(), k],
+            {"section": 1 - self.s},
+        )
+
+    def start(self):
+        self.each(lambda k: self.copy(k).start())
+
+    def send(self):
+        self.each(lambda k: self.give(k).start())
+
+    def drain(self):
+        self.each(lambda k: self.give(k).wait_send())
+
+    def ready(self, layer):
+        for k in range(3):
+            pltpu.make_async_copy(
+                self.own[k], self.v[k].at[layer], self.sem.at[layer, k]
+            ).wait()
+        return [ref.at[layer] for ref in self.v]
 
 
 def dispatch_of(refs, tag):
@@ -541,20 +595,24 @@
 
 def forward_run(refs):
     e, _, _, _, right, left, _ = places()
+    section = lax.axis_index("section")
     greet(e, right, left)
     wait_w = fetch_attn(refs, 0)
-    wait_v = fetch_expert(refs, 0)
+    experts = Experts(refs, 2)
+    experts.start()
     first, early, second = (dispatch_of(refs, tag) for tag in ("a", "b", "c"))
     out0, back1 = combine_of(refs, "a"), combine_of(refs, "b")
     w = refs.some("w", 3)
 
     attend(
-        refs.x[...], refs.route_row0[...], *w, wait_w, refs.packed, refs.blka, *kept_refs(refs, 0)
+        refs.x[section], refs.route_row0[...], *w, wait_w, refs.packed, refs.blka,
+        *kept_refs(refs, 0),
     )
     wait_w = fetch_attn(refs, 1)
     greeted()
     first.start()
-    scaled = (refs.gate_col1[...] * refs.dy[...].astype(f32)).astype(bf16)
+    experts.send()
+    scaled = (refs.gate_col1[...] * refs.dy[section].astype(f32)).astype(bf16)
     pack_tokens(scaled, refs.route_row1[...], refs.packed, refs.blkb)
     for i in range(NZ):
         first.forward(i)
@@ -564,17 +622,19 @@
             early.start()
     first.relay(6)
     first.relay(7)
-    first.rest(lambda g: unpack_rows(refs.rowsa, refs.wide, g))
-
-    wait_v(0)
-    refs.gate0[...] = dot(refs.wide[...], refs.v0[...])
-    wait_v(1)
-    refs.up0[...] = dot(refs.wide[...], refs.v1[...])
-    hidden = (silu_parts(refs.gate0[...])[0] * refs.up0[...]).astype(bf16)
-    wait_v(2)
-    expert_out(hidden, refs.v2, refs.wide)
-    wait_v = fetch_expert(refs, 1)
-    send_back(out0, refs.wide, refs.packed)
+    gw, uw, dw = experts.ready(0)
+
+    def forward0(g):
+        at = chunk_rows(g)
+        rows = unpack_rows(refs.rowsa, refs.wide, g)
+        gate_pre, up_pre = dot(rows, gw[...]), dot(rows, uw[...])
+        refs.gate0[at, :] = gate_pre
+        refs.up0[at, :] = up_pre
+        hidden = (silu_parts(gate_pre)[0] * up_pre).astype(bf16)
+        pack_rows(expert_out(hidden, dw), refs.packed, out0.part, g)
+
+    first.chunks(forward0, out0.start_near)
+    out0.start_far()
     for i in range(NZ):
         out0.relay(i)
     for i in range(NZ):
@@ -596,34 +656,44 @@
             second.relay(i - 2)
     second.relay(6)
     second.relay(7)
-    second.rest(lambda g: unpack_rows(refs.rowsc, refs.wide, g))
-
-    wait_v(0)
-    refs.gate1[...] = dot(refs.wide[...], refs.v0[...])
-    wait_v(1)
-    refs.up1[...] = dot(refs.wide[...], refs.v1[...])
-    early.rest(lambda g: unpack_rows(refs.rowsb, refs.wide, g))
-    wait_v(2)
-    expert_back(refs.wide, refs.gate1[...], refs.up1[...], refs.v0, refs.v1, refs.v2)
-    send_back(back1, refs.wide, refs.packed)
-    hidden = (silu_parts(refs.gate1[...])[0] * refs.up1[...]).astype(bf16)
-    expert_out(hidden, refs.v2, refs.wide)
+    early.wait_right()
+    early.wait_left()
+    early.wait_far()
+    gw1, uw1, dw1 = experts.ready(1)
+
+    def both1(g):
+        at = chunk_rows(g)
+        rows = unpack_rows(refs.rowsc, refs.wide, g)
+        gate_pre, up_pre = dot(rows, gw1[...]), dot(rows, uw1[...])
+        refs.hidden[at, :] = (silu_parts(gate_pre)[0] * up_pre).astype(bf16)
+        rows = unpack_rows(refs.rowsb, refs.wide, g)
+        pack_rows(
+            expert_back(rows, gate_pre, up_pre, gw1, uw1, dw1), refs.packed, back1.part, g
+        )
+
+    def out1(g):
+        pack_rows(expert_out(refs.hidden[chunk_rows(g), :], dw1), refs.packed, refs.part1, g)
+
+    second.chunks(both1, back1.start_near)
+    back1.start_far()
+    pl.loop(0, 2)(out1)
     for i in range(NZ):
         back1.relay(i)
-    for g in range(DP):
-        pack_rows(refs.wide, refs.packed, refs.part1, g)
+    pl.loop(2, DP)(out1)
     for i in range(NZ):
         back1.finish(i)
     back1.arrive()
-    for each in (first, early, second, out0, back1):
+    for each in (first, early, second, out0, back1, experts):
         each.drain()
 
 
 def backward_run(refs):
     e, _, _, _, right, left, _ = places()
+    section = lax.axis_index("section")
     greet(e, right, left)
     wait_w = fetch_attn(refs, 1)
-    wait_v = fetch_expert(refs, 0)
+    experts = Experts(refs, 1)
+    experts.start()
     again = dispatch_of(refs, "a")
     out1, back0 = combine_of(refs, "a"), combine_of(refs, "b")
     w = refs.some("w", 3)
@@ -632,8 +702,9 @@
     greeted()
     out1.start_far()
     out1.start_near()
+    experts.send()
     attend_back(
-        refs.dy[...], refs.act0[...], *[ref[...] for ref in kept_refs(refs, 1)], w, wait_w,
+        refs.dy[section], refs.act0[...], *[ref[...] for ref in kept_refs(refs, 1)], w, wait_w,
         refs.tokens, refs.n1, refs.dl1, refs.dq1, refs.dr1, refs.grad1,
     )
     wait_w = fetch_attn(refs, 0)
@@ -650,11 +721,20 @@
     again.relay(7)
     for i in range(NZ):
         out1.finish(i)
-    again.rest(lambda g: unpack_rows(refs.rowsa, refs.wide, g))
-    for k in range(3):
-        wait_v(k)
-    expert_back(refs.wide, refs.gate0[...], refs.up0[...], refs.v0, refs.v1, refs.v2)
-    send_back(back0, refs.wide, refs.packed)
+    gw, uw, dw = experts.ready(0)
+
+    def backward0(g):
+        at = chunk_rows(g)
+        rows = unpack_rows(refs.rowsa, refs.wide, g)
+        pack_rows(
+            expert_back(rows, refs.gate0[at, :], refs.up0[at, :], gw, uw, dw),
+            refs.packed,
+            back0.part,
+            g,
+        )
+
+    again.chunks(backward0, back0.start_near)
+    back0.start_far()
     for i in range(NZ):
         back0.relay(i)
     out1.arrive()
@@ -667,10 +747,10 @@
     back0.arrive()
     unpack_tokens(refs.homeb, refs.route_col0[...], refs.tokens)
     attend_back(
-        refs.grad1[...], refs.x[...], *[ref[...] for ref in kept_refs(refs, 0)], w, wait_w,
+        refs.grad1[...], refs.x[section], *[ref[...] for ref in kept_refs(refs, 0)], w, wait_w,
         refs.tokens, refs.n0, refs.dl0, refs.dq0, refs.dr0, refs.grad0,
     )
-    for each in (again, out1, back0):
+    for each in (again, out1, back0, experts):
         each.drain()
 
 
@@ -960,10 +1040,6 @@
     attn_own = (w_down[0], w_qk[0], w_up[0])
     experts_own = (e_gate[0, 0], e_up[0, 0], e_down[0, 0])
     attn = attn_own + tuple(swap(w) for w in attn_own)
-    experts = experts_own + tuple(swap(w) for w in experts_own)
-    x = lax.dynamic_index_in_dim(x_in[:, 0], section, 0, keepdims=False)
-    dy = lax.dynamic_index_in_dim(dy_out[:, 0], section, 0, keepdims=False)
-
     def both_layers(table):
         other = swap(lax.dynamic_index_in_dim(table, 1 - section, 0, keepdims=False))
         own = lax.dynamic_index_in_dim(table, section, 0, keepdims=False)
@@ -974,13 +1050,13 @@
     route_rows = tuple(r.reshape(1, SEQ) for r in route_cols)
 
     whole = {
-        "x": (x, VMEM),
-        "dy": (dy, VMEM),
+        "x": (x_in[:, 0], VMEM),
+        "dy": (dy_out[:, 0], VMEM),
         **{f"route_row{k}": (route_rows[k], VMEM) for k in range(2)},
         **{f"route_col{k}": (route_cols[k], VMEM) for k in range(2)},
         **{f"gate_col{k}": (gate_cols[k], VMEM) for k in range(2)},
         **named("attn", [(w, ANY) for w in attn]),
-        **named("expert", [(w, ANY) for w in experts]),
+        **named("expert", [(w, ANY) for w in experts_own]),
     }
     kept = fused(
         forward_run,
@@ -997,8 +1073,8 @@
         },
         {
             **COMMON,
-            "gate1": pltpu.VMEM(PRE, f32),
-            "up1": pltpu.VMEM(PRE, f32),
+            **Experts.scratch(2),
+            "hidden": pltpu.VMEM(PRE, bf16),
             **dispatch_scratch("a"),
             **dispatch_scratch("b"),
             **dispatch_scratch("c"),
@@ -1020,6 +1096,7 @@
         {"act1": shaped(*TOKENS), **factor_shapes(1), **factor_shapes(0)},
         {
             **COMMON,
+            **Experts.scratch(1),
             **dispatch_scratch("a"),
             **combine_scratch("a", skip=("parta",)),
             **combine_scratch("b"),

time: 366 us -> 340 us (0.929); the launches traced: 360 us -> 338 us
  Pallas kernels: 335 us -> 321 us
  waiting for transfers between devices: 8.73 us -> 3.64 us
    pallas_call x2, Pallas kernels: 287 us -> 270 us  [fused(): pl.pallas_call(kernel, name=name, out_shape=list(outs.values()), in_specs...]
    ppermute x8 -> x5, waiting for transfers between devices: 8.73 us -> 3.64 us  [swap(): return lax.ppermute(value, 'section', [(0, 1), (1, 0)])]
  transfers between devices with their start and end apart: 8 -> 5, of which waited for: 5 -> 1; matrix products, arithmetic and copies ran while one was open for 2% -> 1% of each run, Pallas kernels for 0% -> 0%
where the time goes in v4:
time: 340 us; the launch traced here: 338 us
  Pallas kernels  321 us (94%)
  local copies, waits for them, and re-layouts  9.57 us (3%)
  waiting for transfers between devices  3.64 us (1%)
    pallas_call x2, Pallas kernels, fused(): pl.pallas_call(kernel, name=name, out_shape=list(outs.values()), in_specs...  270 us
    pallas_call x1, Pallas kernels, weight_grads(): pl.pallas_call(grads_kernel, name='weight_grads', out_shape=[jax.ShapeDty...  50.8 us
    unnamed x13, local copies, waits for them, and re-layouts  7.84 us
  transfers between devices with their start and end apart: 5, of which 1 were waited for; matrix products, arithmetic and copies ran while one was open for 1% of the time, Pallas kernels for 0%

profile of v4, /device:TPU:0, one launch (start us, length us, event | category | flops | bytes accessed | tf_op | source)
XLA Modules:
  0.0 337.8 jit_solution(10949602928655608776)
XLA Ops:
  0.6 0.1 collective-permute-start.2
  0.7 0.5 collective-permute-start.4
  1.2 0.7 fusion.1
  1.9 0.1 copy.25
  2.0 0.1 collective-permute-start
  2.1 0.7 fusion.3
  2.8 0.1 copy.28
  2.9 0.4 collective-permute-start.1
  3.4 0.3 collective-permute-start.3
  3.6 0.1 copy.29
  3.7 0.1 copy.26
  3.8 3.6 %collective-permute-done = s32[64,1]{1,0:T(8,128)S(1)} collective-permute-done((s32[64,1]{1,0:T(8,128)S(1)}, s32[64,1]{1,0:T(8,128)S(1)}, u32[]{:S(2)}, u32[]{:S(2)}) %collective-permute-start) | collective-permute-done | bytes 288 | tf_op jit(solution)/shard_map/ppermute | solution.py:1035
  7.5 1.3 fusion.4
  8.7 0.0 collective-permute-done.1
  8.7 0.6 broadcast_select_fusion
  9.4 0.0 collective-permute-done.3.refs_12_
  9.4 0.0 copy-start.2
  9.4 0.0 collective-permute-done.2.refs_11_
  9.4 0.0 copy-start
  9.4 0.0 collective-permute-done.4.refs_13_
  9.4 0.6 copy-done.2
  10.0 0.7 copy-done
  10.7 165.9 %forward.1 = (bf16[64,3584]{1,0:T(8,128)(2,1)}, bf16[64,3584]{1,0:T(8,128)(2,1)}, bf16[64,256]{1,0:T(8,128)(2,1)}, bf16[64,256]{1,0:T(8,128)(2,1)}, f32[64,64]{1...) custom-call(bf16[2,64,3584]{2,1,0:T(8,128)(2,1)} %bitcast.39, ...), custom_call_target="tpu_custom_call" | custom-call | tf_op jit(solution)/shard_map/forward/pallas_call | solution.py:451
  176.6 103.9 %backward.1 = (bf16[64,3584]{1,0:T(8,128)(2,1)}, bf16[64,3584]{1,0:T(8,128)(2,1)}, bf16[64,256]{1,0:T(8,128)(2,1)}, bf16[64,256]{1,0:T(8,128)(2,1)}, bf16[64,358...) custom-call(bf16[2,64,3584]{2,1,0:T(8,128)(2,1)} %bitcast.40, ...), custom_call_target="tpu_custom_call" | custom-call | tf_op jit(solution)/shard_map/backward/pallas_call | solution.py:451
  280.5 50.8 %weight_grads.1 = (bf16[2,64,3584]{2,1,0:T(8,128)(2,1)}, bf16[2,64,3584]{2,1,0:T(8,128)(2,1)}, f32[28,256]{1,0:T(8,128)}, f32[2,256]{1,0:T(2,128)}, f32[28,256]{1,0:T(8,128)}) custom-call(bf16[64,3584]{1,0:T(8,128)(2,1)} %get-tuple-element.51.n0, bf16[64,256]{1,0:T(8,128)(2,1)} %get-tuple-element.52.dl0, bf16[64,256]{1,0:T(8,128)(2,1)} %get-tuple-element.38.refs_19_.la0, ...), custom_call_target="tpu_custom_call" | custom-call | tf_op jit(solution)/shard_map/weight_grads/pallas_call | solution.py:1000
  331.3 0.0 copy-start.1
  331.3 1.5 copy.33
  332.7 1.4 copy.34
  334.1 0.0 copy-start.3
  334.1 2.2 copy.38
  336.3 0.0 copy-done.1
  336.3 0.9 copy.39
  337.2 0.0 copy-done.3
  337.2 0.6 copy.40
Async XLA Ops:
  0.6 8.7 %collective-permute-start.2 = (bf16[3584,256]{1,0:T(8,128)(2,1)}, bf16[3584,256]{1,0:T(8,128)(2,1)S(1)}, u32[]{:S(2)}, u32[]{:S(2)}) collective-permute-start(bf16[3584,256]{1,0:T(8,128)(2,1)} %bitcast.27), channel_id=1, source_target_pairs={{0,128},{128,0},{1,129},{129,1},{2,130},{130,2},{3,131},{131,3},{4... | collective-permute-start | bytes 5505032 | tf_op jit(solution)/shard_map/ppermute | solution.py:1035
  0.7 8.6 %collective-permute-start.4 = (bf16[256,3584]{1,0:T(8,128)(2,1)}, bf16[256,3584]{1,0:T(8,128)(2,1)}, u32[]{:S(2)}, u32[]{:S(2)}) collective-permute-start(bf16[256,3584]{1,0:T(8,128)(2,1)} %bitcast.30), channel_id=1, source_target_pairs={{0,128},{128,0},{1,129},{129,1},{2,130},{130,2},{3,131},{131,3},{4... | collective-permute-start | bytes 5505032 | tf_op jit(solution)/shard_map/ppermute | solution.py:1035
  2.0 5.5 %collective-permute-start = (s32[64,1]{1,0:T(8,128)S(1)}, s32[64,1]{1,0:T(8,128)S(1)}, u32[]{:S(2)}, u32[]{:S(2)}) collective-permute-start(s32[64,1]{1,0:T(8,128)S(1)} %copy.25), channel_id=1, source_target_pairs={{0,128},{128,0},{1,129},{129,1},{2,130},{130,2},{3,131},{131,3},{4... | collective-permute-start | bytes 776 | tf_op jit(solution)/shard_map/ppermute | solution.py:1035
  2.9 5.8 %collective-permute-start.1 = (f32[64,1]{1,0:T(8,128)S(1)}, f32[64,1]{1,0:T(8,128)S(1)}, u32[]{:S(2)}, u32[]{:S(2)}) collective-permute-start(f32[64,1]{1,0:T(8,128)S(1)} %copy.28), channel_id=1, source_target_pairs={{0,128},{128,0},{1,129},{129,1},{2,130},{130,2},{3,131},{131,3},{4... | collective-permute-start | bytes 776 | tf_op jit(solution)/shard_map/ppermute | solution.py:1035
  3.4 6.0 %collective-permute-start.3 = (bf16[256,256]{1,0:T(8,128)(2,1)}, bf16[256,256]{1,0:T(8,128)(2,1)S(1)}, u32[]{:S(2)}, u32[]{:S(2)}) collective-permute-start(bf16[256,256]{1,0:T(8,128)(2,1)} %bitcast.45), channel_id=1, source_target_pairs={{0,128},{128,0},{1,129},{129,1},{2,130},{130,2},{3,131},{131,3},{4... | collective-permute-start | bytes 393224 | tf_op jit(solution)/shard_map/ppermute | solution.py:1035
  9.4 0.7 copy-start.2
  9.4 1.3 copy-start
  331.3 5.0 %copy-start.1 = (bf16[2,64,3584]{2,1,0:T(8,128)(2,1)S(1)}, bf16[2,64,3584]{2,1,0:T(8,128)(2,1)}, u32[]{:S(2)}) copy-start(bf16[2,64,3584]{2,1,0:T(8,128)(2,1)} %get-tuple-element.63) | copy-start | bytes 2752516
  334.1 3.1 copy-start.3

commit v5 on v4

--- a/solution.py
+++ b/solution.py
@@ -17,9 +17,9 @@
 CAP = 3
 NZ = 8
 NY = 4
-PIECE = 512
-PIECES = 7
-BLOCK = (8, CAP * PIECE)
+PIECE = 896
+PIECES = 4
+BLOCK = (PIECES, CAP * PIECE)
 PACKED = PIECES * EXPERTS
 ORDER = (0, 1, 7, 2, 6, 3, 5, 4)
 MESH = pl.DeviceIdType.MESH
@@ -56,15 +56,15 @@
 
 
 def spread_matrix():
-    rows = lax.broadcasted_iota(jnp.int32, (EXPERTS * 8, PACKED), 0)
-    cols = lax.broadcasted_iota(jnp.int32, (EXPERTS * 8, PACKED), 1)
-    return ((rows % 8) * EXPERTS + rows // 8 == cols).astype(f32).astype(bf16)
+    rows = lax.broadcasted_iota(jnp.int32, (PACKED, PACKED), 0)
+    cols = lax.broadcasted_iota(jnp.int32, (PACKED, PACKED), 1)
+    return ((rows % PIECES) * EXPERTS + rows // PIECES == cols).astype(f32).astype(bf16)
 
 
 def gather_matrix():
-    rows = lax.broadcasted_iota(jnp.int32, (PACKED, EXPERTS * 8), 0)
-    cols = lax.broadcasted_iota(jnp.int32, (PACKED, EXPERTS * 8), 1)
-    return ((cols % 8) * EXPERTS + cols // 8 == rows).astype(f32).astype(bf16)
+    rows = lax.broadcasted_iota(jnp.int32, (PACKED, PACKED), 0)
+    cols = lax.broadcasted_iota(jnp.int32, (PACKED, PACKED), 1)
+    return ((cols % PIECES) * EXPERTS + cols // PIECES == rows).astype(f32).astype(bf16)
 
 
 def slot_rows(route_row):
@@ -102,7 +102,7 @@
 
 
 def unpack_tokens(blocks_ref, route_col, token_ref):
-    packed = dot(gather_matrix(), blocks_ref[...].reshape(EXPERTS * 8, BLOCK[1])).astype(bf16)
+    packed = dot(gather_matrix(), blocks_ref[...].reshape(PACKED, BLOCK[1])).astype(bf16)
     columns = slot_columns(route_col)
     for r in range(PIECES):
         stacked = jnp.concatenate(
@@ -391,7 +391,7 @@
 
 def unpack_rows(rows, wide, g):
     packed = dot(
-        gather_matrix(), rows[pl.ds(g * EXPERTS, EXPERTS)].reshape(EXPERTS * 8, BLOCK[1])
+        gather_matrix(), rows[pl.ds(g * EXPERTS, EXPERTS)].reshape(PACKED, BLOCK[1])
     ).astype(bf16)
     for s in range(CAP):
         for r in range(PIECES):
@@ -1031,6 +1031,30 @@
     )(*layer0, *layer1)
 
 
+def place_kernel(act, grad, down, qk, up, act_o, grad_o, down_o, qk_o, up_o):
+    act_o[...] = act[...]
+    grad_o[...] = grad[...]
+    down_o[...] = down[...].reshape(28, 1, LAT)
+    qk_o[...] = qk[...]
+    up_o[...] = up[...].reshape(28, 1, LAT)
+
+
+def place_results(results):
+    return pl.pallas_call(
+        place_kernel,
+        name="place_results",
+        out_shape=[
+            shaped(2, *TOKENS),
+            shaped(2, *TOKENS),
+            shaped(28, 1, LAT, dtype=f32),
+            shaped(2, LAT, dtype=f32),
+            shaped(28, 1, LAT, dtype=f32),
+        ],
+        in_specs=[VMEM] * 5,
+        out_specs=[VMEM] * 5,
+    )(*results)
+
+
 def swap(value):
     return lax.ppermute(value, "section", [(0, 1), (1, 0)])
 
@@ -1107,13 +1131,13 @@
         tuple({**kept, **done}[f"{k}{layer}"] for k in ("n", "dl", "latent", "dq", "dr", "mixed", "act", "grad"))
         for layer in range(2)
     ]
-    activations, grads_in, g_down, g_qk, g_up_t = weight_grads(*layers)
+    activations, grads_in, g_down, g_qk, g_up_t = place_results(weight_grads(*layers))
     return (
         activations[None, :, None],
         grads_in[None, :, None],
-        g_down[None],
+        jnp.swapaxes(g_down, 0, 1),
         g_qk[None],
-        g_up_t[None],
+        jnp.swapaxes(g_up_t, 0, 1),
     )
 
 

time: 340 us -> 312 us (0.918)
  Pallas kernels: 321 us -> 299 us
  local copies, waits for them, and re-layouts: 9.57 us -> 2.99 us
    pallas_call x2, Pallas kernels: 270 us -> 244 us  [fused(): pl.pallas_call(kernel, name=name, out_shape=list(outs.values()), in_specs...]
    unnamed x13 -> x4, local copies, waits for them, and re-layouts: 7.84 us -> 1.26 us
where the time goes in v5:
time: 312 us; the launch traced here: 309 us
  Pallas kernels  299 us (96%)
  waiting for transfers between devices  3.82 us (1%)
    pallas_call x2, Pallas kernels, fused(): pl.pallas_call(kernel, name=name, out_shape=list(outs.values()), in_specs...  244 us
    pallas_call x1, Pallas kernels, weight_grads(): pl.pallas_call(grads_kernel, name='weight_grads', out_shape=[jax.ShapeDty...  51.5 us
  transfers between devices with their start and end apart: 5, of which 1 were waited for; matrix products, arithmetic and copies ran while one was open for 1% of the time, Pallas kernels for 0%

profile of v5, /device:TPU:0, one launch (start us, length us, event | category | flops | bytes accessed | tf_op | source)
XLA Modules:
  0.0 309.4 jit_solution(14006073402616491845)
XLA Ops:
  0.6 0.1 collective-permute-start.2
  0.7 0.5 collective-permute-start.4
  1.2 0.7 fusion.1
  1.9 0.1 copy.23
  2.0 0.1 collective-permute-start
  2.1 0.7 fusion.3
  2.8 0.1 copy.26
  2.9 0.4 collective-permute-start.1
  3.4 0.1 collective-permute-start.3
  3.5 0.1 copy.27
  3.6 0.1 copy.24
  3.7 3.8 %collective-permute-done = s32[64,1]{1,0:T(8,128)S(1)} collective-permute-done((s32[64,1]{1,0:T(8,128)S(1)}, s32[64,1]{1,0:T(8,128)S(1)}, u32[]{:S(2)}, u32[]{:S(2)}) %collective-permute-start) | collective-permute-done | bytes 288 | tf_op jit(solution)/shard_map/ppermute | solution.py:1059
  7.5 1.3 fusion.4
  8.7 0.0 collective-permute-done.1
  8.7 0.6 broadcast_select_fusion
  9.4 0.0 collective-permute-done.3.refs_12_
  9.4 0.0 copy-start.1
  9.4 0.0 collective-permute-done.2.refs_11_
  9.4 0.0 copy-start
  9.4 0.0 collective-permute-done.4.refs_13_
  9.4 0.6 copy-done.1
  10.0 0.6 copy-done
  10.6 150.1 %forward.1 = (bf16[64,3584]{1,0:T(8,128)(2,1)}, bf16[64,3584]{1,0:T(8,128)(2,1)}, bf16[64,256]{1,0:T(8,128)(2,1)}, bf16[64,256]{1,0:T(8,128)(2,1)}, f32[64,64]{1...) custom-call(bf16[2,64,3584]{2,1,0:T(8,128)(2,1)} %bitcast.39, ...), custom_call_target="tpu_custom_call" | custom-call | tf_op jit(solution)/shard_map/forward/pallas_call | solution.py:451
  160.8 94.4 %backward.1 = (bf16[64,3584]{1,0:T(8,128)(2,1)}, bf16[64,3584]{1,0:T(8,128)(2,1)}, bf16[64,256]{1,0:T(8,128)(2,1)}, bf16[64,256]{1,0:T(8,128)(2,1)}, bf16[64,358...) custom-call(bf16[2,64,3584]{2,1,0:T(8,128)(2,1)} %bitcast.40, ...), custom_call_target="tpu_custom_call" | custom-call | tf_op jit(solution)/shard_map/backward/pallas_call | solution.py:451
  255.1 51.5 %weight_grads.1 = (bf16[2,64,3584]{2,1,0:T(8,128)(2,1)}, bf16[2,64,3584]{2,1,0:T(8,128)(2,1)}, f32[28,256]{1,0:T(8,128)}, f32[2,256]{1,0:T(2,128)}, f32[28,256]{1,0:T(8,128)}) custom-call(bf16[64,3584]{1,0:T(8,128)(2,1)} %get-tuple-element.56.n0, bf16[64,256]{1,0:T(8,128)(2,1)} %get-tuple-element.57.dl0, bf16[64,256]{1,0:T(8,128)(2,1)} %get-tuple-element.43.refs_19_.la0, ...), custom_call_target="tpu_custom_call" | custom-call | tf_op jit(solution)/shard_map/weight_grads/pallas_call | solution.py:1000
  306.6 2.8 place_results.1
Async XLA Ops:
  0.6 8.7 %collective-permute-start.2 = (bf16[3584,256]{1,0:T(8,128)(2,1)}, bf16[3584,256]{1,0:T(8,128)(2,1)S(1)}, u32[]{:S(2)}, u32[]{:S(2)}) collective-permute-start(bf16[3584,256]{1,0:T(8,128)(2,1)} %bitcast.27), channel_id=1, source_target_pairs={{0,128},{128,0},{1,129},{129,1},{2,130},{130,2},{3,131},{131,3},{4... | collective-permute-start | bytes 5505032 | tf_op jit(solution)/shard_map/ppermute | solution.py:1059
  0.7 8.6 %collective-permute-start.4 = (bf16[256,3584]{1,0:T(8,128)(2,1)}, bf16[256,3584]{1,0:T(8,128)(2,1)}, u32[]{:S(2)}, u32[]{:S(2)}) collective-permute-start(bf16[256,3584]{1,0:T(8,128)(2,1)} %bitcast.30), channel_id=1, source_target_pairs={{0,128},{128,0},{1,129},{129,1},{2,130},{130,2},{3,131},{131,3},{4... | collective-permute-start | bytes 5505032 | tf_op jit(solution)/shard_map/ppermute | solution.py:1059
  2.0 5.5 %collective-permute-start = (s32[64,1]{1,0:T(8,128)S(1)}, s32[64,1]{1,0:T(8,128)S(1)}, u32[]{:S(2)}, u32[]{:S(2)}) collective-permute-start(s32[64,1]{1,0:T(8,128)S(1)} %copy.23), channel_id=1, source_target_pairs={{0,128},{128,0},{1,129},{129,1},{2,130},{130,2},{3,131},{131,3},{4... | collective-permute-start | bytes 776 | tf_op jit(solution)/shard_map/ppermute | solution.py:1059
  2.9 5.8 %collective-permute-start.1 = (f32[64,1]{1,0:T(8,128)S(1)}, f32[64,1]{1,0:T(8,128)S(1)}, u32[]{:S(2)}, u32[]{:S(2)}) collective-permute-start(f32[64,1]{1,0:T(8,128)S(1)} %copy.26), channel_id=1, source_target_pairs={{0,128},{128,0},{1,129},{129,1},{2,130},{130,2},{3,131},{131,3},{4... | collective-permute-start | bytes 776 | tf_op jit(solution)/shard_map/ppermute | solution.py:1059
  3.4 6.0 %collective-permute-start.3 = (bf16[256,256]{1,0:T(8,128)(2,1)}, bf16[256,256]{1,0:T(8,128)(2,1)S(1)}, u32[]{:S(2)}, u32[]{:S(2)}) collective-permute-start(bf16[256,256]{1,0:T(8,128)(2,1)} %bitcast.43), channel_id=1, source_target_pairs={{0,128},{128,0},{1,129},{129,1},{2,130},{130,2},{3,131},{131,3},{4... | collective-permute-start | bytes 393224 | tf_op jit(solution)/shard_map/ppermute | solution.py:1059
  9.4 0.7 copy-start.1
  9.4 1.3 copy-start

commit v6 on v5

--- a/solution.py
+++ b/solution.py
@@ -121,7 +121,7 @@
     return e, d, e // NY, e % NY, (d + 1) % DP, (d + DP - 1) % DP, (d + 2) % DP
 
 
-def greet(e, right, left):
+def greet(e, right, left, more=()):
     barrier = pltpu.get_barrier_semaphore()
     for k in range(1, EXPERTS):
         pl.semaphore_signal(
@@ -130,11 +130,12 @@
     for side in (right, left):
         pl.semaphore_signal(barrier, inc=1, device_id={"dp": side}, device_id_type=MESH)
     partner = {"section": 1 - lax.axis_index("section")}
-    pl.semaphore_signal(barrier, inc=1, device_id=partner, device_id_type=MESH)
-
-
-def greeted():
-    pl.semaphore_wait(pltpu.get_barrier_semaphore(), EXPERTS + 2)
+    for peer in (partner, *more):
+        pl.semaphore_signal(barrier, inc=1, device_id=peer, device_id_type=MESH)
+
+
+def greeted(more=0):
+    pl.semaphore_wait(pltpu.get_barrier_semaphore(), EXPERTS + 2 + more)
 
 
 def remote(src, dst, send, recv, where):
@@ -690,7 +691,9 @@
 def backward_run(refs):
     e, _, _, _, right, left, _ = places()
     section = lax.axis_index("section")
-    greet(e, right, left)
+    grads = Grads(refs)
+    more = grads.peers()
+    greet(e, right, left, more)
     wait_w = fetch_attn(refs, 1)
     experts = Experts(refs, 1)
     experts.start()
@@ -699,7 +702,7 @@
     w = refs.some("w", 3)
 
     unpack_tokens(refs.back1, refs.route_col1[...], refs.tokens)
-    greeted()
+    greeted(len(more))
     out1.start_far()
     out1.start_near()
     experts.send()
@@ -735,32 +738,49 @@
 
     again.chunks(backward0, back0.start_near)
     back0.start_far()
+    grads.lay_x(1, refs.n1, refs.dl1, refs.latent1, refs.dq1)
     for i in range(NZ):
         back0.relay(i)
+    grads.x_ring.start(1)
+    grads.lay_y(1, refs.dr1, refs.mixed1)
+    grads.y_ring.start(1)
     out1.arrive()
     unpack_tokens(refs.homea, refs.route_col1[...], refs.tokens)
     refs.act1[...] = (
         refs.resid1[...].astype(f32) + refs.gate_col1[...] * refs.tokens[...]
     ).astype(bf16)
+    grads.trade(0, refs.act_o, refs.act0, refs.act1)
     for i in range(NZ):
         back0.finish(i)
+    grads.x_ring.relay(1)
+    grads.y_ring.relay(1)
     back0.arrive()
     unpack_tokens(refs.homeb, refs.route_col0[...], refs.tokens)
     attend_back(
         refs.grad1[...], refs.x[section], *[ref[...] for ref in kept_refs(refs, 0)], w, wait_w,
         refs.tokens, refs.n0, refs.dl0, refs.dq0, refs.dr0, refs.grad0,
     )
-    for each in (again, out1, back0, experts):
+    grads.lay_x(0, refs.n0, refs.dl0, refs.latent0, refs.dq0)
+    grads.x_ring.start(0)
+    grads.x_ring.own()
+    grads.lay_y(0, refs.dr0, refs.mixed0)
+    grads.y_ring.start(0)
+    grads.y_ring.own()
+    grads.trade(1, refs.grad_o, refs.grad0, refs.grad1)
+    grads.x_ring.relay(0)
+    grads.y_ring.relay(0)
+    grads.sums()
+    for each in (again, out1, back0, experts, grads):
         each.drain()
 
 
-def factor_shapes(layer):
+def factor_scratch(layer):
     return {
-        f"n{layer}": shaped(*TOKENS),
-        f"dl{layer}": shaped(SEQ, LAT),
-        f"dq{layer}": shaped(SEQ, LAT),
-        f"dr{layer}": shaped(*TOKENS),
-        f"grad{layer}": shaped(*TOKENS),
+        f"n{layer}": pltpu.VMEM(TOKENS, bf16),
+        f"dl{layer}": pltpu.VMEM((SEQ, LAT), bf16),
+        f"dq{layer}": pltpu.VMEM((SEQ, LAT), bf16),
+        f"dr{layer}": pltpu.VMEM(TOKENS, bf16),
+        f"grad{layer}": pltpu.VMEM(TOKENS, bf16),
     }
 
 
@@ -829,18 +849,18 @@
             {"section": 1 - s},
         ).start()
 
-    def relay(self):
-        for layer, way in ((0, 1), (1, 3)):
-            buf = self.relay_buf.at[layer]
-            remote(buf, buf, self.ssem, self.rsem.at[layer], self.near(1)).wait_recv()
-            origin = (self.position + 4 - way) % 4
-            remote(
-                buf,
-                self.got.at[self.section, origin],
-                self.ssem,
-                self.fsem.at[self.section, 2],
-                {**self.near(way), "section": layer},
-            ).start()
+    def relay(self, layer):
+        way = 1 if layer == 0 else 3
+        buf = self.relay_buf.at[layer]
+        remote(buf, buf, self.ssem, self.rsem.at[layer], self.near(1)).wait_recv()
+        origin = (self.position + 4 - way) % 4
+        remote(
+            buf,
+            self.got.at[self.section, origin],
+            self.ssem,
+            self.fsem.at[self.section, 2],
+            {**self.near(way), "section": layer},
+        ).start()
 
     def arrive(self):
         for m in range(2):
@@ -863,172 +883,172 @@
     return total
 
 
-def grads_kernel(
-    n0, dl0, la0, dq0, dr0, mx0, act0, grad0, n1, dl1, la1, dq1, dr1, mx1, act1, grad1,
-    act_o, grad_o, down_o, qk_o, up_o,
-    xs, xg, xr, ys, yg, yr, td, sd, zd, zr, tu, su, zu, zv,
-    xssem, xfsem, xrsem, yssem, yfsem, yrsem, psem, qsem, asem, dsem, dr, usem, ur, zsem, zrecv,
-):
-    s = lax.axis_index("section")
-    e, d, z, y, right, left, opp = places()
-
-    def near_x(k):
-        return {"dp": (d + k) % 4}
-
-    def near_y(k):
-        return {"expert": z * NY + (y + k) % 4}
-
-    def near_z(k):
-        return {"expert": ((z + k) % NZ) * NY + y}
-
-    barrier = pltpu.get_barrier_semaphore()
-    peers = [{"section": 1 - s}]
-    for near in (near_x, near_y):
-        for k in (1, 3):
-            peers += [{**near(k), "section": 0}, {**near(k), "section": 1}]
-        peers.append(near(2))
-    peers += [near_z(k) for k in range(1, NZ)]
-    for peer in peers:
-        pl.semaphore_signal(barrier, inc=1, device_id=peer, device_id_type=MESH)
-    x_ring = Ring(s, d, near_x, xs, xg, xr, xssem, xfsem, xrsem)
-    y_ring = Ring(s, y, near_y, ys, yg, yr, yssem, yfsem, yrsem)
-    factors = ((n0, dl0, la0, dq0, dr0, mx0), (n1, dl1, la1, dq1, dr1, mx1))
-    by_x, by_y, small = quarter_matrix(True), quarter_matrix(False), small_matrix()
-    for layer, (n, dl, la, dq, _, _) in enumerate(factors):
-        lay_out(n[...], by_x, xs, layer)
-        moved = dot(la[...], small).astype(bf16)
+class Grads:
+    def __init__(self, refs):
+        self.refs = refs
+        self.s = lax.axis_index("section")
+        _, self.d, self.z, self.y, _, _, _ = places()
+        self.x_ring = Ring(
+            self.s, self.d, self.near_x, refs.xs, refs.xg, refs.xr, refs.xssem, refs.xfsem, refs.xrsem
+        )
+        self.y_ring = Ring(
+            self.s, self.y, self.near_y, refs.ys, refs.yg, refs.yr, refs.yssem, refs.yfsem, refs.yrsem
+        )
+
+    def near_x(self, k):
+        return {"dp": (self.d + k) % 4}
+
+    def near_y(self, k):
+        return {"expert": self.z * NY + (self.y + k) % 4}
+
+    def near_z(self, k):
+        return {"expert": ((self.z + k) % NZ) * NY + self.y}
+
+    def peers(self):
+        other = {"section": 1 - self.s}
+        return [
+            {**self.near_x(1), **other},
+            {**self.near_x(3), **other},
+            {**self.near_y(1), **other},
+            {**self.near_y(3), **other},
+            self.near_x(2),
+        ]
+
+    def lay_x(self, layer, n, dl, la, dq):
+        xs = self.refs.xs
+        lay_out(n[...], quarter_matrix(True), xs, layer)
+        moved = dot(la[...], small_matrix()).astype(bf16)
         for q in range(4):
             xs[layer, q, :, 1024:1280] = dl[...]
             xs[layer, q, :, 1280:1536] = moved[:, q * 256 : (q + 1) * 256]
             xs[layer, q, :, 1536:1792] = dq[...]
-    pl.semaphore_wait(barrier, len(peers))
-    x_ring.start(0)
-    x_ring.start(1)
-    for layer, (_, _, _, _, dres, mx) in enumerate(factors):
-        lay_out(dres[...], by_y, ys, layer)
+
+    def lay_y(self, layer, dres, mx):
+        lay_out(dres[...], quarter_matrix(False), self.refs.ys, layer)
         for q in range(4):
-            ys[layer, q, :, 1024:1280] = mx[...]
-    y_ring.start(0)
-    y_ring.start(1)
-    x_ring.own()
-    y_ring.own()
-
-    for k, (out, first_layer, second_layer) in enumerate(((act_o, act0, act1), (grad_o, grad0, grad1))):
+            self.refs.ys[layer, q, :, 1024:1280] = mx[...]
+
+    def trade(self, k, out, first_layer, second_layer):
+        refs, s = self.refs, self.s
         for here, keep, give in ((0, first_layer, second_layer), (1, second_layer, first_layer)):
 
             @pl.when(s == here)
             def _():
-                pltpu.make_async_copy(keep, out.at[s], asem.at[k]).start()
-                remote(give, out.at[s], psem, qsem.at[k], {"section": 1 - s}).start()
-
-    x_ring.relay()
-    y_ring.relay()
-
-    def rows(ring, start, width):
-        got = ring.got
-        return jnp.concatenate(
-            [got[m, q, :, start : start + width] for m in range(2) for q in range(4)], axis=0
-        )
-
-    x_ring.arrive()
-    total = t_times(rows(x_ring, 0, 1024), rows(x_ring, 1024, 256)).astype(bf16)
-    total_qk = t_times(rows(x_ring, 1280, 256), rows(x_ring, 1536, 256)).astype(bf16)
-    for q in range(4):
-        for c in range(4):
-            td[q, c * 64 : (c + 1) * 64, :] = total[c * 256 + q * 64 : c * 256 + (q + 1) * 64]
-        td[q, 256:320, :] = total_qk[q * 64 : (q + 1) * 64]
-    for k in (2, 1, 3):
-        remote(td.at[(y + k) % 4], sd.at[y], dsem, dr.at[4 - k - 1], near_y(k)).start()
-    y_ring.arrive()
-    total = t_times(rows(y_ring, 0, 1024), rows(y_ring, 1024, 256)).astype(bf16)
-    for q in range(4):
-        for c in range(4):
-            tu[q, c * 64 : (c + 1) * 64, :] = total[c * 256 + q * 64 : c * 256 + (q + 1) * 64]
-    for k in (2, 1, 3):
-        remote(tu.at[(d + k) % 4], su.at[d], usem, ur.at[4 - k - 1], near_x(k)).start()
-
-    def gathered(buf, recv, position):
-        for k in (1, 2, 3):
-            ref = buf.at[(position + k) % 4]
-            remote(ref, ref, dsem, recv.at[k - 1], near_x(1)).wait_recv()
-        return [buf[(position + k) % 4] for k in (1, 2, 3)]
-
-    summed = fold([td[y]] + gathered(sd, dr, y)).astype(bf16)
-    for k in range(NZ):
-        zd[k, 0:32, :] = summed[k * 32 : (k + 1) * 32]
-        zd[k, 32:40, :] = summed[256 + k * 8 : 264 + k * 8]
-    for k in range(1, NZ):
-        remote(zd.at[(z + k) % NZ], zr.at[z], zsem.at[0], zrecv.at[0, NZ - k - 1], near_z(k)).start()
-    summed = fold([tu[d]] + gathered(su, ur, d)).astype(bf16)
-    for k in range(NZ):
-        zu[k] = summed[k * 32 : (k + 1) * 32]
-    for k in range(1, NZ):
-        remote(zu.at[(z + k) % NZ], zv.at[z], zsem.at[1], zrecv.at[1, NZ - k - 1], near_z(k)).start()
-
-    def last(own, buf, which):
+                pltpu.make_async_copy(keep, out.at[s], refs.asem.at[k]).start()
+                remote(give, out.at[s], refs.psem, refs.qsem.at[k], {"section": 1 - s}).start()
+
+    def sums(self):
+        refs, s, d, z, y = self.refs, self.s, self.d, self.z, self.y
+
+        def rows(ring, start, width):
+            got = ring.got
+            return jnp.concatenate(
+                [got[m, q, :, start : start + width] for m in range(2) for q in range(4)], axis=0
+            )
+
+        x_ring, y_ring = self.x_ring, self.y_ring
+        x_ring.arrive()
+        total = t_times(rows(x_ring, 0, 1024), rows(x_ring, 1024, 256)).astype(bf16)
+        total_qk = t_times(rows(x_ring, 1280, 256), rows(x_ring, 1536, 256)).astype(bf16)
+        for q in range(4):
+            for c in range(4):
+                refs.td[q, c * 64 : (c + 1) * 64, :] = total[c * 256 + q * 64 : c * 256 + (q + 1) * 64]
+            refs.td[q, 256:320, :] = total_qk[q * 64 : (q + 1) * 64]
+        for k in (2, 1, 3):
+            remote(refs.td.at[(y + k) % 4], refs.sd.at[y], refs.dsem, refs.dr.at[4 - k - 1], self.near_y(k)).start()
+        y_ring.arrive()
+        total = t_times(rows(y_ring, 0, 1024), rows(y_ring, 1024, 256)).astype(bf16)
+        for q in range(4):
+            for c in range(4):
+                refs.tu[q, c * 64 : (c + 1) * 64, :] = total[c * 256 + q * 64 : c * 256 + (q + 1) * 64]
+        for k in (2, 1, 3):
+            remote(refs.tu.at[(d + k) % 4], refs.su.at[d], refs.usem, refs.ur.at[4 - k - 1], self.near_x(k)).start()
+
+        def gathered(buf, recv, position):
+            for k in (1, 2, 3):
+                ref = buf.at[(position + k) % 4]
+                remote(ref, ref, refs.dsem, recv.at[k - 1], self.near_x(1)).wait_recv()
+            return [buf[(position + k) % 4] for k in (1, 2, 3)]
+
+        summed = fold([refs.td[y]] + gathered(refs.sd, refs.dr, y)).astype(bf16)
+        for k in range(NZ):
+            refs.zd[k, 0:32, :] = summed[k * 32 : (k + 1) * 32]
+            refs.zd[k, 32:40, :] = summed[256 + k * 8 : 264 + k * 8]
         for k in range(1, NZ):
-            ref = buf.at[(z + k) % NZ]
-            remote(ref, ref, zsem.at[0], zrecv.at[which, k - 1], near_z(1)).wait_recv()
-        return fold([own[z]] + [buf[(z + k) % NZ] for k in range(1, NZ)])
-
-    mine = last(zd, zr, 0)
-    down_o[...] = mine[0:28]
-    qk_o[...] = mine[32:34]
-    mine = last(zu, zv, 1)
-    up_o[...] = mine[0:28]
-
-    x_ring.drain()
-    y_ring.drain()
-    for k, (out, some) in enumerate(((act_o, act0), (grad_o, grad0))):
-        pltpu.make_async_copy(some, out.at[s], asem.at[k]).wait()
-        remote(some, out.at[1 - s], psem, qsem.at[k], {"section": 1 - s}).wait_recv()
-    whole = act_o
-    remote(whole, whole, psem, qsem.at[0], {"section": 1 - s}).wait_send()
-    ref = td.at[pl.ds(0, 3)]
-    remote(ref, ref, dsem, dr.at[0], near_x(1)).wait_send()
-    ref = tu.at[pl.ds(0, 3)]
-    remote(ref, ref, usem, ur.at[0], near_x(1)).wait_send()
-    ref = zd.at[pl.ds(0, NZ - 1)]
-    remote(ref, ref, zsem.at[0], dr.at[0], near_x(1)).wait_send()
-    ref = zu.at[pl.ds(0, NZ - 1)]
-    remote(ref, ref, zsem.at[1], dr.at[0], near_x(1)).wait_send()
-
-
-def weight_grads(layer0, layer1):
+            remote(refs.zd.at[(z + k) % NZ], refs.zr.at[z], refs.zsem.at[0], refs.zrecv.at[0, NZ - k - 1], self.near_z(k)).start()
+        summed = fold([refs.tu[d]] + gathered(refs.su, refs.ur, d)).astype(bf16)
+        for k in range(NZ):
+            refs.zu[k] = summed[k * 32 : (k + 1) * 32]
+        for k in range(1, NZ):
+            remote(refs.zu.at[(z + k) % NZ], refs.zv.at[z], refs.zsem.at[1], refs.zrecv.at[1, NZ - k - 1], self.near_z(k)).start()
+
+        def last(own, buf, which):
+            for k in range(1, NZ):
+                ref = buf.at[(z + k) % NZ]
+                remote(ref, ref, refs.zsem.at[0], refs.zrecv.at[which, k - 1], self.near_z(1)).wait_recv()
+            return fold([own[z]] + [buf[(z + k) % NZ] for k in range(1, NZ)])
+
+        mine = last(refs.zd, refs.zr, 0)
+        refs.down_o[...] = mine[0:28]
+        refs.qk_o[...] = mine[32:34]
+        mine = last(refs.zu, refs.zv, 1)
+        refs.up_o[...] = mine[0:28]
+
+    def drain(self):
+        refs = self.refs
+        self.x_ring.drain()
+        self.y_ring.drain()
+        for k, (out, some) in enumerate(((refs.act_o, refs.act0), (refs.grad_o, refs.grad0))):
+            pltpu.make_async_copy(some, out.at[self.s], refs.asem.at[k]).wait()
+            remote(some, out.at[1 - self.s], refs.psem, refs.qsem.at[k], {"section": 1 - self.s}).wait_recv()
+        whole = refs.act_o
+        remote(whole, whole, refs.psem, refs.qsem.at[0], {"section": 1 - self.s}).wait_send()
+        ref = refs.td.at[pl.ds(0, 3)]
+        remote(ref, ref, refs.dsem, refs.dr.at[0], self.near_x(1)).wait_send()
+        ref = refs.tu.at[pl.ds(0, 3)]
+        remote(ref, ref, refs.usem, refs.ur.at[0], self.near_x(1)).wait_send()
+        ref = refs.zd.at[pl.ds(0, NZ - 1)]
+        remote(ref, ref, refs.zsem.at[0], refs.dr.at[0], self.near_x(1)).wait_send()
+        ref = refs.zu.at[pl.ds(0, NZ - 1)]
+        remote(ref, ref, refs.zsem.at[1], refs.dr.at[0], self.near_x(1)).wait_send()
+
+
+def grads_scratch():
     dma = pltpu.SemaphoreType.DMA
-    ring_sems = [dma, dma((2, 4)), dma((2,))]
-    return pl.pallas_call(
-        grads_kernel,
-        name="weight_grads",
-        out_shape=[
-            jax.ShapeDtypeStruct((2, SEQ, WIDTH), bf16),
-            jax.ShapeDtypeStruct((2, SEQ, WIDTH), bf16),
-            jax.ShapeDtypeStruct((28, LAT), f32),
-            jax.ShapeDtypeStruct((2, LAT), f32),
-            jax.ShapeDtypeStruct((28, LAT), f32),
-        ],
-        in_specs=[VMEM] * 16,
-        out_specs=[VMEM] * 5,
-        scratch_shapes=[
-            pltpu.VMEM((2, 4, SEQ, ROUND), bf16),
-            pltpu.VMEM((2, 4, SEQ, ROUND), bf16),
-            pltpu.VMEM((2, SEQ, ROUND), bf16),
-            pltpu.VMEM((2, 4, SEQ, SIDE), bf16),
-            pltpu.VMEM((2, 4, SEQ, SIDE), bf16),
-            pltpu.VMEM((2, SEQ, SIDE), bf16),
-            pltpu.VMEM((4, 320, LAT), bf16),
-            pltpu.VMEM((4, 320, LAT), bf16),
-            pltpu.VMEM((NZ, 40, LAT), bf16),
-            pltpu.VMEM((NZ, 40, LAT), bf16),
-            pltpu.VMEM((4, 256, LAT), bf16),
-            pltpu.VMEM((4, 256, LAT), bf16),
-            pltpu.VMEM((NZ, 32, LAT), bf16),
-            pltpu.VMEM((NZ, 32, LAT), bf16),
-        ]
-        + ring_sems * 2
-        + [dma, dma((2,)), dma((2,)), dma, dma((3,)), dma, dma((3,)), dma((2,)), dma((2, NZ - 1))],
-        compiler_params=pltpu.CompilerParams(collective_id=2, has_side_effects=True),
-    )(*layer0, *layer1)
+    buffers = {
+        "xs": (2, 4, SEQ, ROUND),
+        "xg": (2, 4, SEQ, ROUND),
+        "xr": (2, SEQ, ROUND),
+        "ys": (2, 4, SEQ, SIDE),
+        "yg": (2, 4, SEQ, SIDE),
+        "yr": (2, SEQ, SIDE),
+        "td": (4, 320, LAT),
+        "sd": (4, 320, LAT),
+        "zd": (NZ, 40, LAT),
+        "zr": (NZ, 40, LAT),
+        "tu": (4, 256, LAT),
+        "su": (4, 256, LAT),
+        "zu": (NZ, 32, LAT),
+        "zv": (NZ, 32, LAT),
+    }
+    sems = {
+        "xssem": dma,
+        "xfsem": dma((2, 4)),
+        "xrsem": dma((2,)),
+        "yssem": dma,
+        "yfsem": dma((2, 4)),
+        "yrsem": dma((2,)),
+        "psem": dma,
+        "qsem": dma((2,)),
+        "asem": dma((2,)),
+        "dsem": dma,
+        "dr": dma((3,)),
+        "usem": dma,
+        "ur": dma((3,)),
+        "zsem": dma((2,)),
+        "zrecv": dma((2, NZ - 1)),
+    }
+    return {**{k: pltpu.VMEM(v, bf16) for k, v in buffers.items()}, **sems}
 
 
 def place_kernel(act, grad, down, qk, up, act_o, grad_o, down_o, qk_o, up_o):
@@ -1117,9 +1137,19 @@
             "parta": (part1, VMEM),
             "back1": (back1, VMEM),
         },
-        {"act1": shaped(*TOKENS), **factor_shapes(1), **factor_shapes(0)},
+        {
+            "act_o": shaped(2, *TOKENS),
+            "grad_o": shaped(2, *TOKENS),
+            "down_o": shaped(28, LAT, dtype=f32),
+            "qk_o": shaped(2, LAT, dtype=f32),
+            "up_o": shaped(28, LAT, dtype=f32),
+        },
         {
             **COMMON,
+            "act1": pltpu.VMEM(TOKENS, bf16),
+            **factor_scratch(0),
+            **factor_scratch(1),
+            **grads_scratch(),
             **Experts.scratch(1),
             **dispatch_scratch("a"),
             **combine_scratch("a", skip=("parta",)),
@@ -1127,11 +1157,7 @@
         },
         1,
     )
-    layers = [
-        tuple({**kept, **done}[f"{k}{layer}"] for k in ("n", "dl", "latent", "dq", "dr", "mixed", "act", "grad"))
-        for layer in range(2)
-    ]
-    activations, grads_in, g_down, g_qk, g_up_t = place_results(weight_grads(*layers))
+    activations, grads_in, g_down, g_qk, g_up_t = place_results(list(done.values()))
     return (
         activations[None, :, None],
         grads_in[None, :, None],

time: 312 us -> 299 us (0.958)
  Pallas kernels: 299 us -> 288 us
    pallas_call x1 -> x0, Pallas kernels: 51.5 us -> none  [weight_grads(): pl.pallas_call(grads_kernel, name='weight_grads', out_shape=[jax.ShapeDty...]
    pallas_call x2, Pallas kernels: 244 us -> 285 us  [fused(): pl.pallas_call(kernel, name=name, out_shape=list(outs.values()), in_specs...]
where the time goes in v6:
time: 299 us; the launch traced here: 298 us
  Pallas kernels  288 us (96%)
  waiting for transfers between devices  3.82 us (1%)
  local copies, waits for them, and re-layouts  3 us (1%)
    pallas_call x2, Pallas kernels, fused(): pl.pallas_call(kernel, name=name, out_shape=list(outs.values()), in_specs...  285 us
  transfers between devices with their start and end apart: 5, of which 1 were waited for; matrix products, arithmetic and copies ran while one was open for 1% of the time, Pallas kernels for 0%

profile of v6, /device:TPU:0, one launch (start us, length us, event | category | flops | bytes accessed | tf_op | source)
XLA Modules:
  0.0 298.2 jit_solution(12702107802141803536)
XLA Ops:
  0.6 0.1 collective-permute-start.2
  0.7 0.5 collective-permute-start.4
  1.2 0.7 fusion.1
  1.9 0.1 copy.23
  2.0 0.1 collective-permute-start
  2.1 0.7 fusion.3
  2.8 0.1 copy.26
  2.9 0.4 collective-permute-start.1
  3.4 0.1 collective-permute-start.3
  3.5 0.1 copy.27
  3.6 0.1 copy.24
  3.7 3.8 %collective-permute-done = s32[64,1]{1,0:T(8,128)S(1)} collective-permute-done((s32[64,1]{1,0:T(8,128)S(1)}, s32[64,1]{1,0:T(8,128)S(1)}, u32[]{:S(2)}, u32[]{:S(2)}) %collective-permute-start) | collective-permute-done | bytes 288 | tf_op jit(solution)/shard_map/ppermute | solution.py:1079
  7.5 1.3 fusion.4
  8.7 0.0 collective-permute-done.1
  8.7 0.6 broadcast_select_fusion
  9.3 0.0 collective-permute-done.3.refs_12_
  9.4 0.0 copy-start.1
  9.4 0.0 collective-permute-done.2.refs_11_
  9.4 0.0 copy-start
  9.4 0.0 collective-permute-done.4.refs_13_
  9.4 0.6 copy-done.1
  10.0 0.6 copy-done
  10.6 150.1 %forward.1 = (bf16[64,3584]{1,0:T(8,128)(2,1)}, bf16[64,3584]{1,0:T(8,128)(2,1)}, bf16[64,256]{1,0:T(8,128)(2,1)}, bf16[64,256]{1,0:T(8,128)(2,1)}, f32[64,64]{1...) custom-call(bf16[2,64,3584]{2,1,0:T(8,128)(2,1)} %bitcast.39, ...), custom_call_target="tpu_custom_call" | custom-call | tf_op jit(solution)/shard_map/forward/pallas_call | solution.py:452
  160.7 134.7 %backward.1 = (bf16[2,64,3584]{2,1,0:T(8,128)(2,1)}, bf16[2,64,3584]{2,1,0:T(8,128)(2,1)}, f32[28,256]{1,0:T(8,128)}, f32[2,256]{1,0:T(2,128)}, f32[28,256]{1,0:T(8,128)}) custom-call(bf16[2,64,3584]{2,1,0:T(8,128)(2,1)} %bitcast.40, bf16[2,64,3584]{2,1,0:T(8,128)(2,1)} %bitcast.42, s32[1,64]{1,0:T(1,128)} %bitcast.49, s32[1,64]{1,0:T(1,128)} %bitcast.47, ...), custom_call_target="tpu_custom_call" | custom-call | tf_op jit(solution)/shard_map/backward/pallas_call | solution.py:452
  295.4 2.8 place_results.1
Async XLA Ops:
  0.6 8.7 %collective-permute-start.2 = (bf16[3584,256]{1,0:T(8,128)(2,1)}, bf16[3584,256]{1,0:T(8,128)(2,1)S(1)}, u32[]{:S(2)}, u32[]{:S(2)}) collective-permute-start(bf16[3584,256]{1,0:T(8,128)(2,1)} %bitcast.27), channel_id=1, source_target_pairs={{0,128},{128,0},{1,129},{129,1},{2,130},{130,2},{3,131},{131,3},{4... | collective-permute-start | bytes 5505032 | tf_op jit(solution)/shard_map/ppermute | solution.py:1079
  0.7 8.6 %collective-permute-start.4 = (bf16[256,3584]{1,0:T(8,128)(2,1)}, bf16[256,3584]{1,0:T(8,128)(2,1)}, u32[]{:S(2)}, u32[]{:S(2)}) collective-permute-start(bf16[256,3584]{1,0:T(8,128)(2,1)} %bitcast.30), channel_id=1, source_target_pairs={{0,128},{128,0},{1,129},{129,1},{2,130},{130,2},{3,131},{131,3},{4... | collective-permute-start | bytes 5505032 | tf_op jit(solution)/shard_map/ppermute | solution.py:1079
  2.0 5.5 %collective-permute-start = (s32[64,1]{1,0:T(8,128)S(1)}, s32[64,1]{1,0:T(8,128)S(1)}, u32[]{:S(2)}, u32[]{:S(2)}) collective-permute-start(s32[64,1]{1,0:T(8,128)S(1)} %copy.23), channel_id=1, source_target_pairs={{0,128},{128,0},{1,129},{129,1},{2,130},{130,2},{3,131},{131,3},{4... | collective-permute-start | bytes 776 | tf_op jit(solution)/shard_map/ppermute | solution.py:1079
  2.9 5.8 %collective-permute-start.1 = (f32[64,1]{1,0:T(8,128)S(1)}, f32[64,1]{1,0:T(8,128)S(1)}, u32[]{:S(2)}, u32[]{:S(2)}) collective-permute-start(f32[64,1]{1,0:T(8,128)S(1)} %copy.26), channel_id=1, source_target_pairs={{0,128},{128,0},{1,129},{129,1},{2,130},{130,2},{3,131},{131,3},{4... | collective-permute-start | bytes 776 | tf_op jit(solution)/shard_map/ppermute | solution.py:1079
  3.4 6.0 %collective-permute-start.3 = (bf16[256,256]{1,0:T(8,128)(2,1)}, bf16[256,256]{1,0:T(8,128)(2,1)S(1)}, u32[]{:S(2)}, u32[]{:S(2)}) collective-permute-start(bf16[256,256]{1,0:T(8,128)(2,1)} %bitcast.43), channel_id=1, source_target_pairs={{0,128},{128,0},{1,129},{129,1},{2,130},{130,2},{3,131},{131,3},{4... | collective-permute-start | bytes 393224 | tf_op jit(solution)/shard_map/ppermute | solution.py:1079
  9.4 0.7 copy-start.1
  9.4 1.3 copy-start

commit v7 on v6

--- a/solution.py
+++ b/solution.py
@@ -647,9 +647,11 @@
     unpack_tokens(refs.homea, refs.route_col0[...], refs.tokens)
     act0 = (refs.resid0[...].astype(f32) + refs.gate_col0[...] * refs.tokens[...]).astype(bf16)
     refs.act0[...] = act0
+    for i in range(4):
+        early.relay(i)
     attend(act0, refs.route_row1[...], *w, wait_w, refs.packed, refs.blkc, *kept_refs(refs, 1))
     second.start()
-    for i in range(NZ):
+    for i in range(4, NZ):
         early.relay(i)
     for i in range(NZ):
         second.forward(i)
@@ -715,15 +717,11 @@
     pack_tokens(scaled, refs.route_row0[...], refs.packed, refs.blka)
     again.start()
     for i in range(NZ):
-        out1.relay(i)
-    for i in range(NZ):
         again.forward(i)
         if i >= 2:
             again.relay(i - 2)
     again.relay(6)
     again.relay(7)
-    for i in range(NZ):
-        out1.finish(i)
     gw, uw, dw = experts.ready(0)
 
     def backward0(g):
@@ -741,21 +739,19 @@
     grads.lay_x(1, refs.n1, refs.dl1, refs.latent1, refs.dq1)
     for i in range(NZ):
         back0.relay(i)
+    for i in range(NZ):
+        out1.relay(i)
     grads.x_ring.start(1)
     grads.lay_y(1, refs.dr1, refs.mixed1)
     grads.y_ring.start(1)
-    out1.arrive()
-    unpack_tokens(refs.homea, refs.route_col1[...], refs.tokens)
-    refs.act1[...] = (
-        refs.resid1[...].astype(f32) + refs.gate_col1[...] * refs.tokens[...]
-    ).astype(bf16)
-    grads.trade(0, refs.act_o, refs.act0, refs.act1)
     for i in range(NZ):
         back0.finish(i)
+    back0.arrive()
+    unpack_tokens(refs.homeb, refs.route_col0[...], refs.tokens)
+    for i in range(NZ):
+        out1.finish(i)
     grads.x_ring.relay(1)
     grads.y_ring.relay(1)
-    back0.arrive()
-    unpack_tokens(refs.homeb, refs.route_col0[...], refs.tokens)
     attend_back(
         refs.grad1[...], refs.x[section], *[ref[...] for ref in kept_refs(refs, 0)], w, wait_w,
         refs.tokens, refs.n0, refs.dl0, refs.dq0, refs.dr0, refs.grad0,
@@ -767,6 +763,12 @@
     grads.y_ring.start(0)
     grads.y_ring.own()
     grads.trade(1, refs.grad_o, refs.grad0, refs.grad1)
+    out1.arrive()
+    unpack_tokens(refs.homea, refs.route_col1[...], refs.tokens)
+    refs.act1[...] = (
+        refs.resid1[...].astype(f32) + refs.gate_col1[...] * refs.tokens[...]
+    ).astype(bf16)
+    grads.trade(0, refs.act_o, refs.act0, refs.act1)
     grads.x_ring.relay(0)
     grads.y_ring.relay(0)
     grads.sums()
@@ -947,6 +949,13 @@
             )
 
         x_ring, y_ring = self.x_ring, self.y_ring
+        y_ring.arrive()
+        total = t_times(rows(y_ring, 0, 1024), rows(y_ring, 1024, 256)).astype(bf16)
+        for q in range(4):
+            for c in range(4):
+                refs.tu[q, c * 64 : (c + 1) * 64, :] = total[c * 256 + q * 64 : c * 256 + (q + 1) * 64]
+        for k in (2, 1, 3):
+            remote(refs.tu.at[(d + k) % 4], refs.su.at[d], refs.usem, refs.ur.at[4 - k - 1], self.near_x(k)).start()
         x_ring.arrive()
         total = t_times(rows(x_ring, 0, 1024), rows(x_ring, 1024, 256)).astype(bf16)
         total_qk = t_times(rows(x_ring, 1280, 256), rows(x_ring, 1536, 256)).astype(bf16)
@@ -956,13 +965,6 @@
             refs.td[q, 256:320, :] = total_qk[q * 64 : (q + 1) * 64]
         for k in (2, 1, 3):
             remote(refs.td.at[(y + k) % 4], refs.sd.at[y], refs.dsem, refs.dr.at[4 - k - 1], self.near_y(k)).start()
-        y_ring.arrive()
-        total = t_times(rows(y_ring, 0, 1024), rows(y_ring, 1024, 256)).astype(bf16)
-        for q in range(4):
-            for c in range(4):
-                refs.tu[q, c * 64 : (c + 1) * 64, :] = total[c * 256 + q * 64 : c * 256 + (q + 1) * 64]
-        for k in (2, 1, 3):
-            remote(refs.tu.at[(d + k) % 4], refs.su.at[d], refs.usem, refs.ur.at[4 - k - 1], self.near_x(k)).start()
 
         def gathered(buf, recv, position):
             for k in (1, 2, 3):

time: 299 us -> 296 us (0.990)
  Pallas kernels: 288 us -> 283 us
    pallas_call x2, Pallas kernels: 285 us -> 280 us  [fused(): pl.pallas_call(kernel, name=name, out_shape=list(outs.values()), in_specs...]
where the time goes in v7:
time: 296 us; the launch traced here: 294 us
  Pallas kernels  283 us (96%)
  waiting for transfers between devices  3.82 us (1%)
  local copies, waits for them, and re-layouts  3 us (1%)
    pallas_call x2, Pallas kernels, fused(): pl.pallas_call(kernel, name=name, out_shape=list(outs.values()), in_specs...  280 us
  transfers between devices with their start and end apart: 5, of which 1 were waited for; matrix products, arithmetic and copies ran while one was open for 1% of the time, Pallas kernels for 0%

profile of v7, /device:TPU:0, one launch (start us, length us, event | category | flops | bytes accessed | tf_op | source)
XLA Modules:
  0.0 293.9 jit_solution(520309164078842589)
XLA Ops:
  0.6 0.1 collective-permute-start.2
  0.7 0.5 collective-permute-start.4
  1.2 0.7 fusion.1
  1.9 0.1 copy.23
  2.0 0.1 collective-permute-start
  2.1 0.7 fusion.3
  2.8 0.1 copy.26
  2.9 0.4 collective-permute-start.1
  3.4 0.1 collective-permute-start.3
  3.5 0.1 copy.27
  3.6 0.1 copy.24
  3.7 3.8 %collective-permute-done = s32[64,1]{1,0:T(8,128)S(1)} collective-permute-done((s32[64,1]{1,0:T(8,128)S(1)}, s32[64,1]{1,0:T(8,128)S(1)}, u32[]{:S(2)}, u32[]{:S(2)}) %collective-permute-start) | collective-permute-done | bytes 288 | tf_op jit(solution)/shard_map/ppermute | solution.py:1081
  7.5 1.3 fusion.4
  8.7 0.0 collective-permute-done.1
  8.7 0.6 broadcast_select_fusion
  9.3 0.0 collective-permute-done.3.refs_12_
  9.4 0.0 copy-start.1
  9.4 0.0 collective-permute-done.2.refs_11_
  9.4 0.0 copy-start
  9.4 0.0 collective-permute-done.4.refs_13_
  9.4 0.6 copy-done.1
  10.0 0.6 copy-done
  10.6 149.8 %forward.1 = (bf16[64,3584]{1,0:T(8,128)(2,1)}, bf16[64,3584]{1,0:T(8,128)(2,1)}, bf16[64,256]{1,0:T(8,128)(2,1)}, bf16[64,256]{1,0:T(8,128)(2,1)}, f32[64,64]{1...) custom-call(bf16[2,64,3584]{2,1,0:T(8,128)(2,1)} %bitcast.39, ...), custom_call_target="tpu_custom_call" | custom-call | tf_op jit(solution)/shard_map/forward/pallas_call | solution.py:452
  160.4 130.6 %backward.1 = (bf16[2,64,3584]{2,1,0:T(8,128)(2,1)}, bf16[2,64,3584]{2,1,0:T(8,128)(2,1)}, f32[28,256]{1,0:T(8,128)}, f32[2,256]{1,0:T(2,128)}, f32[28,256]{1,0:T(8,128)}) custom-call(bf16[2,64,3584]{2,1,0:T(8,128)(2,1)} %bitcast.40, bf16[2,64,3584]{2,1,0:T(8,128)(2,1)} %bitcast.42, s32[1,64]{1,0:T(1,128)} %bitcast.49, s32[1,64]{1,0:T(1,128)} %bitcast.47, ...), custom_call_target="tpu_custom_call" | custom-call | tf_op jit(solution)/shard_map/backward/pallas_call | solution.py:452
  291.1 2.8 place_results.1
Async XLA Ops:
  0.6 8.7 %collective-permute-start.2 = (bf16[3584,256]{1,0:T(8,128)(2,1)}, bf16[3584,256]{1,0:T(8,128)(2,1)S(1)}, u32[]{:S(2)}, u32[]{:S(2)}) collective-permute-start(bf16[3584,256]{1,0:T(8,128)(2,1)} %bitcast.27), channel_id=1, source_target_pairs={{0,128},{128,0},{1,129},{129,1},{2,130},{130,2},{3,131},{131,3},{4... | collective-permute-start | bytes 5505032 | tf_op jit(solution)/shard_map/ppermute | solution.py:1081
  0.7 8.6 %collective-permute-start.4 = (bf16[256,3584]{1,0:T(8,128)(2,1)}, bf16[256,3584]{1,0:T(8,128)(2,1)}, u32[]{:S(2)}, u32[]{:S(2)}) collective-permute-start(bf16[256,3584]{1,0:T(8,128)(2,1)} %bitcast.30), channel_id=1, source_target_pairs={{0,128},{128,0},{1,129},{129,1},{2,130},{130,2},{3,131},{131,3},{4... | collective-permute-start | bytes 5505032 | tf_op jit(solution)/shard_map/ppermute | solution.py:1081
  2.0 5.5 %collective-permute-start = (s32[64,1]{1,0:T(8,128)S(1)}, s32[64,1]{1,0:T(8,128)S(1)}, u32[]{:S(2)}, u32[]{:S(2)}) collective-permute-start(s32[64,1]{1,0:T(8,128)S(1)} %copy.23), channel_id=1, source_target_pairs={{0,128},{128,0},{1,129},{129,1},{2,130},{130,2},{3,131},{131,3},{4... | collective-permute-start | bytes 776 | tf_op jit(solution)/shard_map/ppermute | solution.py:1081
  2.9 5.8 %collective-permute-start.1 = (f32[64,1]{1,0:T(8,128)S(1)}, f32[64,1]{1,0:T(8,128)S(1)}, u32[]{:S(2)}, u32[]{:S(2)}) collective-permute-start(f32[64,1]{1,0:T(8,128)S(1)} %copy.26), channel_id=1, source_target_pairs={{0,128},{128,0},{1,129},{129,1},{2,130},{130,2},{3,131},{131,3},{4... | collective-permute-start | bytes 776 | tf_op jit(solution)/shard_map/ppermute | solution.py:1081
  3.4 6.0 %collective-permute-start.3 = (bf16[256,256]{1,0:T(8,128)(2,1)}, bf16[256,256]{1,0:T(8,128)(2,1)S(1)}, u32[]{:S(2)}, u32[]{:S(2)}) collective-permute-start(bf16[256,256]{1,0:T(8,128)(2,1)} %bitcast.43), channel_id=1, source_target_pairs={{0,128},{128,0},{1,129},{129,1},{2,130},{130,2},{3,131},{131,3},{4... | collective-permute-start | bytes 393224 | tf_op jit(solution)/shard_map/ppermute | solution.py:1081
  9.4 0.7 copy-start.1
  9.4 1.3 copy-start
